TPU v7x, 32 devices: a whole 2x2x4 slice. The times are simulated.
32 devices in a mesh: groups: 2 (over y), section: 4 (over z), dp: 4 (over x, core).
Axes of the slice: x: 2, y: 2, z: 4, core: 2. Of those that a mesh axis runs over, the one named last changes fastest.
Arguments:
- stream_in: bfloat16 [1152, 3072], P(('groups', 'dp')), parts along dimension 0, may hold values from -6 to 6
- out_grad: bfloat16 [1152, 3072], P(('groups', 'dp')), parts along dimension 0, may hold values from -6 to 6
- mask_blocks: int32 [24, 3, 3], P(('groups', 'dp')), parts along dimension 0, may hold values from 0 to 2, as said below
- norm_gain: float32 [4, 3072], P('section'), may hold values from 0.4 to 1.6
- w_joined: bfloat16 [4, 3072, 1664], P('section', 'dp'), may hold values from -0.109375 to 0.109375
- w_out: bfloat16 [4, 1536, 3072], P('section', 'dp'), may hold values from -0.15625 to 0.15625
Outputs:
- grad_joined: float32 [8, 3072, 1664], P(('groups', 'section'), 'dp'), parts along dimension 0
- grad_out: float32 [8, 1536, 3072], P(('groups', 'section'), 'dp'), parts along dimension 0
- gain_grad: float32 [8, 3072], P(('groups', 'section')), parts along dimension 0
There are 2 independent parts, one for each index of `groups`. A program takes and returns all parts, laid end to end along the dimension named above; an argument that names none is the same for every part. Nothing has to cross between parts.
Inputs may be any that keep to these rules, and one draw needn't show every extreme that they name: `mask_blocks`: entry 0 of the list of query block i is i itself.
All inputs are finite; a program needn't handle non-finite values.
Results may differ from a plain program's by a relative error of at most 0.024.
Values may be sent and summed in bfloat16 or wider, within the bound.
A program may use at most 128 MiB of HBM per device.

v0:
```python
import jax
import jax.numpy as jnp
from jax import lax
from jax.sharding import PartitionSpec as P

NUM_HEADS = 24
HEAD_DIM = 64
BLOCK_LEN = 16


EPSILON = 1e-05


def from_behind(value, axis, steps):
    count = lax.axis_size(axis)
    initial, last = (max(0, -steps), min(count, count - steps))
    return lax.ppermute(value, axis, [(source, source + steps) for source in range(initial, last)])


def allowed_tokens(links, block_len):
    count = links.shape[1]
    block_hits = links[:, :, :, None] == jnp.arange(count, dtype=jnp.int32)[None, None, None, :]
    blocks = jnp.any(block_hits, axis=2)
    return jnp.repeat(jnp.repeat(blocks, block_len, axis=1), block_len, axis=2)


def normalize(stream, gain_row):
    stream_wide = stream.astype(jnp.float32)
    inv_rms = lax.rsqrt(jnp.mean(stream_wide * stream_wide, axis=-1, keepdims=True) + EPSILON)
    normed = (stream_wide * inv_rms * gain_row).astype(jnp.bfloat16)
    return (stream_wide, inv_rms, normed)


def project(normed, weight):
    batch_size, length, model_width = normed.shape
    flat = jnp.dot(normed.reshape(-1, model_width), weight, preferred_element_type=jnp.float32)
    return flat.astype(jnp.bfloat16).reshape(batch_size, length, weight.shape[1])


def attend(joined_rows, allowed):
    batch_size, length, _ = joined_rows.shape
    inner_width = NUM_HEADS * HEAD_DIM
    queries = joined_rows[:, :, :inner_width].reshape(batch_size, length, NUM_HEADS, HEAD_DIM)
    key_rows = joined_rows[:, :, inner_width : inner_width + HEAD_DIM]
    values = joined_rows[:, :, inner_width + HEAD_DIM :]
    scores = jnp.einsum(
        "bihd,bjd->bhij", queries, key_rows, preferred_element_type=jnp.float32
    ) * HEAD_DIM ** (-0.5)
    scores = jnp.where(allowed[:, None], scores, -1e30)
    row_max = jnp.max(scores, axis=-1, keepdims=True)
    exp_scores = jnp.exp(scores - row_max)
    attn_probs = exp_scores / jnp.sum(exp_scores, axis=-1, keepdims=True)
    probs_half = attn_probs.astype(jnp.bfloat16)
    mixed_heads = jnp.einsum(
        "bhij,bjd->bihd", probs_half, values, preferred_element_type=jnp.float32
    )
    mixed_heads = mixed_heads.astype(jnp.bfloat16).reshape(batch_size, length, inner_width)
    return (queries, key_rows, values, attn_probs, probs_half, mixed_heads)


def layer_forward(stream, gain_row, w_joined, w_out, allowed):
    stream_wide, inv_rms, normed = normalize(stream, gain_row)
    joined_rows = project(normed, w_joined)
    mixed_heads = attend(joined_rows, allowed)[5]
    batch_size, length, model_width = stream.shape
    update = jnp.dot(
        mixed_heads.reshape(-1, mixed_heads.shape[2]), w_out, preferred_element_type=jnp.float32
    )
    result = (stream_wide + update.reshape(batch_size, length, model_width)).astype(jnp.bfloat16)
    return (result, joined_rows)


def layer_backward(stream, gain_row, joined_rows, w_joined, w_out, allowed, upstream):
    stream_wide, inv_rms, normed = normalize(stream, gain_row)
    queries, key_rows, values, attn_probs, probs_half, mixed_heads = attend(joined_rows, allowed)
    batch_size, length, model_width = stream.shape
    inner_width = NUM_HEADS * HEAD_DIM
    grad_mixed = lax.dot_general(
        upstream.reshape(-1, model_width),
        w_out,
        (((1,), (1,)), ((), ())),
        preferred_element_type=jnp.float32,
    )
    grad_mixed = grad_mixed.astype(jnp.bfloat16).reshape(batch_size, length, NUM_HEADS, HEAD_DIM)
    grad_probs = jnp.einsum(
        "bihd,bjd->bhij", grad_mixed, values, preferred_element_type=jnp.float32
    )
    grad_values = jnp.einsum(
        "bhij,bihd->bjd", probs_half, grad_mixed, preferred_element_type=jnp.float32
    )
    inner_sum = jnp.sum(attn_probs * grad_probs, axis=-1, keepdims=True)
    grad_scores = (attn_probs * (grad_probs - inner_sum) * HEAD_DIM ** (-0.5)).astype(jnp.bfloat16)
    grad_queries = jnp.einsum(
        "bhij,bjd->bihd", grad_scores, key_rows, preferred_element_type=jnp.float32
    )
    grad_keys = jnp.einsum(
        "bhij,bihd->bjd", grad_scores, queries, preferred_element_type=jnp.float32
    )
    grad_joined_rows = jnp.concatenate(
        [grad_queries.reshape(batch_size, length, inner_width), grad_keys, grad_values], axis=-1
    ).astype(jnp.bfloat16)
    grad_normed = lax.dot_general(
        grad_joined_rows.reshape(-1, grad_joined_rows.shape[2]),
        w_joined,
        (((1,), (1,)), ((), ())),
        preferred_element_type=jnp.float32,
    )
    grad_normed = grad_normed.reshape(batch_size, length, model_width)
    gained = grad_normed * gain_row
    grad_stream = inv_rms * gained - stream_wide * inv_rms**3 * jnp.mean(
        stream_wide * gained, axis=-1, keepdims=True
    )
    down_grad = (upstream.astype(jnp.float32) + grad_stream).astype(jnp.bfloat16)
    gain_part = jnp.sum((grad_normed * stream_wide * inv_rms).reshape(-1, model_width), axis=0)
    return (down_grad, normed, grad_joined_rows, mixed_heads, gain_part)


def pass_forward(values):
    return from_behind(values, "section", 1)


def pass_backward(values):
    return from_behind(values, "section", -1)


def body(stream_in, out_grad, mask_blocks, norm_gain, w_joined, w_out):
    gathered = (
        lax.all_gather(w_joined, "dp", axis=1, tiled=True),
        lax.all_gather(w_out, "dp", axis=1, tiled=True),
    )
    full_joined = gathered[0][0]
    full_out = gathered[1][0]
    gain_row = norm_gain[0]
    sections = lax.axis_size("section")
    section_index = lax.axis_index("section")
    micro_count = mask_blocks.shape[0]
    model_width = stream_in.shape[1]
    length = stream_in.shape[0] // micro_count
    joined_width = full_joined.shape[1]
    inner_width = full_out.shape[0]
    per_group = micro_count // micro_count
    inputs = stream_in.reshape(micro_count, per_group, length, model_width)
    upstreams = out_grad.reshape(micro_count, per_group, length, model_width)
    allowed = allowed_tokens(mask_blocks, BLOCK_LEN).reshape(micro_count, per_group, length, length)
    step_count = micro_count + sections - 1
    keep_shape = (1,)

    def forward_step(step_now, state_now):
        incoming, kept_inputs, kept_joined = state_now
        slot_index = step_now - section_index
        active = jnp.logical_and(slot_index >= 0, slot_index < micro_count)
        group_index = jnp.clip(slot_index, 0, micro_count - 1)
        source = jnp.where(section_index == 0, inputs[group_index], incoming)

        def forward_run(kept_pair):
            result, joined_rows = layer_forward(
                source, gain_row, full_joined, full_out, allowed[group_index]
            )
            new_inputs = lax.dynamic_update_index_in_dim(kept_pair[0], source, group_index, 0)
            new_joined = kept_pair[1]
            return (result, new_inputs, new_joined)

        def forward_rest(kept_pair):
            return (jnp.zeros_like(source), kept_pair[0], kept_pair[1])

        result, kept_inputs, kept_joined = lax.cond(
            active, forward_run, forward_rest, (kept_inputs, kept_joined)
        )
        return (pass_forward(result), kept_inputs, kept_joined)

    start_state = (
        jnp.zeros((per_group, length, model_width), jnp.bfloat16),
        jnp.zeros((micro_count, per_group, length, model_width), jnp.bfloat16),
        jnp.zeros(keep_shape, jnp.bfloat16),
    )
    _, kept_inputs, kept_joined = lax.fori_loop(0, step_count, forward_step, start_state)

    def backward_step(step_now, state_now):
        incoming, stores = state_now
        slot_index = step_now - (sections - 1 - section_index)
        active = jnp.logical_and(slot_index >= 0, slot_index < micro_count)
        group_index = jnp.clip(slot_index, 0, micro_count - 1)
        upstream = jnp.where(section_index == sections - 1, upstreams[group_index], incoming)

        def backward_run(store_now):
            source = kept_inputs[group_index]
            joined_rows = project(normalize(source, gain_row)[2], full_joined)
            down_grad, normed, grad_joined_rows, mixed_heads, gain_part = layer_backward(
                source, gain_row, joined_rows, full_joined, full_out, allowed[group_index], upstream
            )
            new_store = (
                lax.dynamic_update_index_in_dim(store_now[0], normed, group_index, 0),
                lax.dynamic_update_index_in_dim(store_now[1], grad_joined_rows, group_index, 0),
                lax.dynamic_update_index_in_dim(store_now[2], mixed_heads, group_index, 0),
                lax.dynamic_update_index_in_dim(store_now[3], upstream, group_index, 0),
                store_now[4] + gain_part,
            )
            return (down_grad, new_store)

        def backward_rest(store_now):
            return (jnp.zeros_like(upstream), store_now)

        down_grad, stores = lax.cond(active, backward_run, backward_rest, stores)
        return (pass_backward(down_grad), stores)

    empty_stores = (
        jnp.zeros((micro_count, per_group, length, model_width), jnp.bfloat16),
        jnp.zeros((micro_count, per_group, length, joined_width), jnp.bfloat16),
        jnp.zeros((micro_count, per_group, length, inner_width), jnp.bfloat16),
        jnp.zeros((micro_count, per_group, length, model_width), jnp.bfloat16),
        jnp.zeros((model_width,), jnp.float32),
    )
    start_back = (jnp.zeros((per_group, length, model_width), jnp.bfloat16), empty_stores)
    _, stores = lax.fori_loop(0, step_count, backward_step, start_back)
    rows_normed = stores[0].reshape(-1, model_width)
    rows_joined = stores[1].reshape(-1, joined_width)
    rows_mixed = stores[2].reshape(-1, inner_width)
    rows_upstream = stores[3].reshape(-1, model_width)
    columns = rows_normed
    grad_joined = lax.psum_scatter(
        lax.dot_general(
            columns, rows_joined, (((0,), (0,)), ((), ())), preferred_element_type=jnp.float32
        ).astype(jnp.bfloat16),
        "dp",
        scatter_dimension=0,
        tiled=True,
    ).astype(jnp.float32)
    columns = rows_mixed
    grad_output = lax.psum_scatter(
        lax.dot_general(
            columns, rows_upstream, (((0,), (0,)), ((), ())), preferred_element_type=jnp.float32
        ).astype(jnp.bfloat16),
        "dp",
        scatter_dimension=0,
        tiled=True,
    ).astype(jnp.float32)
    gain_total = lax.psum(stores[4], "dp")
    return (grad_joined[None], grad_output[None], gain_total[None])


def solution(mesh):
    return jax.shard_map(
        body,
        mesh=mesh,
        in_specs=(
            P(("groups", "dp"), None),
            P(("groups", "dp"), None),
            P(("groups", "dp"), None, None),
            P("section", None),
            P("section", "dp", None),
            P("section", "dp", None),
        ),
        out_specs=(
            P(("groups", "section"), "dp", None),
            P(("groups", "section"), "dp", None),
            P(("groups", "section"), None),
        ),
        check_vma=False,
    )
```

profile of v0, /device:TPU:0, one launch (start us, length us, event | category | flops | bytes accessed | tf_op | source)
XLA Modules:
  0.0 678.1 jit_solution(13582287614701834989)
XLA Ops:
  9.8 66.7 %all-gather.5.cloned.1.call-done = bf16[1,1536,3072]{2,1,0:T(8,128)(2,1)} async-done(((bf16[1,384,3072]{2,1,0:T(8,128)(2,1)}), bf16[1,1536,3072]{2,1,0:T(8,128)(2,1)}) %all-gather.5.cloned.1.call-update) | async-done | bytes 9437200 | tf_op jit(solution)/shard_map/all_gather | solution.py:129
  76.5 70.3 %all-gather.3.cloned.1.call-done = bf16[1,3072,1664]{2,1,0:T(8,128)(2,1)} async-done(((bf16[1,768,1664]{2,1,0:T(8,128)(2,1)}), bf16[1,3072,1664]{2,1,0:T(8,128)(2,1)}) %all-gather.3.cloned.1.call-update) | async-done | bytes 10223632 | tf_op jit(solution)/shard_map/all_gather | solution.py:128
  146.9 123.2 %while.46 = (s32[]{:T(128)}, bf16[1,48,3072]{2,1,0:T(8,128)(2,1)S(1)}, bf16[3,1,48,3072]{3,2,1,0:T(8,128)(2,1)S(1)}, s32[]{:T(128)}, pred[]{:T(512)}, /*index=5*...) while((s32[]{:T(128)}, ...), condition=%wide.region_7.8_spmd.clone, body=%wide.region_1.7_spmd.clone.sunk | while | flops 960089920 | bytes 26255604 | solution.py:176
  147.0 14.0 %conditional.6 = (bf16[1,48,3072]{2,1,0:T(8,128)(2,1)S(1)}, bf16[3,1,48,3072]{3,2,1,0:T(8,128)(2,1)S(1)}) conditional(s32[]{:T(128)} %convert_element_type.279, bf16[3,1,48,3072]{3,2,1,0:T(8,128)(2,1)S(1)} %get-tuple-element.1143, (pred[]{:T(512)}, s32[]{:T(128)}, bf16[3,1,48,3072]{3,2,1,0:T(8,128)(2,1)}, bf16[1,48,3072]{2,1,0:T(8,128)(2,1)S(1)}, ...), branch_computations={%region_2.2_spmd, %region_3.6_spmd} | conditional | flops 960089920 | bytes 25068336 | solution.py:166
  162.3 6.9 %collective-permute-done = bf16[1,48,3072]{2,1,0:T(8,128)(2,1)S(1)} collective-permute-done((bf16[1,48,3072]{2,1,0:T(8,128)(2,1)S(1)}, bf16[1,48,3072]{2,1,0:T(8,128)(2,1)S(1)}, u32[]{:S(2)}, u32[]{:S(2)}) %collective-permute-start) | collective-permute-done | bytes 294944 | tf_op jit(solution)/shard_map/while/body/eval_jaxpr/ppermute | solution.py:17
  169.3 14.0 %conditional.6 = (bf16[1,48,3072]{2,1,0:T(8,128)(2,1)S(1)}, bf16[3,1,48,3072]{3,2,1,0:T(8,128)(2,1)S(1)}) conditional(s32[]{:T(128)} %convert_element_type.279, bf16[3,1,48,3072]{3,2,1,0:T(8,128)(2,1)S(1)} %get-tuple-element.1143, (pred[]{:T(512)}, s32[]{:T(128)}, bf16[3,1,48,3072]{3,2,1,0:T(8,128)(2,1)}, bf16[1,48,3072]{2,1,0:T(8,128)(2,1)S(1)}, ...), branch_computations={%region_2.2_spmd, %region_3.6_spmd} | conditional | flops 960089920 | bytes 25068336 | solution.py:166
  187.7 6.2 collective-permute-done
  193.9 14.0 %conditional.6 = (bf16[1,48,3072]{2,1,0:T(8,128)(2,1)S(1)}, bf16[3,1,48,3072]{3,2,1,0:T(8,128)(2,1)S(1)}) conditional(s32[]{:T(128)} %convert_element_type.279, bf16[3,1,48,3072]{3,2,1,0:T(8,128)(2,1)S(1)} %get-tuple-element.1143, (pred[]{:T(512)}, s32[]{:T(128)}, bf16[3,1,48,3072]{3,2,1,0:T(8,128)(2,1)}, bf16[1,48,3072]{2,1,0:T(8,128)(2,1)S(1)}, ...), branch_computations={%region_2.2_spmd, %region_3.6_spmd} | conditional | flops 960089920 | bytes 25068336 | solution.py:166
  217.6 18.4 %collective-permute-start = (bf16[1,48,3072]{2,1,0:T(8,128)(2,1)S(1)}, bf16[1,48,3072]{2,1,0:T(8,128)(2,1)S(1)}, u32[]{:S(2)}, u32[]{:S(2)}) collective-permute-start(bf16[1,48,3072]{2,1,0:T(8,128)(2,1)S(1)} %get-tuple-element.1089), channel_id=1, source_target_pairs={{0,4},{4,8},{8,12},{1,5},{5,9},{9,13},{2,6},{6,10},{10,14},{3,7},{... | collective-permute-start | bytes 884744 | tf_op jit(solution)/shard_map/while/body/eval_jaxpr/ppermute | solution.py:17
  249.1 16.8 %collective-permute-start = (bf16[1,48,3072]{2,1,0:T(8,128)(2,1)S(1)}, bf16[1,48,3072]{2,1,0:T(8,128)(2,1)S(1)}, u32[]{:S(2)}, u32[]{:S(2)}) collective-permute-start(bf16[1,48,3072]{2,1,0:T(8,128)(2,1)S(1)} %get-tuple-element.1089), channel_id=1, source_target_pairs={{0,4},{4,8},{8,12},{1,5},{5,9},{9,13},{2,6},{6,10},{10,14},{3,7},{... | collective-permute-start | bytes 884744 | tf_op jit(solution)/shard_map/while/body/eval_jaxpr/ppermute | solution.py:17
  273.0 224.6 %while.47 = (s32[]{:T(128)}, bf16[1,48,3072]{2,1,0:T(8,128)(2,1)S(1)}, bf16[3,1,48,3072]{3,2,1,0:T(8,128)(2,1)}, bf16[3,1,48,1664]{3,2,1,0:T(8,128)(2,1)S(1)}, b...) while((s32[]{:T(128)}, ...), condition=%wide.region_17.18_spmd.clone, body=%wide.region_8.17_spmd.clone.sunk | while | flops 1482513152 | bytes 44681152 | solution.py:214
  274.4 7.8 %collective-permute-done.1 = bf16[1,48,3072]{2,1,0:T(8,128)(2,1)S(1)} collective-permute-done((bf16[1,48,3072]{2,1,0:T(8,128)(2,1)S(1)}, bf16[1,48,3072]{2,1,0:T(8,128)(2,1)S(1)}, u32[]{:S(2)}, u32[]{:S(2)}) %collective-permute-start.1) | collective-permute-done | bytes 294944 | tf_op jit(solution)/shard_map/while/body/eval_jaxpr/ppermute | solution.py:17
  283.5 19.8 %collective-permute-done.1 = bf16[1,48,3072]{2,1,0:T(8,128)(2,1)S(1)} collective-permute-done((bf16[1,48,3072]{2,1,0:T(8,128)(2,1)S(1)}, bf16[1,48,3072]{2,1,0:T(8,128)(2,1)S(1)}, u32[]{:S(2)}, u32[]{:S(2)}) %collective-permute-start.1) | collective-permute-done | bytes 294944 | tf_op jit(solution)/shard_map/while/body/eval_jaxpr/ppermute | solution.py:17
  304.7 87.0 %collective-permute-done.1 = bf16[1,48,3072]{2,1,0:T(8,128)(2,1)S(1)} collective-permute-done((bf16[1,48,3072]{2,1,0:T(8,128)(2,1)S(1)}, bf16[1,48,3072]{2,1,0:T(8,128)(2,1)S(1)}, u32[]{:S(2)}, u32[]{:S(2)}) %collective-permute-start.1) | collective-permute-done | bytes 294944 | tf_op jit(solution)/shard_map/while/body/eval_jaxpr/ppermute | solution.py:17
  391.7 26.7 %conditional.7 = (bf16[1,48,3072]{2,1,0:T(8,128)(2,1)S(1)}, bf16[3,1,48,3072]{3,2,1,0:T(8,128)(2,1)}, bf16[3,1,48,1664]{3,2,1,0:T(8,128)(2,1)S(1)}, bf16[3,1,48,...) conditional(s32[]{:T(128)} %convert_element_type.280, ...), branch_computations={%region_9.9_spmd, %region_10.16_spmd} | conditional | flops 1482513152 | bytes 43493764 | solution.py:203
  401.8 6.6 convolution_convert_fusion.3
  410.8 7.2 %fusion.40 = (f32[3072]{0:T(1024)S(1)}, f32[48]{0:T(128)S(1)}, f32[48,3072]{1,0:T(8,128)S(1)}) fusion(f32[48]{0:T(128)S(1)} %get-tuple-element.937, bf16[3,1,48,3072]{3,2,1,0:T(8,128)(2,1)S(1)} %get-tuple-element.767, s32[]{:T(128)S(6)} %min.21, f32[3072]{0:T(1024)S(1)} %bitcast.198, bf16[48,1664]{1,0:T(8,128)(2,1)S(1)} %concatenate.26, ...), kind=kOutput, calls=%fused_computation.62 | convolution fusion | flops 491762624 | bytes 11293060 | tf_op jit(solution)/shard_map/while/body/eval_jaxpr/cond/branch_1_fun/dot_general | solution.py:102
  419.7 7.3 %collective-permute-done.1 = bf16[1,48,3072]{2,1,0:T(8,128)(2,1)S(1)} collective-permute-done((bf16[1,48,3072]{2,1,0:T(8,128)(2,1)S(1)}, bf16[1,48,3072]{2,1,0:T(8,128)(2,1)S(1)}, u32[]{:S(2)}, u32[]{:S(2)}) %collective-permute-start.1) | collective-permute-done | bytes 294944 | tf_op jit(solution)/shard_map/while/body/eval_jaxpr/ppermute | solution.py:17
  427.0 26.7 %conditional.7 = (bf16[1,48,3072]{2,1,0:T(8,128)(2,1)S(1)}, bf16[3,1,48,3072]{3,2,1,0:T(8,128)(2,1)}, bf16[3,1,48,1664]{3,2,1,0:T(8,128)(2,1)S(1)}, bf16[3,1,48,...) conditional(s32[]{:T(128)} %convert_element_type.280, ...), branch_computations={%region_9.9_spmd, %region_10.16_spmd} | conditional | flops 1482513152 | bytes 43493764 | solution.py:203
  437.2 6.6 convolution_convert_fusion.3
  446.1 7.2 %fusion.40 = (f32[3072]{0:T(1024)S(1)}, f32[48]{0:T(128)S(1)}, f32[48,3072]{1,0:T(8,128)S(1)}) fusion(f32[48]{0:T(128)S(1)} %get-tuple-element.937, bf16[3,1,48,3072]{3,2,1,0:T(8,128)(2,1)S(1)} %get-tuple-element.767, s32[]{:T(128)S(6)} %min.21, f32[3072]{0:T(1024)S(1)} %bitcast.198, bf16[48,1664]{1,0:T(8,128)(2,1)S(1)} %concatenate.26, ...), kind=kOutput, calls=%fused_computation.62 | convolution fusion | flops 491762624 | bytes 11293060 | tf_op jit(solution)/shard_map/while/body/eval_jaxpr/cond/branch_1_fun/dot_general | solution.py:102
  455.0 7.3 %collective-permute-done.1 = bf16[1,48,3072]{2,1,0:T(8,128)(2,1)S(1)} collective-permute-done((bf16[1,48,3072]{2,1,0:T(8,128)(2,1)S(1)}, bf16[1,48,3072]{2,1,0:T(8,128)(2,1)S(1)}, u32[]{:S(2)}, u32[]{:S(2)}) %collective-permute-start.1) | collective-permute-done | bytes 294944 | tf_op jit(solution)/shard_map/while/body/eval_jaxpr/ppermute | solution.py:17
  462.3 26.7 %conditional.7 = (bf16[1,48,3072]{2,1,0:T(8,128)(2,1)S(1)}, bf16[3,1,48,3072]{3,2,1,0:T(8,128)(2,1)}, bf16[3,1,48,1664]{3,2,1,0:T(8,128)(2,1)S(1)}, bf16[3,1,48,...) conditional(s32[]{:T(128)} %convert_element_type.280, ...), branch_computations={%region_9.9_spmd, %region_10.16_spmd} | conditional | flops 1482513152 | bytes 43493764 | solution.py:203
  462.6 5.9 fusion.20
  472.5 6.6 convolution_convert_fusion.3
  481.4 7.2 %fusion.40 = (f32[3072]{0:T(1024)S(1)}, f32[48]{0:T(128)S(1)}, f32[48,3072]{1,0:T(8,128)S(1)}) fusion(f32[48]{0:T(128)S(1)} %get-tuple-element.937, bf16[3,1,48,3072]{3,2,1,0:T(8,128)(2,1)S(1)} %get-tuple-element.767, s32[]{:T(128)S(6)} %min.21, f32[3072]{0:T(1024)S(1)} %bitcast.198, bf16[48,1664]{1,0:T(8,128)(2,1)S(1)} %concatenate.26, ...), kind=kOutput, calls=%fused_computation.62 | convolution fusion | flops 491762624 | bytes 11293060 | tf_op jit(solution)/shard_map/while/body/eval_jaxpr/cond/branch_1_fun/dot_general | solution.py:102
  490.3 7.3 %collective-permute-done.1 = bf16[1,48,3072]{2,1,0:T(8,128)(2,1)S(1)} collective-permute-done((bf16[1,48,3072]{2,1,0:T(8,128)(2,1)S(1)}, bf16[1,48,3072]{2,1,0:T(8,128)(2,1)S(1)}, u32[]{:S(2)}, u32[]{:S(2)}) %collective-permute-start.1) | collective-permute-done | bytes 294944 | tf_op jit(solution)/shard_map/while/body/eval_jaxpr/ppermute | solution.py:17
  497.6 7.6 %bitcast_convert_fusion.1 = bf16[1536,3072]{1,0:T(8,128)(2,1)} fusion(bf16[3,1,48,3072]{3,2,1,0:T(8,128)(2,1)} %get-tuple-element.812, bf16[3,1,48,1536]{3,2,1,0:T(8,128)(2,1)} %get-tuple-element.811), kind=kOutput, calls=%fused_computation.97 | convolution fusion | flops 1363673088 | bytes 10764288 | tf_op jit(solution)/shard_map/dot_general | solution.py:230
  505.5 10.6 %bitcast_convert_fusion = bf16[3072,1664]{1,0:T(8,128)(2,1)} fusion(bf16[3,1,48,3072]{3,2,1,0:T(8,128)(2,1)} %get-tuple-element.809, bf16[3,1,48,1664]{3,2,1,0:T(8,128)(2,1)S(1)} %get-tuple-element.810), kind=kOutput, calls=%fused_computation.96 | convolution fusion | flops 1477312512 | bytes 11587584 | tf_op jit(solution)/shard_map/dot_general | solution.py:221
  516.2 10.7 %psum.7 = f32[1,3072]{1,0:T(1,128)} all-reduce(f32[1,3072]{1,0:T(1,128)S(1)} %bitcast.206), channel_id=1, replica_groups=mesh['groups'=2,'section'=4,'dp'=4] {'dp'}, use_global_device_ids=true, to_apply=%region_20.21 | all-reduce | flops 3072 | bytes 24576 | tf_op jit(solution)/shard_map/psum | solution.py:237
  526.9 54.2 %reduce-scatter.5.cloned.1.call-done = bf16[384,3072]{1,0:T(8,128)(2,1)} async-done(((bf16[1536,3072]{1,0:T(8,128)(2,1)}), bf16[384,3072]{1,0:T(8,128)(2,1)}) %reduce-scatter.5.cloned.1.call-update) | async-done | bytes 2359312 | tf_op jit(solution)/shard_map/reduce_scatter | solution.py:229
  585.5 81.7 %reduce-scatter.3.cloned.1.call-done = bf16[768,1664]{1,0:T(8,128)(2,1)} async-done(((bf16[3072,1664]{1,0:T(8,128)(2,1)}), bf16[768,1664]{1,0:T(8,128)(2,1)}) %reduce-scatter.3.cloned.1.call-update) | async-done | bytes 2555920 | tf_op jit(solution)/shard_map/reduce_scatter | solution.py:220
  (188 shorter events, 129.4 us)
Async XLA Ops:
  7.2 69.4 %all-gather.5.cloned.1.call-start = ((), (), s32[]{:S(2)}) async-start(), calls=%async_computation.3 | async-start | bytes 11796480 | tf_op jit(solution)/shard_map/all_gather | solution.py:129
  7.9 138.9 %all-gather.3.cloned.1.call-start = ((), (), s32[]{:S(2)}) async-start(), calls=%async_computation.2 | async-start | bytes 12779520 | tf_op jit(solution)/shard_map/all_gather | solution.py:128
  8.6 572.5 %reduce-scatter.5.cloned.1.call-start = ((), (), s32[]{:S(2)}) async-start(), calls=%async_computation.5 | async-start | bytes 11796480 | tf_op jit(solution)/shard_map/reduce_scatter | solution.py:229
  161.0 8.3 %collective-permute-start = (bf16[1,48,3072]{2,1,0:T(8,128)(2,1)S(1)}, bf16[1,48,3072]{2,1,0:T(8,128)(2,1)S(1)}, u32[]{:S(2)}, u32[]{:S(2)}) collective-permute-start(bf16[1,48,3072]{2,1,0:T(8,128)(2,1)S(1)} %get-tuple-element.1089), channel_id=1, source_target_pairs={{0,4},{4,8},{8,12},{1,5},{5,9},{9,13},{2,6},{6,10},{10,14},{3,7},{... | collective-permute-start | bytes 884744 | tf_op jit(solution)/shard_map/while/body/eval_jaxpr/ppermute | solution.py:17
  183.3 10.6 %collective-permute-start = (bf16[1,48,3072]{2,1,0:T(8,128)(2,1)S(1)}, bf16[1,48,3072]{2,1,0:T(8,128)(2,1)S(1)}, u32[]{:S(2)}, u32[]{:S(2)}) collective-permute-start(bf16[1,48,3072]{2,1,0:T(8,128)(2,1)S(1)} %get-tuple-element.1089), channel_id=1, source_target_pairs={{0,4},{4,8},{8,12},{1,5},{5,9},{9,13},{2,6},{6,10},{10,14},{3,7},{... | collective-permute-start | bytes 884744 | tf_op jit(solution)/shard_map/while/body/eval_jaxpr/ppermute | solution.py:17
  207.9 9.7 %collective-permute-start = (bf16[1,48,3072]{2,1,0:T(8,128)(2,1)S(1)}, bf16[1,48,3072]{2,1,0:T(8,128)(2,1)S(1)}, u32[]{:S(2)}, u32[]{:S(2)}) collective-permute-start(bf16[1,48,3072]{2,1,0:T(8,128)(2,1)S(1)} %get-tuple-element.1089), channel_id=1, source_target_pairs={{0,4},{4,8},{8,12},{1,5},{5,9},{9,13},{2,6},{6,10},{10,14},{3,7},{... | collective-permute-start | bytes 884744 | tf_op jit(solution)/shard_map/while/body/eval_jaxpr/ppermute | solution.py:17
  217.6 22.7 %collective-permute-start = (bf16[1,48,3072]{2,1,0:T(8,128)(2,1)S(1)}, bf16[1,48,3072]{2,1,0:T(8,128)(2,1)S(1)}, u32[]{:S(2)}, u32[]{:S(2)}) collective-permute-start(bf16[1,48,3072]{2,1,0:T(8,128)(2,1)S(1)} %get-tuple-element.1089), channel_id=1, source_target_pairs={{0,4},{4,8},{8,12},{1,5},{5,9},{9,13},{2,6},{6,10},{10,14},{3,7},{... | collective-permute-start | bytes 884744 | tf_op jit(solution)/shard_map/while/body/eval_jaxpr/ppermute | solution.py:17
  240.4 8.6 %collective-permute-start = (bf16[1,48,3072]{2,1,0:T(8,128)(2,1)S(1)}, bf16[1,48,3072]{2,1,0:T(8,128)(2,1)S(1)}, u32[]{:S(2)}, u32[]{:S(2)}) collective-permute-start(bf16[1,48,3072]{2,1,0:T(8,128)(2,1)S(1)} %get-tuple-element.1089), channel_id=1, source_target_pairs={{0,4},{4,8},{8,12},{1,5},{5,9},{9,13},{2,6},{6,10},{10,14},{3,7},{... | collective-permute-start | bytes 884744 | tf_op jit(solution)/shard_map/while/body/eval_jaxpr/ppermute | solution.py:17
  249.1 21.0 %collective-permute-start = (bf16[1,48,3072]{2,1,0:T(8,128)(2,1)S(1)}, bf16[1,48,3072]{2,1,0:T(8,128)(2,1)S(1)}, u32[]{:S(2)}, u32[]{:S(2)}) collective-permute-start(bf16[1,48,3072]{2,1,0:T(8,128)(2,1)S(1)} %get-tuple-element.1089), channel_id=1, source_target_pairs={{0,4},{4,8},{8,12},{1,5},{5,9},{9,13},{2,6},{6,10},{10,14},{3,7},{... | collective-permute-start | bytes 884744 | tf_op jit(solution)/shard_map/while/body/eval_jaxpr/ppermute | solution.py:17
  273.1 9.1 %collective-permute-start.1 = (bf16[1,48,3072]{2,1,0:T(8,128)(2,1)S(1)}, bf16[1,48,3072]{2,1,0:T(8,128)(2,1)S(1)}, u32[]{:S(2)}, u32[]{:S(2)}) collective-permute-start(bf16[1,48,3072]{2,1,0:T(8,128)(2,1)S(1)} %get-tuple-element.1106), channel_id=1, source_target_pairs={{4,0},{8,4},{12,8},{5,1},{9,5},{13,9},{6,2},{10,6},{14,10},{7,3},{... | collective-permute-start | bytes 884744 | tf_op jit(solution)/shard_map/while/body/eval_jaxpr/ppermute | solution.py:17
  282.2 21.1 %collective-permute-start.1 = (bf16[1,48,3072]{2,1,0:T(8,128)(2,1)S(1)}, bf16[1,48,3072]{2,1,0:T(8,128)(2,1)S(1)}, u32[]{:S(2)}, u32[]{:S(2)}) collective-permute-start(bf16[1,48,3072]{2,1,0:T(8,128)(2,1)S(1)} %get-tuple-element.1106), channel_id=1, source_target_pairs={{4,0},{8,4},{12,8},{5,1},{9,5},{13,9},{6,2},{10,6},{14,10},{7,3},{... | collective-permute-start | bytes 884744 | tf_op jit(solution)/shard_map/while/body/eval_jaxpr/ppermute | solution.py:17
  303.4 88.3 %collective-permute-start.1 = (bf16[1,48,3072]{2,1,0:T(8,128)(2,1)S(1)}, bf16[1,48,3072]{2,1,0:T(8,128)(2,1)S(1)}, u32[]{:S(2)}, u32[]{:S(2)}) collective-permute-start(bf16[1,48,3072]{2,1,0:T(8,128)(2,1)S(1)} %get-tuple-element.1106), channel_id=1, source_target_pairs={{4,0},{8,4},{12,8},{5,1},{9,5},{13,9},{6,2},{10,6},{14,10},{7,3},{... | collective-permute-start | bytes 884744 | tf_op jit(solution)/shard_map/while/body/eval_jaxpr/ppermute | solution.py:17
  391.9 8.0 %copy-start = (f32[1,3072]{1,0:T(1,128)S(1)}, f32[1,3072]{1,0:T(1,128)}, u32[]{:S(2)}) copy-start(f32[1,3072]{1,0:T(1,128)} %get-tuple-element.768) | copy-start | bytes 36868 | tf_op jit(solution)/shard_map/while/body/eval_jaxpr/cond
  418.4 8.6 %collective-permute-start.1 = (bf16[1,48,3072]{2,1,0:T(8,128)(2,1)S(1)}, bf16[1,48,3072]{2,1,0:T(8,128)(2,1)S(1)}, u32[]{:S(2)}, u32[]{:S(2)}) collective-permute-start(bf16[1,48,3072]{2,1,0:T(8,128)(2,1)S(1)} %get-tuple-element.1106), channel_id=1, source_target_pairs={{4,0},{8,4},{12,8},{5,1},{9,5},{13,9},{6,2},{10,6},{14,10},{7,3},{... | collective-permute-start | bytes 884744 | tf_op jit(solution)/shard_map/while/body/eval_jaxpr/ppermute | solution.py:17
  427.3 8.0 %copy-start = (f32[1,3072]{1,0:T(1,128)S(1)}, f32[1,3072]{1,0:T(1,128)}, u32[]{:S(2)}) copy-start(f32[1,3072]{1,0:T(1,128)} %get-tuple-element.768) | copy-start | bytes 36868 | tf_op jit(solution)/shard_map/while/body/eval_jaxpr/cond
  453.7 8.6 %collective-permute-start.1 = (bf16[1,48,3072]{2,1,0:T(8,128)(2,1)S(1)}, bf16[1,48,3072]{2,1,0:T(8,128)(2,1)S(1)}, u32[]{:S(2)}, u32[]{:S(2)}) collective-permute-start(bf16[1,48,3072]{2,1,0:T(8,128)(2,1)S(1)} %get-tuple-element.1106), channel_id=1, source_target_pairs={{4,0},{8,4},{12,8},{5,1},{9,5},{13,9},{6,2},{10,6},{14,10},{7,3},{... | collective-permute-start | bytes 884744 | tf_op jit(solution)/shard_map/while/body/eval_jaxpr/ppermute | solution.py:17
  462.6 8.0 %copy-start = (f32[1,3072]{1,0:T(1,128)S(1)}, f32[1,3072]{1,0:T(1,128)}, u32[]{:S(2)}) copy-start(f32[1,3072]{1,0:T(1,128)} %get-tuple-element.768) | copy-start | bytes 36868 | tf_op jit(solution)/shard_map/while/body/eval_jaxpr/cond
  489.0 8.6 %collective-permute-start.1 = (bf16[1,48,3072]{2,1,0:T(8,128)(2,1)S(1)}, bf16[1,48,3072]{2,1,0:T(8,128)(2,1)S(1)}, u32[]{:S(2)}, u32[]{:S(2)}) collective-permute-start(bf16[1,48,3072]{2,1,0:T(8,128)(2,1)S(1)} %get-tuple-element.1106), channel_id=1, source_target_pairs={{4,0},{8,4},{12,8},{5,1},{9,5},{13,9},{6,2},{10,6},{14,10},{7,3},{... | collective-permute-start | bytes 884744 | tf_op jit(solution)/shard_map/while/body/eval_jaxpr/ppermute | solution.py:17
  505.3 162.0 %reduce-scatter.3.cloned.1.call-start = ((), (), s32[]{:S(2)}) async-start(), calls=%async_computation.4 | async-start | bytes 12779520 | tf_op jit(solution)/shard_map/reduce_scatter | solution.py:220
Sparse Core Ops, SparseCore 0:
  9.6 66.9 all-gather.4
  78.1 68.6 all-gather.2
  505.4 75.6 reduce-scatter.4
  583.6 83.6 reduce-scatter.2
where the time goes:
time: 679 us; the launch traced here: 678 us
  waiting for transfers between devices  442 us (65%)
  matrix products  120 us (18%)
  starting transfers between devices  57.8 us (9%)
  other arithmetic  21.6 us (3%)
  between operations  13.8 us (2%)
  local copies, waits for them, and re-layouts  11.3 us (2%)
  blocking collectives  10.7 us (2%)
    ppermute x12, waiting for transfers between devices, from_behind(): lax.ppermute(value, axis, [(source, source + steps) for source in range(i...  168 us
    reduce_scatter x1, waiting for transfers between devices, body(): lax.psum_scatter(lax.dot_general(columns, rows_joined, (((0,), (0,)), (()...  81.7 us
    all_gather x1, waiting for transfers between devices, body(): lax.all_gather(w_joined, 'dp', axis=1, tiled=True)  70.3 us
    all_gather x1, waiting for transfers between devices, body(): lax.all_gather(w_out, 'dp', axis=1, tiled=True)  66.7 us
    ppermute x12, starting transfers between devices, from_behind(): lax.ppermute(value, axis, [(source, source + steps) for source in range(i...  57.4 us
    reduce_scatter x1, waiting for transfers between devices, body(): lax.psum_scatter(lax.dot_general(columns, rows_upstream, (((0,), (0,)), (...  54.2 us
    dot_general x6, matrix products, project(): jnp.dot(normed.reshape(-1, model_width), weight, preferred_element_type=j...  35.1 us
    dot_general x3, matrix products, layer_backward(): lax.dot_general(grad_joined_rows.reshape(-1, grad_joined_rows.shape[2]),...  21.5 us
  transfers between devices with their start and end apart: 16, of which 16 were waited for; matrix products, arithmetic and copies ran while one was open for 2% of the time, Pallas kernels for 0%

commit v1 on v0

v1 whole, which is shorter than its diff:
```python
import jax
import jax.numpy as jnp
from jax import lax
from jax.sharding import PartitionSpec as P

NUM_HEADS = 24
HEAD_DIM = 64
BLOCK_LEN = 16


EPSILON = 1e-05


def from_behind(value, axis, steps):
    count = lax.axis_size(axis)
    initial, last = (max(0, -steps), min(count, count - steps))
    return lax.ppermute(value, axis, [(source, source + steps) for source in range(initial, last)])


def allowed_tokens(links, block_len):
    count = links.shape[1]
    block_hits = links[:, :, :, None] == jnp.arange(count, dtype=jnp.int32)[None, None, None, :]
    blocks = jnp.any(block_hits, axis=2)
    return jnp.repeat(jnp.repeat(blocks, block_len, axis=1), block_len, axis=2)


def normalize(stream, gain_row):
    stream_wide = stream.astype(jnp.float32)
    inv_rms = lax.rsqrt(jnp.mean(stream_wide * stream_wide, axis=-1, keepdims=True) + EPSILON)
    normed = (stream_wide * inv_rms * gain_row).astype(jnp.bfloat16)
    return (stream_wide, inv_rms, normed)


def project(normed, weight):
    batch_size, length, model_width = normed.shape
    flat = jnp.dot(normed.reshape(-1, model_width), weight, preferred_element_type=jnp.float32)
    return flat.astype(jnp.bfloat16).reshape(batch_size, length, weight.shape[1])


def attend(joined_rows, allowed):
    batch_size, length, _ = joined_rows.shape
    inner_width = NUM_HEADS * HEAD_DIM
    queries = joined_rows[:, :, :inner_width].reshape(batch_size, length, NUM_HEADS, HEAD_DIM)
    key_rows = joined_rows[:, :, inner_width : inner_width + HEAD_DIM]
    values = joined_rows[:, :, inner_width + HEAD_DIM :]
    scores = jnp.einsum(
        "bihd,bjd->bhij", queries, key_rows, preferred_element_type=jnp.float32
    ) * HEAD_DIM ** (-0.5)
    scores = jnp.where(allowed[:, None], scores, -1e30)
    row_max = jnp.max(scores, axis=-1, keepdims=True)
    exp_scores = jnp.exp(scores - row_max)
    attn_probs = exp_scores / jnp.sum(exp_scores, axis=-1, keepdims=True)
    probs_half = attn_probs.astype(jnp.bfloat16)
    mixed_heads = jnp.einsum(
        "bhij,bjd->bihd", probs_half, values, preferred_element_type=jnp.float32
    )
    mixed_heads = mixed_heads.astype(jnp.bfloat16).reshape(batch_size, length, inner_width)
    return (queries, key_rows, values, attn_probs, probs_half, mixed_heads)


def layer_forward(stream, gain_row, w_joined, w_out, allowed):
    stream_wide, inv_rms, normed = normalize(stream, gain_row)
    joined_rows = project(normed, w_joined)
    _, _, _, attn_probs, _, mixed_heads = attend(joined_rows, allowed)
    batch_size, length, model_width = stream.shape
    update = jnp.dot(
        mixed_heads.reshape(-1, mixed_heads.shape[2]), w_out, preferred_element_type=jnp.float32
    )
    result = (stream_wide + update.reshape(batch_size, length, model_width)).astype(jnp.bfloat16)
    return (result, normed, joined_rows, attn_probs, mixed_heads)


def layer_backward(stream, gain_row, joined_rows, attn_probs, w_joined, w_out, upstream):
    batch_size, length, model_width = stream.shape
    inner_width = NUM_HEADS * HEAD_DIM
    stream_wide = stream.astype(jnp.float32)
    inv_rms = lax.rsqrt(jnp.mean(stream_wide * stream_wide, axis=-1, keepdims=True) + EPSILON)
    queries = joined_rows[:, :, :inner_width].reshape(batch_size, length, NUM_HEADS, HEAD_DIM)
    key_rows = joined_rows[:, :, inner_width : inner_width + HEAD_DIM]
    values = joined_rows[:, :, inner_width + HEAD_DIM :]
    probs_half = attn_probs.astype(jnp.bfloat16)
    grad_mixed = lax.dot_general(
        upstream.reshape(-1, model_width),
        w_out,
        (((1,), (1,)), ((), ())),
        preferred_element_type=jnp.float32,
    )
    grad_mixed = grad_mixed.astype(jnp.bfloat16).reshape(batch_size, length, NUM_HEADS, HEAD_DIM)
    grad_probs = jnp.einsum(
        "bihd,bjd->bhij", grad_mixed, values, preferred_element_type=jnp.float32
    )
    grad_values = jnp.einsum(
        "bhij,bihd->bjd", probs_half, grad_mixed, preferred_element_type=jnp.float32
    )
    inner_sum = jnp.sum(attn_probs * grad_probs, axis=-1, keepdims=True)
    grad_scores = (attn_probs * (grad_probs - inner_sum) * HEAD_DIM ** (-0.5)).astype(jnp.bfloat16)
    grad_queries = jnp.einsum(
        "bhij,bjd->bihd", grad_scores, key_rows, preferred_element_type=jnp.float32
    )
    grad_keys = jnp.einsum(
        "bhij,bihd->bjd", grad_scores, queries, preferred_element_type=jnp.float32
    )
    grad_joined_rows = jnp.concatenate(
        [grad_queries.reshape(batch_size, length, inner_width), grad_keys, grad_values], axis=-1
    ).astype(jnp.bfloat16)
    grad_normed = lax.dot_general(
        grad_joined_rows.reshape(-1, grad_joined_rows.shape[2]),
        w_joined,
        (((1,), (1,)), ((), ())),
        preferred_element_type=jnp.float32,
    )
    grad_normed = grad_normed.reshape(batch_size, length, model_width)
    gained = grad_normed * gain_row
    grad_stream = inv_rms * gained - stream_wide * inv_rms**3 * jnp.mean(
        stream_wide * gained, axis=-1, keepdims=True
    )
    down_grad = (upstream.astype(jnp.float32) + grad_stream).astype(jnp.bfloat16)
    gain_part = jnp.sum((grad_normed * stream_wide * inv_rms).reshape(-1, model_width), axis=0)
    return (down_grad, grad_joined_rows, gain_part)


def pick(stack, index):
    return lax.dynamic_index_in_dim(stack, index, 0, keepdims=False)


def gather_weights(w_joined, w_out):
    return (
        lax.all_gather(w_joined[0], "dp", axis=0, tiled=True),
        lax.all_gather(w_out[0], "dp", axis=0, tiled=True),
    )


def share_columns(rows):
    n = lax.axis_size("dp")
    me = lax.axis_index("dp")
    slots, length, total = rows.shape
    width = total // n
    taken = jnp.zeros((slots, n, length, width), rows.dtype)
    for shift in range(n):
        target = lax.rem(me + shift, n)
        piece = lax.dynamic_slice_in_dim(rows, target * width, width, 2)
        if shift:
            piece = lax.ppermute(piece, "dp", [(i, (i + shift) % n) for i in range(n)])
        source = lax.rem(me + n - shift, n)
        taken = lax.dynamic_update_slice_in_dim(taken, piece[:, None], source, 1)
    return taken


def body(stream_in, out_grad, mask_blocks, norm_gain, w_joined, w_out):
    full_joined, full_out = gather_weights(w_joined, w_out)
    gain_row = norm_gain[0]
    sections = lax.axis_size("section")
    section_index = lax.axis_index("section")
    micro_count = mask_blocks.shape[0]
    model_width = stream_in.shape[1]
    length = stream_in.shape[0] // micro_count
    inputs = stream_in.reshape(micro_count, 1, length, model_width)
    upstreams = out_grad.reshape(micro_count, 1, length, model_width)
    allowed = allowed_tokens(mask_blocks, BLOCK_LEN).reshape(micro_count, 1, length, length)
    step_count = micro_count + sections - 1

    def forward_step(step, state):
        incoming, kept = state
        slot = step - section_index
        active = jnp.logical_and(slot >= 0, slot < micro_count)
        group_index = jnp.clip(slot, 0, micro_count - 1)
        source = jnp.where(section_index == 0, pick(inputs, group_index), incoming)
        result, normed, joined_rows, attn_probs, mixed_heads = layer_forward(
            source, gain_row, full_joined, full_out, pick(allowed, group_index)
        )
        place = jnp.where(active, group_index, micro_count)
        values = (source, joined_rows, attn_probs, normed, mixed_heads)
        kept = tuple(
            lax.dynamic_update_index_in_dim(store, value, place, 0)
            for store, value in zip(kept, values)
        )
        return (from_behind(result, "section", 1), kept)

    def store_of(*shape, dtype=jnp.bfloat16):
        return jnp.zeros((micro_count + 1,) + shape, dtype)

    joined_width = full_joined.shape[1]
    inner_width = full_out.shape[0]
    rest = jnp.zeros((1, length, model_width), jnp.bfloat16)
    kept = (
        store_of(1, length, model_width),
        store_of(1, length, joined_width),
        store_of(1, NUM_HEADS, length, length, dtype=jnp.float32),
        store_of(1, length, model_width),
        store_of(1, length, inner_width),
    )
    _, kept = lax.fori_loop(0, step_count, forward_step, (rest, kept))
    sources, joineds, probs, normeds, mixeds = kept
    columns_normed = share_columns(normeds[:micro_count, 0])
    columns_mixed = share_columns(mixeds[:micro_count, 0])

    behind = sections - 1 - section_index
    replicas = lax.axis_size("dp")

    def place_of(slot):
        return jnp.where(jnp.logical_and(slot >= 0, slot < micro_count), slot, micro_count)

    def backward_step(step, state):
        incoming, last_rows, all_upstream, all_joined, gain_sum = state
        slot = step - behind
        active = jnp.logical_and(slot >= 0, slot < micro_count)
        group_index = jnp.clip(slot, 0, micro_count - 1)
        upstream = jnp.where(section_index == sections - 1, pick(upstreams, group_index), incoming)
        shared_upstream = lax.all_gather(upstream[0], "dp", axis=0)
        shared_joined = lax.all_gather(last_rows, "dp", axis=0)
        down_grad, grad_joined_rows, gain_part = layer_backward(
            pick(sources, group_index),
            gain_row,
            pick(joineds, group_index),
            pick(probs, group_index),
            full_joined,
            full_out,
            upstream,
        )
        all_upstream = lax.dynamic_update_index_in_dim(
            all_upstream, shared_upstream, place_of(slot), 0
        )
        all_joined = lax.dynamic_update_index_in_dim(
            all_joined, shared_joined, place_of(slot - 1), 0
        )
        gain_sum = gain_sum + jnp.where(active, gain_part, 0.0)
        incoming = from_behind(down_grad, "section", -1)
        return (incoming, grad_joined_rows[0], all_upstream, all_joined, gain_sum)

    start_back = (
        rest,
        jnp.zeros((length, joined_width), jnp.bfloat16),
        store_of(replicas, length, model_width),
        store_of(replicas, length, joined_width),
        jnp.zeros((model_width,), jnp.float32),
    )
    _, last_rows, all_upstream, all_joined, gain_sum = lax.fori_loop(
        0, step_count, backward_step, start_back
    )
    all_joined = lax.dynamic_update_index_in_dim(
        all_joined,
        lax.all_gather(last_rows, "dp", axis=0),
        place_of(step_count - 1 - behind),
        0,
    )
    gain_total = jnp.sum(lax.all_gather(gain_sum, "dp", axis=0), axis=0)
    valid_upstream = all_upstream[:micro_count]
    valid_joined = all_joined[:micro_count]

    def flat(rows):
        return rows.reshape(-1, rows.shape[-1])

    over_rows = (((0,), (0,)), ((), ()))
    grad_joined = lax.dot_general(
        flat(columns_normed), flat(valid_joined), over_rows, preferred_element_type=jnp.float32
    )
    grad_output = lax.dot_general(
        flat(columns_mixed), flat(valid_upstream), over_rows, preferred_element_type=jnp.float32
    )
    return (grad_joined[None], grad_output[None], gain_total[None])


def solution(mesh):
    return jax.shard_map(
        body,
        mesh=mesh,
        in_specs=(
            P(("groups", "dp"), None),
            P(("groups", "dp"), None),
            P(("groups", "dp"), None, None),
            P("section", None),
            P("section", "dp", None),
            P("section", "dp", None),
        ),
        out_specs=(
            P(("groups", "section"), "dp", None),
            P(("groups", "section"), "dp", None),
            P(("groups", "section"), None),
        ),
        check_vma=False,
    )
```

time: 679 us -> 667 us (0.982)
  waiting for transfers between devices: 442 us -> 188 us
  matrix products: 120 us -> 208 us
  local copies, waits for them, and re-layouts: 11.3 us -> 90.4 us
  blocking collectives: 10.7 us -> 58.4 us
  other arithmetic: 21.6 us -> 60.8 us
  starting transfers between devices: 57.8 us -> 40.5 us
    reduce_scatter x2 -> x0, waiting for transfers between devices: 136 us -> none  [the longest x1 81.7 us: body(): lax.psum_scatter(lax.dot_general(columns, rows_joined, (((0,), (0,)), (()...]
    ppermute x12, waiting for transfers between devices: 168 us -> 45.4 us  [from_behind(): lax.ppermute(value, axis, [(source, source + steps) for source in range(i...]
    all_gather x0 -> x8, blocking collectives: none -> 58.4 us  [the longest x6 44.4 us: backward_step(): shared_joined = lax.all_gather(last_rows, 'dp', axis=0)]
    dynamic_update_slice x6 -> x25, local copies, waits for them, and re-layouts: 2.08 us -> 35.6 us  [the longest x6 14.2 us: backward_step(): lax.dynamic_update_index_in_dim(all_upstream, shared_upstream, place_of(s...]
    dot_general x3 -> x6, matrix products: 21.5 us -> 43.3 us  [layer_backward(): lax.dot_general(grad_joined_rows.reshape(-1, grad_joined_rows.shape[2]),...]
    dot_general x3 -> x6, matrix products: 16.3 us -> 37.3 us  [layer_forward(): jnp.dot(mixed_heads.reshape(-1, mixed_heads.shape[2]), w_out, preferred_e...]
    dot_general x3 -> x6, matrix products: 19.9 us -> 40.7 us  [layer_backward(): lax.dot_general(upstream.reshape(-1, model_width), w_out, (((1,), (1,)),...]
    ppermute x12, starting transfers between devices: 57.4 us -> 37.1 us  [from_behind(): lax.ppermute(value, axis, [(source, source + steps) for source in range(i...]
  transfers between devices with their start and end apart: 16 -> 26, of which waited for: 16 -> 12; matrix products, arithmetic and copies ran while one was open for 2% -> 33% of each run, Pallas kernels for 0% -> 0%
where the time goes in v1:
time: 667 us; the launch traced here: 663 us
  matrix products  208 us (31%)
  waiting for transfers between devices  188 us (28%)
  local copies, waits for them, and re-layouts  90.4 us (14%)
  other arithmetic  60.8 us (9%)
  blocking collectives  58.4 us (9%)
  starting transfers between devices  40.5 us (6%)
  between operations  14.3 us (2%)
    all_gather x1, waiting for transfers between devices, gather_weights(): lax.all_gather(w_joined[0], 'dp', axis=0, tiled=True)  70.3 us
    all_gather x1, waiting for transfers between devices, gather_weights(): lax.all_gather(w_out[0], 'dp', axis=0, tiled=True)  67.4 us
    ppermute x12, waiting for transfers between devices, from_behind(): lax.ppermute(value, axis, [(source, source + steps) for source in range(i...  45.4 us
    all_gather x6, blocking collectives, backward_step(): shared_joined = lax.all_gather(last_rows, 'dp', axis=0)  44.4 us
    dot_general x6, matrix products, layer_backward(): lax.dot_general(grad_joined_rows.reshape(-1, grad_joined_rows.shape[2]),...  43.3 us
    dot_general x6, matrix products, layer_backward(): lax.dot_general(upstream.reshape(-1, model_width), w_out, (((1,), (1,)),...  40.7 us
    dot_general x6, matrix products, project(): jnp.dot(normed.reshape(-1, model_width), weight, preferred_element_type=j...  39.1 us
    dot_general x6, matrix products, layer_forward(): jnp.dot(mixed_heads.reshape(-1, mixed_heads.shape[2]), w_out, preferred_e...  37.3 us
  transfers between devices with their start and end apart: 26, of which 12 were waited for; matrix products, arithmetic and copies ran while one was open for 33% of the time, Pallas kernels for 0%

profile of v1, /device:TPU:0, one launch (start us, length us, event | category | flops | bytes accessed | tf_op | source)
XLA Modules:
  0.0 662.7 jit_solution(814957823230022412)
XLA Ops:
  9.2 67.4 %all-gather.14.cloned.1.call-done = bf16[1,1536,3072]{2,1,0:T(8,128)(2,1)} async-done(((bf16[1,384,3072]{2,1,0:T(8,128)(2,1)}), bf16[1,1536,3072]{2,1,0:T(8,128)(2,1)}) %all-gather.14.cloned.1.call-update) | async-done | bytes 9437200 | tf_op jit(solution)/shard_map/all_gather | solution.py:129
  76.5 70.3 %all-gather.12.cloned.1.call-done = bf16[1,3072,1664]{2,1,0:T(8,128)(2,1)} async-done(((bf16[1,768,1664]{2,1,0:T(8,128)(2,1)}), bf16[1,3072,1664]{2,1,0:T(8,128)(2,1)}) %all-gather.12.cloned.1.call-update) | async-done | bytes 10223632 | tf_op jit(solution)/shard_map/all_gather | solution.py:128
  152.4 185.4 %while.48 = (s32[]{:T(128)}, bf16[1,48,3072]{2,1,0:T(8,128)(2,1)}, bf16[4,1,48,3072]{3,2,1,0:T(8,128)(2,1)}, bf16[4,1,48,1664]{3,2,1,0:T(8,128)(2,1)}, f32[4,1,2...) while((s32[]{:T(128)}, bf16[1,48,3072]{2,1,0:T(8,128)(2,1)}, ...), condition=%wide.region_5.6_spmd, body=%wide.region_1.5_spmd.sunk | while | flops 960790336 | bytes 28933956 | solution.py:192
  250.1 6.5 bitcast_dynamic-update-slice_fusion.17
  280.6 6.5 bitcast_dynamic-update-slice_fusion.17
  310.8 6.5 bitcast_dynamic-update-slice_fusion.17
  348.5 270.0 %while.49 = (s32[]{:T(128)}, bf16[1,48,3072]{2,1,0:T(8,128)(2,1)}, bf16[48,1664]{1,0:T(8,128)(2,1)S(1)}, bf16[4,4,48,3072]{3,2,1,0:T(8,128)(2,1)}, bf16[4,4,48,1...) while((s32[]{:T(128)}, bf16[1,48,3072]{2,1,0:T(8,128)(2,1)}, ...), condition=%wide.region_11.12_spmd.clone, body=%wide.region_6.11_spmd.clone.sunk | while | flops 975469632 | bytes 40366604 | solution.py:237
  351.3 6.8 %convolution_convert_fusion.5 = bf16[48,1536]{1,0:T(8,128)(2,1)S(1)} fusion(bf16[1536,3072]{1,0:T(8,128)(2,1)} %get-tuple-element.1081, bf16[1,48,3072]{2,1,0:T(8,128)(2,1)} %bitcast_select_fusion.4), kind=kOutput, calls=%fused_computation.31.clone.1 | convolution fusion | flops 453058560 | bytes 9879552 | tf_op jit(solution)/shard_map/while/body/eval_jaxpr/dot_general | solution.py:82
  365.2 7.8 %all-gather.7 = bf16[192,1664]{1,0:T(8,128)(2,1)S(1)} all-gather(bf16[48,1664]{1,0:T(8,128)(2,1)S(1)} %get-tuple-element.1050), channel_id=2, replica_groups=mesh['groups'=2,'section'=4,'dp'=4] {'dp'}, dimensions={0}, use_global_device_ids=true | all-gather | bytes 798720 | tf_op jit(solution)/shard_map/while/body/eval_jaxpr/all_gather | solution.py:210
  373.1 7.2 %fusion.106 = (f32[3072]{0:T(1024)S(1)}, f32[48]{0:T(128)S(1)}, f32[48,3072]{1,0:T(8,128)S(1)}) fusion(f32[48]{0:T(128)S(1)} %get-tuple-element.966, bf16[4,1,48,3072]{3,2,1,0:T(8,128)(2,1)} %get-tuple-element.1078, s32[]{:T(128)S(6)} %min.23, f32[3072]{0:T(1024)S(1)} %bitcast.279, bf16[48,1664]{1,0:T(8,128)(2,1)S(1)} %concatenate.21, ...), kind=kOutput, calls=%fused_computation.52.clone.1 | convolution fusion | flops 491762624 | bytes 11293060 | tf_op jit(solution)/shard_map/while/body/eval_jaxpr/dot_general | solution.py:106
  387.0 7.3 %collective-permute-done.1 = bf16[1,48,3072]{2,1,0:T(8,128)(2,1)} collective-permute-done((bf16[1,48,3072]{2,1,0:T(8,128)(2,1)}, bf16[1,48,3072]{2,1,0:T(8,128)(2,1)}, u32[]{:S(2)}, u32[]{:S(2)}) %collective-permute-start.1) | collective-permute-done | bytes 294944 | tf_op jit(solution)/shard_map/while/body/eval_jaxpr/ppermute | solution.py:17
  397.1 6.8 %convolution_convert_fusion.5 = bf16[48,1536]{1,0:T(8,128)(2,1)S(1)} fusion(bf16[1536,3072]{1,0:T(8,128)(2,1)} %get-tuple-element.1081, bf16[1,48,3072]{2,1,0:T(8,128)(2,1)} %bitcast_select_fusion.4), kind=kOutput, calls=%fused_computation.31.clone.1 | convolution fusion | flops 453058560 | bytes 9879552 | tf_op jit(solution)/shard_map/while/body/eval_jaxpr/dot_general | solution.py:82
  411.0 7.3 %all-gather.7 = bf16[192,1664]{1,0:T(8,128)(2,1)S(1)} all-gather(bf16[48,1664]{1,0:T(8,128)(2,1)S(1)} %get-tuple-element.1050), channel_id=2, replica_groups=mesh['groups'=2,'section'=4,'dp'=4] {'dp'}, dimensions={0}, use_global_device_ids=true | all-gather | bytes 798720 | tf_op jit(solution)/shard_map/while/body/eval_jaxpr/all_gather | solution.py:210
  418.5 7.2 %fusion.106 = (f32[3072]{0:T(1024)S(1)}, f32[48]{0:T(128)S(1)}, f32[48,3072]{1,0:T(8,128)S(1)}) fusion(f32[48]{0:T(128)S(1)} %get-tuple-element.966, bf16[4,1,48,3072]{3,2,1,0:T(8,128)(2,1)} %get-tuple-element.1078, s32[]{:T(128)S(6)} %min.23, f32[3072]{0:T(1024)S(1)} %bitcast.279, bf16[48,1664]{1,0:T(8,128)(2,1)S(1)} %concatenate.21, ...), kind=kOutput, calls=%fused_computation.52.clone.1 | convolution fusion | flops 491762624 | bytes 11293060 | tf_op jit(solution)/shard_map/while/body/eval_jaxpr/dot_general | solution.py:106
  432.3 6.8 %collective-permute-done.1 = bf16[1,48,3072]{2,1,0:T(8,128)(2,1)} collective-permute-done((bf16[1,48,3072]{2,1,0:T(8,128)(2,1)}, bf16[1,48,3072]{2,1,0:T(8,128)(2,1)}, u32[]{:S(2)}, u32[]{:S(2)}) %collective-permute-start.1) | collective-permute-done | bytes 294944 | tf_op jit(solution)/shard_map/while/body/eval_jaxpr/ppermute | solution.py:17
  441.9 6.8 %convolution_convert_fusion.5 = bf16[48,1536]{1,0:T(8,128)(2,1)S(1)} fusion(bf16[1536,3072]{1,0:T(8,128)(2,1)} %get-tuple-element.1081, bf16[1,48,3072]{2,1,0:T(8,128)(2,1)} %bitcast_select_fusion.4), kind=kOutput, calls=%fused_computation.31.clone.1 | convolution fusion | flops 453058560 | bytes 9879552 | tf_op jit(solution)/shard_map/while/body/eval_jaxpr/dot_general | solution.py:82
  455.9 7.3 %all-gather.7 = bf16[192,1664]{1,0:T(8,128)(2,1)S(1)} all-gather(bf16[48,1664]{1,0:T(8,128)(2,1)S(1)} %get-tuple-element.1050), channel_id=2, replica_groups=mesh['groups'=2,'section'=4,'dp'=4] {'dp'}, dimensions={0}, use_global_device_ids=true | all-gather | bytes 798720 | tf_op jit(solution)/shard_map/while/body/eval_jaxpr/all_gather | solution.py:210
  463.3 7.2 %fusion.106 = (f32[3072]{0:T(1024)S(1)}, f32[48]{0:T(128)S(1)}, f32[48,3072]{1,0:T(8,128)S(1)}) fusion(f32[48]{0:T(128)S(1)} %get-tuple-element.966, bf16[4,1,48,3072]{3,2,1,0:T(8,128)(2,1)} %get-tuple-element.1078, s32[]{:T(128)S(6)} %min.23, f32[3072]{0:T(1024)S(1)} %bitcast.279, bf16[48,1664]{1,0:T(8,128)(2,1)S(1)} %concatenate.21, ...), kind=kOutput, calls=%fused_computation.52.clone.1 | convolution fusion | flops 491762624 | bytes 11293060 | tf_op jit(solution)/shard_map/while/body/eval_jaxpr/dot_general | solution.py:106
  477.1 6.8 %collective-permute-done.1 = bf16[1,48,3072]{2,1,0:T(8,128)(2,1)} collective-permute-done((bf16[1,48,3072]{2,1,0:T(8,128)(2,1)}, bf16[1,48,3072]{2,1,0:T(8,128)(2,1)}, u32[]{:S(2)}, u32[]{:S(2)}) %collective-permute-start.1) | collective-permute-done | bytes 294944 | tf_op jit(solution)/shard_map/while/body/eval_jaxpr/ppermute | solution.py:17
  486.8 6.8 %convolution_convert_fusion.5 = bf16[48,1536]{1,0:T(8,128)(2,1)S(1)} fusion(bf16[1536,3072]{1,0:T(8,128)(2,1)} %get-tuple-element.1081, bf16[1,48,3072]{2,1,0:T(8,128)(2,1)} %bitcast_select_fusion.4), kind=kOutput, calls=%fused_computation.31.clone.1 | convolution fusion | flops 453058560 | bytes 9879552 | tf_op jit(solution)/shard_map/while/body/eval_jaxpr/dot_general | solution.py:82
  500.7 7.3 %all-gather.7 = bf16[192,1664]{1,0:T(8,128)(2,1)S(1)} all-gather(bf16[48,1664]{1,0:T(8,128)(2,1)S(1)} %get-tuple-element.1050), channel_id=2, replica_groups=mesh['groups'=2,'section'=4,'dp'=4] {'dp'}, dimensions={0}, use_global_device_ids=true | all-gather | bytes 798720 | tf_op jit(solution)/shard_map/while/body/eval_jaxpr/all_gather | solution.py:210
  508.2 7.2 %fusion.106 = (f32[3072]{0:T(1024)S(1)}, f32[48]{0:T(128)S(1)}, f32[48,3072]{1,0:T(8,128)S(1)}) fusion(f32[48]{0:T(128)S(1)} %get-tuple-element.966, bf16[4,1,48,3072]{3,2,1,0:T(8,128)(2,1)} %get-tuple-element.1078, s32[]{:T(128)S(6)} %min.23, f32[3072]{0:T(1024)S(1)} %bitcast.279, bf16[48,1664]{1,0:T(8,128)(2,1)S(1)} %concatenate.21, ...), kind=kOutput, calls=%fused_computation.52.clone.1 | convolution fusion | flops 491762624 | bytes 11293060 | tf_op jit(solution)/shard_map/while/body/eval_jaxpr/dot_general | solution.py:106
  522.0 6.8 %collective-permute-done.1 = bf16[1,48,3072]{2,1,0:T(8,128)(2,1)} collective-permute-done((bf16[1,48,3072]{2,1,0:T(8,128)(2,1)}, bf16[1,48,3072]{2,1,0:T(8,128)(2,1)}, u32[]{:S(2)}, u32[]{:S(2)}) %collective-permute-start.1) | collective-permute-done | bytes 294944 | tf_op jit(solution)/shard_map/while/body/eval_jaxpr/ppermute | solution.py:17
  531.6 6.8 %convolution_convert_fusion.5 = bf16[48,1536]{1,0:T(8,128)(2,1)S(1)} fusion(bf16[1536,3072]{1,0:T(8,128)(2,1)} %get-tuple-element.1081, bf16[1,48,3072]{2,1,0:T(8,128)(2,1)} %bitcast_select_fusion.4), kind=kOutput, calls=%fused_computation.31.clone.1 | convolution fusion | flops 453058560 | bytes 9879552 | tf_op jit(solution)/shard_map/while/body/eval_jaxpr/dot_general | solution.py:82
  545.6 7.3 %all-gather.7 = bf16[192,1664]{1,0:T(8,128)(2,1)S(1)} all-gather(bf16[48,1664]{1,0:T(8,128)(2,1)S(1)} %get-tuple-element.1050), channel_id=2, replica_groups=mesh['groups'=2,'section'=4,'dp'=4] {'dp'}, dimensions={0}, use_global_device_ids=true | all-gather | bytes 798720 | tf_op jit(solution)/shard_map/while/body/eval_jaxpr/all_gather | solution.py:210
  553.0 7.2 %fusion.106 = (f32[3072]{0:T(1024)S(1)}, f32[48]{0:T(128)S(1)}, f32[48,3072]{1,0:T(8,128)S(1)}) fusion(f32[48]{0:T(128)S(1)} %get-tuple-element.966, bf16[4,1,48,3072]{3,2,1,0:T(8,128)(2,1)} %get-tuple-element.1078, s32[]{:T(128)S(6)} %min.23, f32[3072]{0:T(1024)S(1)} %bitcast.279, bf16[48,1664]{1,0:T(8,128)(2,1)S(1)} %concatenate.21, ...), kind=kOutput, calls=%fused_computation.52.clone.1 | convolution fusion | flops 491762624 | bytes 11293060 | tf_op jit(solution)/shard_map/while/body/eval_jaxpr/dot_general | solution.py:106
  566.8 6.9 %collective-permute-done.1 = bf16[1,48,3072]{2,1,0:T(8,128)(2,1)} collective-permute-done((bf16[1,48,3072]{2,1,0:T(8,128)(2,1)}, bf16[1,48,3072]{2,1,0:T(8,128)(2,1)}, u32[]{:S(2)}, u32[]{:S(2)}) %collective-permute-start.1) | collective-permute-done | bytes 294944 | tf_op jit(solution)/shard_map/while/body/eval_jaxpr/ppermute | solution.py:17
  576.5 6.8 %convolution_convert_fusion.5 = bf16[48,1536]{1,0:T(8,128)(2,1)S(1)} fusion(bf16[1536,3072]{1,0:T(8,128)(2,1)} %get-tuple-element.1081, bf16[1,48,3072]{2,1,0:T(8,128)(2,1)} %bitcast_select_fusion.4), kind=kOutput, calls=%fused_computation.31.clone.1 | convolution fusion | flops 453058560 | bytes 9879552 | tf_op jit(solution)/shard_map/while/body/eval_jaxpr/dot_general | solution.py:82
  590.4 7.3 %all-gather.7 = bf16[192,1664]{1,0:T(8,128)(2,1)S(1)} all-gather(bf16[48,1664]{1,0:T(8,128)(2,1)S(1)} %get-tuple-element.1050), channel_id=2, replica_groups=mesh['groups'=2,'section'=4,'dp'=4] {'dp'}, dimensions={0}, use_global_device_ids=true | all-gather | bytes 798720 | tf_op jit(solution)/shard_map/while/body/eval_jaxpr/all_gather | solution.py:210
  597.9 7.2 %fusion.106 = (f32[3072]{0:T(1024)S(1)}, f32[48]{0:T(128)S(1)}, f32[48,3072]{1,0:T(8,128)S(1)}) fusion(f32[48]{0:T(128)S(1)} %get-tuple-element.966, bf16[4,1,48,3072]{3,2,1,0:T(8,128)(2,1)} %get-tuple-element.1078, s32[]{:T(128)S(6)} %min.23, f32[3072]{0:T(1024)S(1)} %bitcast.279, bf16[48,1664]{1,0:T(8,128)(2,1)S(1)} %concatenate.21, ...), kind=kOutput, calls=%fused_computation.52.clone.1 | convolution fusion | flops 491762624 | bytes 11293060 | tf_op jit(solution)/shard_map/while/body/eval_jaxpr/dot_general | solution.py:106
  611.7 6.8 %collective-permute-done.1 = bf16[1,48,3072]{2,1,0:T(8,128)(2,1)} collective-permute-done((bf16[1,48,3072]{2,1,0:T(8,128)(2,1)}, bf16[1,48,3072]{2,1,0:T(8,128)(2,1)}, u32[]{:S(2)}, u32[]{:S(2)}) %collective-permute-start.1) | collective-permute-done | bytes 294944 | tf_op jit(solution)/shard_map/while/body/eval_jaxpr/ppermute | solution.py:17
  618.5 8.6 %all-gather.3 = bf16[192,1664]{1,0:T(8,128)(2,1)S(1)} all-gather(bf16[48,1664]{1,0:T(8,128)(2,1)S(1)} %get-tuple-element.640), channel_id=5, replica_groups=mesh['groups'=2,'section'=4,'dp'=4] {'dp'}, dimensions={0}, use_global_device_ids=true | all-gather | bytes 798720 | tf_op jit(solution)/shard_map/all_gather | solution.py:242
  (451 shorter events, 310.9 us)
Async XLA Ops:
  7.2 69.4 %all-gather.14.cloned.1.call-start = ((), (), s32[]{:S(2)}) async-start(), calls=%async_computation.1 | async-start | bytes 11796480 | tf_op jit(solution)/shard_map/all_gather | solution.py:129
  7.9 138.9 %all-gather.12.cloned.1.call-start = ((), (), s32[]{:S(2)}) async-start(), calls=%async_computation | async-start | bytes 12779520 | tf_op jit(solution)/shard_map/all_gather | solution.py:128
  173.6 10.5 %collective-permute-start = (bf16[1,48,3072]{2,1,0:T(8,128)(2,1)}, bf16[1,48,3072]{2,1,0:T(8,128)(2,1)}, u32[]{:S(2)}, u32[]{:S(2)}) collective-permute-start(bf16[1,48,3072]{2,1,0:T(8,128)(2,1)} %fusion.90), channel_id=1, source_target_pairs={{0,4},{4,8},{8,12},{1,5},{5,9},{9,13},{2,6},{6,10},{10,14},{3,7},{... | collective-permute-start | bytes 884744 | tf_op jit(solution)/shard_map/while/body/eval_jaxpr/ppermute | solution.py:17
  205.3 10.6 %collective-permute-start = (bf16[1,48,3072]{2,1,0:T(8,128)(2,1)}, bf16[1,48,3072]{2,1,0:T(8,128)(2,1)}, u32[]{:S(2)}, u32[]{:S(2)}) collective-permute-start(bf16[1,48,3072]{2,1,0:T(8,128)(2,1)} %fusion.90), channel_id=1, source_target_pairs={{0,4},{4,8},{8,12},{1,5},{5,9},{9,13},{2,6},{6,10},{10,14},{3,7},{... | collective-permute-start | bytes 884744 | tf_op jit(solution)/shard_map/while/body/eval_jaxpr/ppermute | solution.py:17
  237.1 9.7 %collective-permute-start = (bf16[1,48,3072]{2,1,0:T(8,128)(2,1)}, bf16[1,48,3072]{2,1,0:T(8,128)(2,1)}, u32[]{:S(2)}, u32[]{:S(2)}) collective-permute-start(bf16[1,48,3072]{2,1,0:T(8,128)(2,1)} %fusion.90), channel_id=1, source_target_pairs={{0,4},{4,8},{8,12},{1,5},{5,9},{9,13},{2,6},{6,10},{10,14},{3,7},{... | collective-permute-start | bytes 884744 | tf_op jit(solution)/shard_map/while/body/eval_jaxpr/ppermute | solution.py:17
  268.1 9.3 %collective-permute-start = (bf16[1,48,3072]{2,1,0:T(8,128)(2,1)}, bf16[1,48,3072]{2,1,0:T(8,128)(2,1)}, u32[]{:S(2)}, u32[]{:S(2)}) collective-permute-start(bf16[1,48,3072]{2,1,0:T(8,128)(2,1)} %fusion.90), channel_id=1, source_target_pairs={{0,4},{4,8},{8,12},{1,5},{5,9},{9,13},{2,6},{6,10},{10,14},{3,7},{... | collective-permute-start | bytes 884744 | tf_op jit(solution)/shard_map/while/body/eval_jaxpr/ppermute | solution.py:17
  298.6 9.0 %collective-permute-start = (bf16[1,48,3072]{2,1,0:T(8,128)(2,1)}, bf16[1,48,3072]{2,1,0:T(8,128)(2,1)}, u32[]{:S(2)}, u32[]{:S(2)}) collective-permute-start(bf16[1,48,3072]{2,1,0:T(8,128)(2,1)} %fusion.90), channel_id=1, source_target_pairs={{0,4},{4,8},{8,12},{1,5},{5,9},{9,13},{2,6},{6,10},{10,14},{3,7},{... | collective-permute-start | bytes 884744 | tf_op jit(solution)/shard_map/while/body/eval_jaxpr/ppermute | solution.py:17
  328.8 9.0 %collective-permute-start = (bf16[1,48,3072]{2,1,0:T(8,128)(2,1)}, bf16[1,48,3072]{2,1,0:T(8,128)(2,1)}, u32[]{:S(2)}, u32[]{:S(2)}) collective-permute-start(bf16[1,48,3072]{2,1,0:T(8,128)(2,1)} %fusion.90), channel_id=1, source_target_pairs={{0,4},{4,8},{8,12},{1,5},{5,9},{9,13},{2,6},{6,10},{10,14},{3,7},{... | collective-permute-start | bytes 884744 | tf_op jit(solution)/shard_map/while/body/eval_jaxpr/ppermute | solution.py:17
  340.1 310.2 %collective-permute-start.4 = (bf16[3,48,768]{2,1,0:T(8,128)(2,1)}, bf16[3,48,768]{2,1,0:T(8,128)(2,1)}, u32[]{:S(2)}, u32[]{:S(2)}) collective-permute-start(bf16[3,48,768]{2,1,0:T(8,128)(2,1)} %get-tuple-element.763), channel_id=1, source_target_pairs={{0,3},{1,0},{2,1},{3,2},{4,7},{5,4},{6,5},{7,6},{8,11},{9,8},{10,9... | collective-permute-start | bytes 663560 | tf_op jit(solution)/shard_map/ppermute | solution.py:143
  340.1 309.2 %collective-permute-start.3 = (bf16[3,48,768]{2,1,0:T(8,128)(2,1)}, bf16[3,48,768]{2,1,0:T(8,128)(2,1)}, u32[]{:S(2)}, u32[]{:S(2)}) collective-permute-start(bf16[3,48,768]{2,1,0:T(8,128)(2,1)} %get-tuple-element.764), channel_id=1, source_target_pairs={{0,2},{1,3},{2,0},{3,1},{4,6},{5,7},{6,4},{7,5},{8,10},{9,11},{10,... | collective-permute-start | bytes 663560 | tf_op jit(solution)/shard_map/ppermute | solution.py:143
  340.6 307.7 %collective-permute-start.2 = (bf16[3,48,768]{2,1,0:T(8,128)(2,1)}, bf16[3,48,768]{2,1,0:T(8,128)(2,1)}, u32[]{:S(2)}, u32[]{:S(2)}) collective-permute-start(bf16[3,48,768]{2,1,0:T(8,128)(2,1)} %get-tuple-element.765), channel_id=1, source_target_pairs={{0,1},{1,2},{2,3},{3,0},{4,5},{5,6},{6,7},{7,4},{8,9},{9,10},{10,1... | collective-permute-start | bytes 663560 | tf_op jit(solution)/shard_map/ppermute | solution.py:143
  341.7 298.5 %collective-permute-start.7 = (bf16[3,48,384]{2,1,0:T(8,128)(2,1)}, bf16[3,48,384]{2,1,0:T(8,128)(2,1)}, u32[]{:S(2)}, u32[]{:S(2)}) collective-permute-start(bf16[3,48,384]{2,1,0:T(8,128)(2,1)} %get-tuple-element.767), channel_id=1, source_target_pairs={{0,3},{1,0},{2,1},{3,2},{4,7},{5,4},{6,5},{7,6},{8,11},{9,8},{10,9... | collective-permute-start | bytes 331784 | tf_op jit(solution)/shard_map/ppermute | solution.py:143
  348.5 36.1 %all-gather.16.cloned.1.call-start = ((), (), s32[]{:S(2)}) async-start(), calls=%async_computation.2 | async-start | bytes 1474560 | tf_op jit(solution)/shard_map/while/body/eval_jaxpr/all_gather | solution.py:209
  373.1 10.5 %copy-start.13 = (f32[3072]{0:T(1024)S(1)}, f32[3072]{0:T(1024)}, u32[]{:S(2)}) copy-start(f32[3072]{0:T(1024)} %get-tuple-element.1053) | copy-start | bytes 36868 | tf_op jit(solution)/shard_map/while
  382.3 11.9 %collective-permute-start.1 = (bf16[1,48,3072]{2,1,0:T(8,128)(2,1)}, bf16[1,48,3072]{2,1,0:T(8,128)(2,1)}, u32[]{:S(2)}, u32[]{:S(2)}) collective-permute-start(bf16[1,48,3072]{2,1,0:T(8,128)(2,1)} %fusion.107), channel_id=1, source_target_pairs={{4,0},{8,4},{12,8},{5,1},{9,5},{13,9},{6,2},{10,6},{14,10},{7,3},{... | collective-permute-start | bytes 884744 | tf_op jit(solution)/shard_map/while/body/eval_jaxpr/ppermute | solution.py:17
  383.7 10.6 %copy-start.14 = (f32[3072]{0:T(1024)}, f32[3072]{0:T(1024)S(1)}, u32[]{:S(2)}) copy-start(f32[3072]{0:T(1024)S(1)} %select_add_fusion.2) | copy-start | bytes 36868 | tf_op jit(solution)/shard_map/while
  394.2 35.7 %all-gather.16.cloned.1.call-start = ((), (), s32[]{:S(2)}) async-start(), calls=%async_computation.2 | async-start | bytes 1474560 | tf_op jit(solution)/shard_map/while/body/eval_jaxpr/all_gather | solution.py:209
  418.4 10.5 %copy-start.13 = (f32[3072]{0:T(1024)S(1)}, f32[3072]{0:T(1024)}, u32[]{:S(2)}) copy-start(f32[3072]{0:T(1024)} %get-tuple-element.1053) | copy-start | bytes 36868 | tf_op jit(solution)/shard_map/while
  427.6 11.5 %collective-permute-start.1 = (bf16[1,48,3072]{2,1,0:T(8,128)(2,1)}, bf16[1,48,3072]{2,1,0:T(8,128)(2,1)}, u32[]{:S(2)}, u32[]{:S(2)}) collective-permute-start(bf16[1,48,3072]{2,1,0:T(8,128)(2,1)} %fusion.107), channel_id=1, source_target_pairs={{4,0},{8,4},{12,8},{5,1},{9,5},{13,9},{6,2},{10,6},{14,10},{7,3},{... | collective-permute-start | bytes 884744 | tf_op jit(solution)/shard_map/while/body/eval_jaxpr/ppermute | solution.py:17
  439.1 35.6 %all-gather.16.cloned.1.call-start = ((), (), s32[]{:S(2)}) async-start(), calls=%async_computation.2 | async-start | bytes 1474560 | tf_op jit(solution)/shard_map/while/body/eval_jaxpr/all_gather | solution.py:209
  463.3 10.5 %copy-start.13 = (f32[3072]{0:T(1024)S(1)}, f32[3072]{0:T(1024)}, u32[]{:S(2)}) copy-start(f32[3072]{0:T(1024)} %get-tuple-element.1053) | copy-start | bytes 36868 | tf_op jit(solution)/shard_map/while
  472.5 11.5 %collective-permute-start.1 = (bf16[1,48,3072]{2,1,0:T(8,128)(2,1)}, bf16[1,48,3072]{2,1,0:T(8,128)(2,1)}, u32[]{:S(2)}, u32[]{:S(2)}) collective-permute-start(bf16[1,48,3072]{2,1,0:T(8,128)(2,1)} %fusion.107), channel_id=1, source_target_pairs={{4,0},{8,4},{12,8},{5,1},{9,5},{13,9},{6,2},{10,6},{14,10},{7,3},{... | collective-permute-start | bytes 884744 | tf_op jit(solution)/shard_map/while/body/eval_jaxpr/ppermute | solution.py:17
  483.9 35.7 %all-gather.16.cloned.1.call-start = ((), (), s32[]{:S(2)}) async-start(), calls=%async_computation.2 | async-start | bytes 1474560 | tf_op jit(solution)/shard_map/while/body/eval_jaxpr/all_gather | solution.py:209
  508.2 10.5 %copy-start.13 = (f32[3072]{0:T(1024)S(1)}, f32[3072]{0:T(1024)}, u32[]{:S(2)}) copy-start(f32[3072]{0:T(1024)} %get-tuple-element.1053) | copy-start | bytes 36868 | tf_op jit(solution)/shard_map/while
  517.3 11.5 %collective-permute-start.1 = (bf16[1,48,3072]{2,1,0:T(8,128)(2,1)}, bf16[1,48,3072]{2,1,0:T(8,128)(2,1)}, u32[]{:S(2)}, u32[]{:S(2)}) collective-permute-start(bf16[1,48,3072]{2,1,0:T(8,128)(2,1)} %fusion.107), channel_id=1, source_target_pairs={{4,0},{8,4},{12,8},{5,1},{9,5},{13,9},{6,2},{10,6},{14,10},{7,3},{... | collective-permute-start | bytes 884744 | tf_op jit(solution)/shard_map/while/body/eval_jaxpr/ppermute | solution.py:17
  528.8 35.6 %all-gather.16.cloned.1.call-start = ((), (), s32[]{:S(2)}) async-start(), calls=%async_computation.2 | async-start | bytes 1474560 | tf_op jit(solution)/shard_map/while/body/eval_jaxpr/all_gather | solution.py:209
  562.2 11.5 %collective-permute-start.1 = (bf16[1,48,3072]{2,1,0:T(8,128)(2,1)}, bf16[1,48,3072]{2,1,0:T(8,128)(2,1)}, u32[]{:S(2)}, u32[]{:S(2)}) collective-permute-start(bf16[1,48,3072]{2,1,0:T(8,128)(2,1)} %fusion.107), channel_id=1, source_target_pairs={{4,0},{8,4},{12,8},{5,1},{9,5},{13,9},{6,2},{10,6},{14,10},{7,3},{... | collective-permute-start | bytes 884744 | tf_op jit(solution)/shard_map/while/body/eval_jaxpr/ppermute | solution.py:17
  573.6 35.7 %all-gather.16.cloned.1.call-start = ((), (), s32[]{:S(2)}) async-start(), calls=%async_computation.2 | async-start | bytes 1474560 | tf_op jit(solution)/shard_map/while/body/eval_jaxpr/all_gather | solution.py:209
  597.8 10.5 %copy-start.13 = (f32[3072]{0:T(1024)S(1)}, f32[3072]{0:T(1024)}, u32[]{:S(2)}) copy-start(f32[3072]{0:T(1024)} %get-tuple-element.1053) | copy-start | bytes 36868 | tf_op jit(solution)/shard_map/while
  607.0 11.5 %collective-permute-start.1 = (bf16[1,48,3072]{2,1,0:T(8,128)(2,1)}, bf16[1,48,3072]{2,1,0:T(8,128)(2,1)}, u32[]{:S(2)}, u32[]{:S(2)}) collective-permute-start(bf16[1,48,3072]{2,1,0:T(8,128)(2,1)} %fusion.107), channel_id=1, source_target_pairs={{4,0},{8,4},{12,8},{5,1},{9,5},{13,9},{6,2},{10,6},{14,10},{7,3},{... | collective-permute-start | bytes 884744 | tf_op jit(solution)/shard_map/while/body/eval_jaxpr/ppermute | solution.py:17
  618.5 15.6 %collective-permute-start.5 = (bf16[3,48,384]{2,1,0:T(8,128)(2,1)}, bf16[3,48,384]{2,1,0:T(8,128)(2,1)S(1)}, u32[]{:S(2)}, u32[]{:S(2)}) collective-permute-start(bf16[3,48,384]{2,1,0:T(8,128)(2,1)} %get-tuple-element.769), channel_id=1, source_target_pairs={{0,1},{1,2},{2,3},{3,0},{4,5},{5,6},{6,7},{7,4},{8,9},{9,10},{10,1... | collective-permute-start | bytes 331784 | tf_op jit(solution)/shard_map/ppermute | solution.py:143
  634.1 5.5 collective-permute-start.6
  (67 other events, 363.4 us)
Sparse Core Ops, SparseCore 0:
  9.6 66.9 all-gather.13
  78.1 68.6 all-gather.11
  350.9 19.0 all-gather.15
  396.3 16.7 all-gather.15
  441.2 17.1 all-gather.15
  486.0 17.0 all-gather.15
  531.2 17.2 all-gather.15
  576.0 17.0 all-gather.15

commit v2 on v0

--- a/solution.py
+++ b/solution.py
@@ -1,6 +1,10 @@
+import functools
+
 import jax
 import jax.numpy as jnp
 from jax import lax
+from jax.experimental import pallas as pl
+from jax.experimental.pallas import tpu as pltpu
 from jax.sharding import PartitionSpec as P
 
 NUM_HEADS = 24
@@ -123,13 +127,169 @@
     return from_behind(values, "section", -1)
 
 
+CORES = 2
+CHUNKS = 4
+
+
+def gather_kernel(chips, groups, joined_ref, out_ref, full_joined, full_out, local_sems, *sems):
+    send_x, recv_x, send_y, recv_y, send_own, recv_own, send_c, recv_c = sems
+    me = lax.axis_index("dp")
+    chip, core = me // CORES, lax.rem(me, CORES)
+    group = lax.axis_index("groups")
+    sibling = me + 1 - 2 * core
+    pairs = ((joined_ref, full_joined), (out_ref, full_out))
+
+    barrier = pltpu.get_barrier_semaphore()
+    partners = [{"dp": sibling}]
+    partners += [{"dp": lax.rem(chip + k, chips) * CORES + core} for k in range(1, chips)]
+    partners += [{"groups": lax.rem(group + g, groups)} for g in range(1, groups)]
+    for partner in partners:
+        pl.semaphore_signal(
+            barrier, inc=1, device_id=partner, device_id_type=pl.DeviceIdType.MESH
+        )
+    pl.semaphore_wait(barrier, len(partners))
+
+    def remote(src, dst, send_sem, recv_sem, partner):
+        return pltpu.make_async_remote_copy(
+            src_ref=src,
+            dst_ref=dst,
+            send_sem=send_sem,
+            recv_sem=recv_sem,
+            device_id=partner,
+            device_id_type=pl.DeviceIdType.MESH,
+        )
+
+    def span(w, owner, part, chunk):
+        rows = pairs[w][0].shape[0]
+        size = rows // (groups * CHUNKS)
+        inside = (part * CHUNKS + chunk) * size
+        return pl.ds(inside, size), pl.ds(owner * rows + inside, size)
+
+    first = {}
+    for w, (mine, full) in enumerate(pairs):
+        for chunk in range(CHUNKS):
+            for k in range(1, chips):
+                here, there = span(w, me, group, chunk)
+                copy = remote(
+                    mine.at[here],
+                    full.at[there],
+                    send_x.at[w, chunk, k - 1],
+                    recv_x.at[w, chunk, k - 1],
+                    partners[k],
+                )
+                copy.start()
+                first[w, chunk, k] = copy
+    own, local = [], []
+    for w, (mine, full) in enumerate(pairs):
+        rows = mine.shape[0]
+        place = full.at[pl.ds(me * rows, rows)]
+        own.append(remote(mine, place, send_own.at[w], recv_own.at[w], partners[0]))
+        own[-1].start()
+        local.append(pltpu.make_async_copy(mine, place, local_sems.at[w]))
+        local[-1].start()
+
+    second, third = {}, []
+    order = [
+        (w, chunk, k) for w in range(2) for chunk in range(CHUNKS) for k in range(1, chips)
+    ]
+
+    def hand_over(w, chunk, k):
+        owner = lax.rem(chip + chips - k, chips) * CORES + core
+        for g in range(1, groups):
+            second[w, chunk, k, g].wait_recv()
+            part = lax.rem(group + groups - g, groups)
+            _, place = span(w, owner, part, chunk)
+            copy = remote(
+                pairs[w][1].at[place],
+                pairs[w][1].at[place],
+                send_c.at[w, chunk, k - 1, g],
+                recv_c.at[w, chunk, k - 1, g],
+                partners[0],
+            )
+            copy.start()
+            third.append(copy)
+
+    for at, (w, chunk, k) in enumerate(order):
+        first[w, chunk, k].wait_recv()
+        owner = lax.rem(chip + chips - k, chips) * CORES + core
+        _, place = span(w, owner, group, chunk)
+        block = pairs[w][1].at[place]
+        for g in range(1, groups):
+            copy = remote(
+                block,
+                block,
+                send_y.at[w, chunk, k - 1, g - 1],
+                recv_y.at[w, chunk, k - 1, g - 1],
+                partners[chips - 1 + g],
+            )
+            copy.start()
+            second[w, chunk, k, g] = copy
+        copy = remote(
+            block,
+            block,
+            send_c.at[w, chunk, k - 1, 0],
+            recv_c.at[w, chunk, k - 1, 0],
+            partners[0],
+        )
+        copy.start()
+        third.append(copy)
+        if at:
+            hand_over(*order[at - 1])
+    hand_over(*order[-1])
+
+    for copy in local:
+        copy.wait()
+    for copy in own:
+        copy.wait()
+    for copy in first.values():
+        copy.wait_send()
+    for copy in second.values():
+        copy.wait_send()
+    for copy in third:
+        copy.wait()
+
+
+def gather_weights(w_joined, w_out):
+    replicas = lax.axis_size("dp")
+    chips, groups = replicas // CORES, lax.axis_size("groups")
+    shards = (w_joined[0], w_out[0])
+    x_shape = (2, CHUNKS, chips - 1)
+    dma = pltpu.SemaphoreType.DMA
+    anywhere = pl.BlockSpec(memory_space=pl.ANY)
+    return pl.pallas_call(
+        functools.partial(gather_kernel, chips, groups),
+        out_shape=[
+            jax.ShapeDtypeStruct((replicas * each.shape[0], each.shape[1]), each.dtype)
+            for each in shards
+        ],
+        in_specs=[anywhere] * 2,
+        out_specs=[anywhere] * 2,
+        scratch_shapes=[dma((2,)), dma(x_shape), dma(x_shape)]
+        + [dma(x_shape + (groups - 1,))] * 2
+        + [dma((2,))] * 2
+        + [dma(x_shape + (groups,))] * 2,
+        compiler_params=pltpu.CompilerParams(collective_id=0, has_side_effects=True),
+    )(*shards)
+
+
+def share_columns(rows):
+    n = lax.axis_size("dp")
+    me = lax.axis_index("dp")
+    count, total = rows.shape
+    width = total // n
+    taken = jnp.zeros((n, count, width), rows.dtype)
+    for shift in range(n):
+        target = lax.rem(me + shift, n)
+        piece = lax.dynamic_slice_in_dim(rows, target * width, width, 1)
+        if shift:
+            piece = lax.ppermute(piece, "dp", [(i, (i + shift) % n) for i in range(n)])
+        source = lax.rem(me + n - shift, n)
+        taken = lax.dynamic_update_slice_in_dim(taken, piece[None], source, 0)
+    return taken.reshape(n * count, width)
+
+
 def body(stream_in, out_grad, mask_blocks, norm_gain, w_joined, w_out):
-    gathered = (
-        lax.all_gather(w_joined, "dp", axis=1, tiled=True),
-        lax.all_gather(w_out, "dp", axis=1, tiled=True),
-    )
-    full_joined = gathered[0][0]
-    full_out = gathered[1][0]
+    full_joined, full_out = gather_weights(w_joined, w_out)
     gain_row = norm_gain[0]
     sections = lax.axis_size("section")
     section_index = lax.axis_index("section")
@@ -143,7 +303,7 @@
     upstreams = out_grad.reshape(micro_count, per_group, length, model_width)
     allowed = allowed_tokens(mask_blocks, BLOCK_LEN).reshape(micro_count, per_group, length, length)
     step_count = micro_count + sections - 1
-    keep_shape = (1,)
+    keep_shape = (micro_count, per_group, length, joined_width)
 
     def forward_step(step_now, state_now):
         incoming, kept_inputs, kept_joined = state_now
@@ -157,7 +317,7 @@
                 source, gain_row, full_joined, full_out, allowed[group_index]
             )
             new_inputs = lax.dynamic_update_index_in_dim(kept_pair[0], source, group_index, 0)
-            new_joined = kept_pair[1]
+            new_joined = lax.dynamic_update_index_in_dim(kept_pair[1], joined_rows, group_index, 0)
             return (result, new_inputs, new_joined)
 
         def forward_rest(kept_pair):
@@ -184,7 +344,7 @@
 
         def backward_run(store_now):
             source = kept_inputs[group_index]
-            joined_rows = project(normalize(source, gain_row)[2], full_joined)
+            joined_rows = kept_joined[group_index]
             down_grad, normed, grad_joined_rows, mixed_heads, gain_part = layer_backward(
                 source, gain_row, joined_rows, full_joined, full_out, allowed[group_index], upstream
             )
@@ -216,25 +376,16 @@
     rows_joined = stores[1].reshape(-1, joined_width)
     rows_mixed = stores[2].reshape(-1, inner_width)
     rows_upstream = stores[3].reshape(-1, model_width)
-    columns = rows_normed
-    grad_joined = lax.psum_scatter(
-        lax.dot_general(
-            columns, rows_joined, (((0,), (0,)), ((), ())), preferred_element_type=jnp.float32
-        ).astype(jnp.bfloat16),
-        "dp",
-        scatter_dimension=0,
-        tiled=True,
-    ).astype(jnp.float32)
-    columns = rows_mixed
-    grad_output = lax.psum_scatter(
-        lax.dot_general(
-            columns, rows_upstream, (((0,), (0,)), ((), ())), preferred_element_type=jnp.float32
-        ).astype(jnp.bfloat16),
-        "dp",
-        scatter_dimension=0,
-        tiled=True,
-    ).astype(jnp.float32)
-    gain_total = lax.psum(stores[4], "dp")
+    over_rows = (((0,), (0,)), ((), ()))
+    gain_total = jnp.sum(lax.all_gather(stores[4], "dp", axis=0), axis=0)
+    all_upstream = lax.all_gather(rows_upstream, "dp", axis=0, tiled=True)
+    all_joined = lax.all_gather(rows_joined, "dp", axis=0, tiled=True)
+    grad_output = lax.dot_general(
+        share_columns(rows_mixed), all_upstream, over_rows, preferred_element_type=jnp.float32
+    )
+    grad_joined = lax.dot_general(
+        share_columns(rows_normed), all_joined, over_rows, preferred_element_type=jnp.float32
+    )
     return (grad_joined[None], grad_output[None], gain_total[None])
 
 

time: 679 us -> 573 us (0.84)
  waiting for transfers between devices: 442 us -> 178 us
  Pallas kernels: 0 us -> 154 us
  matrix products: 120 us -> 98.4 us
  local copies, waits for them, and re-layouts: 11.3 us -> 27 us
  blocking collectives: 10.7 us -> 20.7 us
    pallas_call x0 -> x1, Pallas kernels: none -> 154 us  [gather_weights(): pl.pallas_call(functools.partial(gather_kernel, chips, groups), out_shape...]
    reduce_scatter x2 -> x0, waiting for transfers between devices: 136 us -> none  [the longest x1 81.7 us: body(): lax.psum_scatter(lax.dot_general(columns, rows_joined, (((0,), (0,)), (()...]
    all_gather x2, waiting for transfers between devices: 137 us -> 17.8 us  [the longest x1 17.8 us: body(): all_upstream = lax.all_gather(rows_upstream, 'dp', axis=0, tiled=True)]
    all_gather x0 -> x1, blocking collectives: none -> 20.7 us  [body(): gain_total = jnp.sum(lax.all_gather(stores[4], 'dp', axis=0), axis=0)]
    dot_general x6 -> x3, matrix products: 35.1 us -> 19.6 us  [project(): jnp.dot(normed.reshape(-1, model_width), weight, preferred_element_type=j...]
    ppermute x12, waiting for transfers between devices: 168 us -> 156 us  [from_behind(): lax.ppermute(value, axis, [(source, source + steps) for source in range(i...]
    psum x1 -> x0, blocking collectives: 10.7 us -> none  [body(): gain_total = lax.psum(stores[4], 'dp')]
    broadcast_in_dim x2 -> x0, other arithmetic: 8.78 us -> none  [body(): return (grad_joined[None], grad_output[None], gain_total[None])]
  transfers between devices with their start and end apart: 16 -> 20, of which waited for: 16 -> 14; matrix products, arithmetic and copies ran while one was open for 2% -> 2% of each run, Pallas kernels for 0% -> 0%
where the time goes in v2:
time: 573 us; the launch traced here: 572 us
  waiting for transfers between devices  178 us (31%)
  Pallas kernels  154 us (27%)
  matrix products  98.4 us (17%)
  starting transfers between devices  64 us (11%)
  local copies, waits for them, and re-layouts  27 us (5%)
  blocking collectives  20.7 us (4%)
  other arithmetic  15.4 us (3%)
  between operations  14.2 us (2%)
    ppermute x12, waiting for transfers between devices, from_behind(): lax.ppermute(value, axis, [(source, source + steps) for source in range(i...  156 us
    pallas_call x1, Pallas kernels, gather_weights(): pl.pallas_call(functools.partial(gather_kernel, chips, groups), out_shape...  154 us
    ppermute x12, starting transfers between devices, from_behind(): lax.ppermute(value, axis, [(source, source + steps) for source in range(i...  58.6 us
    dot_general x3, matrix products, layer_backward(): lax.dot_general(grad_joined_rows.reshape(-1, grad_joined_rows.shape[2]),...  21.7 us
    all_gather x1, blocking collectives, body(): gain_total = jnp.sum(lax.all_gather(stores[4], 'dp', axis=0), axis=0)  20.7 us
    dot_general x3, matrix products, layer_backward(): lax.dot_general(upstream.reshape(-1, model_width), w_out, (((1,), (1,)),...  19.8 us
    dot_general x3, matrix products, project(): jnp.dot(normed.reshape(-1, model_width), weight, preferred_element_type=j...  19.6 us
    all_gather x1, waiting for transfers between devices, body(): all_upstream = lax.all_gather(rows_upstream, 'dp', axis=0, tiled=True)  17.8 us
  transfers between devices with their start and end apart: 20, of which 14 were waited for; matrix products, arithmetic and copies ran while one was open for 2% of the time, Pallas kernels for 0%

profile of v2, /device:TPU:0, one launch (start us, length us, event | category | flops | bytes accessed | tf_op | source)
XLA Modules:
  0.0 572.2 jit_solution(6853732698818590128)
XLA Ops:
  8.3 153.7 %shard_map.85 = (bf16[3072,1664]{1,0:T(8,128)(2,1)}, bf16[1536,3072]{1,0:T(8,128)(2,1)}) custom-call(bf16[768,1664]{1,0:T(8,128)(2,1)} %bitcast.204, bf16[384,3072]{1,0:T(8,128)(2,1)} %bitcast.208), custom_call_target="tpu_custom_call" | custom-call | tf_op jit(solution)/shard_map/pallas_call | solution.py:259
  162.9 123.9 %while.45 = (s32[]{:T(128)}, bf16[1,48,3072]{2,1,0:T(8,128)(2,1)S(1)}, bf16[3,1,48,3072]{3,2,1,0:T(8,128)(2,1)S(1)}, bf16[3,1,48,1664]{3,2,1,0:T(8,128)(2,1)}, s...) while((s32[]{:T(128)}, ...), condition=%wide.region_7.8_spmd.clone, body=%wide.region_1.7_spmd.clone.sunk | while | flops 960089920 | bytes 26415392 | solution.py:336
  163.0 14.7 %conditional.6 = (bf16[1,48,3072]{2,1,0:T(8,128)(2,1)S(1)}, bf16[3,1,48,3072]{3,2,1,0:T(8,128)(2,1)S(1)}, bf16[3,1,48,1664]{3,2,1,0:T(8,128)(2,1)}) conditional(s32[]{:T(128)} %convert_element_type.242, (bf16[3,1,48,3072]{3,2,1,0:T(8,128)(2,1)S(1)}, bf16[3,1,48,1664]{3,2,1,0:T(8,128)(2,1)}) %tuple.126, (pred[]{:T(512)}, s32[]{:T(128)}, ...), branch_computations={%region_2.2_spmd, %region_3.6_spmd} | conditional | flops 960089920 | bytes 25228092 | solution.py:326
  164.2 6.5 %bitcast_dynamic-update-slice_fusion.1 = (bf16[3,1,48,1664]{3,2,1,0:T(8,128)(2,1)}, bf16[48,1664]{1,0:T(8,128)(2,1)S(1)}) fusion(bf16[3,1,48,1664]{3,2,1,0:T(8,128)(2,1)} %get-tuple-element.807, s32[]{:T(128)S(6)} %min.20, bf16[3072,1664]{1,0:T(8,128)(2,1)} %get-tuple-element.803, bf16[1,48,3072]{2,1,0:T(8,128)(2,1)S(1)} %get-tuple-element.1013, ...), kind=kOutput, calls=%fused_computation.26 | convolution fusion | flops 491403264 | bytes 10850500 | tf_op jit(solution)/shard_map/while/body/eval_jaxpr/cond/branch_1_fun/dot_general | solution.py:40
  179.0 6.2 %collective-permute-done = bf16[1,48,3072]{2,1,0:T(8,128)(2,1)S(1)} collective-permute-done((bf16[1,48,3072]{2,1,0:T(8,128)(2,1)S(1)}, bf16[1,48,3072]{2,1,0:T(8,128)(2,1)S(1)}, u32[]{:S(2)}, u32[]{:S(2)}) %collective-permute-start) | collective-permute-done | bytes 294944 | tf_op jit(solution)/shard_map/while/body/eval_jaxpr/ppermute | solution.py:21
  185.2 14.7 %conditional.6 = (bf16[1,48,3072]{2,1,0:T(8,128)(2,1)S(1)}, bf16[3,1,48,3072]{3,2,1,0:T(8,128)(2,1)S(1)}, bf16[3,1,48,1664]{3,2,1,0:T(8,128)(2,1)}) conditional(s32[]{:T(128)} %convert_element_type.242, (bf16[3,1,48,3072]{3,2,1,0:T(8,128)(2,1)S(1)}, bf16[3,1,48,1664]{3,2,1,0:T(8,128)(2,1)}) %tuple.126, (pred[]{:T(512)}, s32[]{:T(128)}, ...), branch_computations={%region_2.2_spmd, %region_3.6_spmd} | conditional | flops 960089920 | bytes 25228092 | solution.py:326
  186.5 6.5 %bitcast_dynamic-update-slice_fusion.1 = (bf16[3,1,48,1664]{3,2,1,0:T(8,128)(2,1)}, bf16[48,1664]{1,0:T(8,128)(2,1)S(1)}) fusion(bf16[3,1,48,1664]{3,2,1,0:T(8,128)(2,1)} %get-tuple-element.807, s32[]{:T(128)S(6)} %min.20, bf16[3072,1664]{1,0:T(8,128)(2,1)} %get-tuple-element.803, bf16[1,48,3072]{2,1,0:T(8,128)(2,1)S(1)} %get-tuple-element.1013, ...), kind=kOutput, calls=%fused_computation.26 | convolution fusion | flops 491403264 | bytes 10850500 | tf_op jit(solution)/shard_map/while/body/eval_jaxpr/cond/branch_1_fun/dot_general | solution.py:40
  194.4 5.4 fusion.5
  209.7 14.7 %conditional.6 = (bf16[1,48,3072]{2,1,0:T(8,128)(2,1)S(1)}, bf16[3,1,48,3072]{3,2,1,0:T(8,128)(2,1)S(1)}, bf16[3,1,48,1664]{3,2,1,0:T(8,128)(2,1)}) conditional(s32[]{:T(128)} %convert_element_type.242, (bf16[3,1,48,3072]{3,2,1,0:T(8,128)(2,1)S(1)}, bf16[3,1,48,1664]{3,2,1,0:T(8,128)(2,1)}) %tuple.126, (pred[]{:T(512)}, s32[]{:T(128)}, ...), branch_computations={%region_2.2_spmd, %region_3.6_spmd} | conditional | flops 960089920 | bytes 25228092 | solution.py:326
  210.9 6.5 %bitcast_dynamic-update-slice_fusion.1 = (bf16[3,1,48,1664]{3,2,1,0:T(8,128)(2,1)}, bf16[48,1664]{1,0:T(8,128)(2,1)S(1)}) fusion(bf16[3,1,48,1664]{3,2,1,0:T(8,128)(2,1)} %get-tuple-element.807, s32[]{:T(128)S(6)} %min.20, bf16[3072,1664]{1,0:T(8,128)(2,1)} %get-tuple-element.803, bf16[1,48,3072]{2,1,0:T(8,128)(2,1)S(1)} %get-tuple-element.1013, ...), kind=kOutput, calls=%fused_computation.26 | convolution fusion | flops 491403264 | bytes 10850500 | tf_op jit(solution)/shard_map/while/body/eval_jaxpr/cond/branch_1_fun/dot_general | solution.py:40
  233.3 19.0 %collective-permute-start = (bf16[1,48,3072]{2,1,0:T(8,128)(2,1)S(1)}, bf16[1,48,3072]{2,1,0:T(8,128)(2,1)S(1)}, u32[]{:S(2)}, u32[]{:S(2)}) collective-permute-start(bf16[1,48,3072]{2,1,0:T(8,128)(2,1)S(1)} %get-tuple-element.1191), channel_id=1, source_target_pairs={{0,4},{4,8},{8,12},{1,5},{5,9},{9,13},{2,6},{6,10},{10,14},{3,7},{... | collective-permute-start | bytes 884744 | tf_op jit(solution)/shard_map/while/body/eval_jaxpr/ppermute | solution.py:21
  265.3 17.4 %collective-permute-start = (bf16[1,48,3072]{2,1,0:T(8,128)(2,1)S(1)}, bf16[1,48,3072]{2,1,0:T(8,128)(2,1)S(1)}, u32[]{:S(2)}, u32[]{:S(2)}) collective-permute-start(bf16[1,48,3072]{2,1,0:T(8,128)(2,1)S(1)} %get-tuple-element.1191), channel_id=1, source_target_pairs={{0,4},{4,8},{8,12},{1,5},{5,9},{9,13},{2,6},{6,10},{10,14},{3,7},{... | collective-permute-start | bytes 884744 | tf_op jit(solution)/shard_map/while/body/eval_jaxpr/ppermute | solution.py:21
  289.6 209.9 %while.46 = (s32[]{:T(128)}, bf16[1,48,3072]{2,1,0:T(8,128)(2,1)S(1)}, bf16[3,1,48,3072]{3,2,1,0:T(8,128)(2,1)}, bf16[3,1,48,1664]{3,2,1,0:T(8,128)(2,1)}, bf16[...) while((s32[]{:T(128)}, ...), condition=%wide.region_17.18_spmd.clone, body=%wide.region_8.17_spmd.clone.sunk | while | flops 991109952 | bytes 41387848 | solution.py:374
  291.7 8.0 %collective-permute-done.1 = bf16[1,48,3072]{2,1,0:T(8,128)(2,1)S(1)} collective-permute-done((bf16[1,48,3072]{2,1,0:T(8,128)(2,1)}, bf16[1,48,3072]{2,1,0:T(8,128)(2,1)S(1)}, u32[]{:S(2)}, u32[]{:S(2)}) %collective-permute-start.1) | collective-permute-done | bytes 294944 | tf_op jit(solution)/shard_map/while/body/eval_jaxpr/ppermute | solution.py:21
  301.7 20.1 %collective-permute-done.1 = bf16[1,48,3072]{2,1,0:T(8,128)(2,1)S(1)} collective-permute-done((bf16[1,48,3072]{2,1,0:T(8,128)(2,1)}, bf16[1,48,3072]{2,1,0:T(8,128)(2,1)S(1)}, u32[]{:S(2)}, u32[]{:S(2)}) %collective-permute-start.1) | collective-permute-done | bytes 294944 | tf_op jit(solution)/shard_map/while/body/eval_jaxpr/ppermute | solution.py:21
  323.9 77.1 %collective-permute-done.1 = bf16[1,48,3072]{2,1,0:T(8,128)(2,1)S(1)} collective-permute-done((bf16[1,48,3072]{2,1,0:T(8,128)(2,1)}, bf16[1,48,3072]{2,1,0:T(8,128)(2,1)S(1)}, u32[]{:S(2)}, u32[]{:S(2)}) %collective-permute-start.1) | collective-permute-done | bytes 294944 | tf_op jit(solution)/shard_map/while/body/eval_jaxpr/ppermute | solution.py:21
  401.0 24.0 %conditional.7 = (bf16[1,48,3072]{2,1,0:T(8,128)(2,1)}, bf16[3,1,48,3072]{3,2,1,0:T(8,128)(2,1)}, bf16[3,1,48,1664]{3,2,1,0:T(8,128)(2,1)}, bf16[3,1,48,1536]{3,...) conditional(s32[]{:T(128)} %convert_element_type.243, ...), branch_computations={%region_9.9_spmd, %region_10.16_spmd} | conditional | flops 991109952 | bytes 40200444 | solution.py:363
  405.8 6.6 %convolution_convert_fusion.2 = bf16[48,1536]{1,0:T(8,128)(2,1)S(1)} fusion(bf16[1536,3072]{1,0:T(8,128)(2,1)} %get-tuple-element.835, bf16[1,48,3072]{2,1,0:T(8,128)(2,1)S(1)} %get-tuple-element.1015), kind=kOutput, calls=%fused_computation.31 | convolution fusion | flops 453058560 | bytes 9879552 | tf_op jit(solution)/shard_map/while/body/eval_jaxpr/cond/branch_1_fun/dot_general | solution.py:82
  416.8 7.2 %fusion.35 = (f32[3072]{0:T(1024)S(1)}, f32[48]{0:T(128)S(1)}, f32[48,3072]{1,0:T(8,128)S(1)}) fusion(f32[48]{0:T(128)S(1)} %get-tuple-element.1021, bf16[3,1,48,3072]{3,2,1,0:T(8,128)(2,1)S(1)} %get-tuple-element.832, s32[]{:T(128)S(6)} %min.21, f32[3072]{0:T(1024)S(1)} %bitcast.201, bf16[48,1664]{1,0:T(8,128)(2,1)S(1)} %concatenate.26, ...), kind=kOutput, calls=%fused_computation.57 | convolution fusion | flops 491762624 | bytes 11293060 | tf_op jit(solution)/shard_map/while/body/eval_jaxpr/cond/branch_1_fun/dot_general | solution.py:106
  426.3 7.5 %collective-permute-done.1 = bf16[1,48,3072]{2,1,0:T(8,128)(2,1)S(1)} collective-permute-done((bf16[1,48,3072]{2,1,0:T(8,128)(2,1)}, bf16[1,48,3072]{2,1,0:T(8,128)(2,1)S(1)}, u32[]{:S(2)}, u32[]{:S(2)}) %collective-permute-start.1) | collective-permute-done | bytes 294944 | tf_op jit(solution)/shard_map/while/body/eval_jaxpr/ppermute | solution.py:21
  433.9 24.0 %conditional.7 = (bf16[1,48,3072]{2,1,0:T(8,128)(2,1)}, bf16[3,1,48,3072]{3,2,1,0:T(8,128)(2,1)}, bf16[3,1,48,1664]{3,2,1,0:T(8,128)(2,1)}, bf16[3,1,48,1536]{3,...) conditional(s32[]{:T(128)} %convert_element_type.243, ...), branch_computations={%region_9.9_spmd, %region_10.16_spmd} | conditional | flops 991109952 | bytes 40200444 | solution.py:363
  438.6 6.6 %convolution_convert_fusion.2 = bf16[48,1536]{1,0:T(8,128)(2,1)S(1)} fusion(bf16[1536,3072]{1,0:T(8,128)(2,1)} %get-tuple-element.835, bf16[1,48,3072]{2,1,0:T(8,128)(2,1)S(1)} %get-tuple-element.1015), kind=kOutput, calls=%fused_computation.31 | convolution fusion | flops 453058560 | bytes 9879552 | tf_op jit(solution)/shard_map/while/body/eval_jaxpr/cond/branch_1_fun/dot_general | solution.py:82
  449.7 7.2 %fusion.35 = (f32[3072]{0:T(1024)S(1)}, f32[48]{0:T(128)S(1)}, f32[48,3072]{1,0:T(8,128)S(1)}) fusion(f32[48]{0:T(128)S(1)} %get-tuple-element.1021, bf16[3,1,48,3072]{3,2,1,0:T(8,128)(2,1)S(1)} %get-tuple-element.832, s32[]{:T(128)S(6)} %min.21, f32[3072]{0:T(1024)S(1)} %bitcast.201, bf16[48,1664]{1,0:T(8,128)(2,1)S(1)} %concatenate.26, ...), kind=kOutput, calls=%fused_computation.57 | convolution fusion | flops 491762624 | bytes 11293060 | tf_op jit(solution)/shard_map/while/body/eval_jaxpr/cond/branch_1_fun/dot_general | solution.py:106
  459.2 7.5 %collective-permute-done.1 = bf16[1,48,3072]{2,1,0:T(8,128)(2,1)S(1)} collective-permute-done((bf16[1,48,3072]{2,1,0:T(8,128)(2,1)}, bf16[1,48,3072]{2,1,0:T(8,128)(2,1)S(1)}, u32[]{:S(2)}, u32[]{:S(2)}) %collective-permute-start.1) | collective-permute-done | bytes 294944 | tf_op jit(solution)/shard_map/while/body/eval_jaxpr/ppermute | solution.py:21
  466.7 24.0 %conditional.7 = (bf16[1,48,3072]{2,1,0:T(8,128)(2,1)}, bf16[3,1,48,3072]{3,2,1,0:T(8,128)(2,1)}, bf16[3,1,48,1664]{3,2,1,0:T(8,128)(2,1)}, bf16[3,1,48,1536]{3,...) conditional(s32[]{:T(128)} %convert_element_type.243, ...), branch_computations={%region_9.9_spmd, %region_10.16_spmd} | conditional | flops 991109952 | bytes 40200444 | solution.py:363
  471.4 6.6 %convolution_convert_fusion.2 = bf16[48,1536]{1,0:T(8,128)(2,1)S(1)} fusion(bf16[1536,3072]{1,0:T(8,128)(2,1)} %get-tuple-element.835, bf16[1,48,3072]{2,1,0:T(8,128)(2,1)S(1)} %get-tuple-element.1015), kind=kOutput, calls=%fused_computation.31 | convolution fusion | flops 453058560 | bytes 9879552 | tf_op jit(solution)/shard_map/while/body/eval_jaxpr/cond/branch_1_fun/dot_general | solution.py:82
  482.5 7.2 %fusion.35 = (f32[3072]{0:T(1024)S(1)}, f32[48]{0:T(128)S(1)}, f32[48,3072]{1,0:T(8,128)S(1)}) fusion(f32[48]{0:T(128)S(1)} %get-tuple-element.1021, bf16[3,1,48,3072]{3,2,1,0:T(8,128)(2,1)S(1)} %get-tuple-element.832, s32[]{:T(128)S(6)} %min.21, f32[3072]{0:T(1024)S(1)} %bitcast.201, bf16[48,1664]{1,0:T(8,128)(2,1)S(1)} %concatenate.26, ...), kind=kOutput, calls=%fused_computation.57 | convolution fusion | flops 491762624 | bytes 11293060 | tf_op jit(solution)/shard_map/while/body/eval_jaxpr/cond/branch_1_fun/dot_general | solution.py:106
  492.0 7.5 %collective-permute-done.1 = bf16[1,48,3072]{2,1,0:T(8,128)(2,1)S(1)} collective-permute-done((bf16[1,48,3072]{2,1,0:T(8,128)(2,1)}, bf16[1,48,3072]{2,1,0:T(8,128)(2,1)S(1)}, u32[]{:S(2)}, u32[]{:S(2)}) %collective-permute-start.1) | collective-permute-done | bytes 294944 | tf_op jit(solution)/shard_map/while/body/eval_jaxpr/ppermute | solution.py:21
  506.6 20.7 %all-gather = f32[12288]{0:T(1024)S(1)} all-gather(f32[3072]{0:T(1024)S(1)} %get-tuple-element.886), channel_id=2, replica_groups=mesh['groups'=2,'section'=4,'dp'=4] {'dp'}, dimensions={0}, use_global_device_ids=true | all-gather | bytes 61440 | tf_op jit(solution)/shard_map/all_gather | solution.py:380
  535.1 6.3 %convolution_bitcast_fusion.5 = f32[1,768,1664]{2,1,0:T(8,128)} fusion(bf16[576,768]{1,0:T(8,128)(2,1)S(1)} %bitcast.211, bf16[576,1664]{1,0:T(8,128)(2,1)} %all-gather.4.cloned.1.call-done), kind=kOutput, calls=%fused_computation.89 | convolution fusion | flops 1472200704 | bytes 7913472 | tf_op jit(solution)/shard_map/dot_general | solution.py:386
  541.4 17.8 %all-gather.6.cloned.1.call-done = bf16[576,3072]{1,0:T(8,128)(2,1)} async-done(((bf16[144,3072]{1,0:T(8,128)(2,1)}), bf16[576,3072]{1,0:T(8,128)(2,1)}) %all-gather.6.cloned.1.call-update) | async-done | bytes 3538960 | tf_op jit(solution)/shard_map/all_gather | solution.py:381
  559.2 6.2 %convolution_bitcast_fusion.4 = f32[1,384,3072]{2,1,0:T(8,128)} fusion(bf16[576,384]{1,0:T(8,128)(2,1)S(1)} %bitcast.207, bf16[576,3072]{1,0:T(8,128)(2,1)} %all-gather.6.cloned.1.call-done), kind=kOutput, calls=%fused_computation.88 | convolution fusion | flops 1358954496 | bytes 8699904 | tf_op jit(solution)/shard_map/dot_general | solution.py:383
  (222 shorter events, 117.5 us)
Async XLA Ops:
  7.2 527.9 %all-gather.4.cloned.1.call-start = ((), (), s32[]{:S(2)}) async-start(), calls=%async_computation | async-start | bytes 2396160 | tf_op jit(solution)/shard_map/all_gather | solution.py:382
  177.7 7.5 %collective-permute-start = (bf16[1,48,3072]{2,1,0:T(8,128)(2,1)S(1)}, bf16[1,48,3072]{2,1,0:T(8,128)(2,1)S(1)}, u32[]{:S(2)}, u32[]{:S(2)}) collective-permute-start(bf16[1,48,3072]{2,1,0:T(8,128)(2,1)S(1)} %get-tuple-element.1191), channel_id=1, source_target_pairs={{0,4},{4,8},{8,12},{1,5},{5,9},{9,13},{2,6},{6,10},{10,14},{3,7},{... | collective-permute-start | bytes 884744 | tf_op jit(solution)/shard_map/while/body/eval_jaxpr/ppermute | solution.py:21
  199.9 9.8 %collective-permute-start = (bf16[1,48,3072]{2,1,0:T(8,128)(2,1)S(1)}, bf16[1,48,3072]{2,1,0:T(8,128)(2,1)S(1)}, u32[]{:S(2)}, u32[]{:S(2)}) collective-permute-start(bf16[1,48,3072]{2,1,0:T(8,128)(2,1)S(1)} %get-tuple-element.1191), channel_id=1, source_target_pairs={{0,4},{4,8},{8,12},{1,5},{5,9},{9,13},{2,6},{6,10},{10,14},{3,7},{... | collective-permute-start | bytes 884744 | tf_op jit(solution)/shard_map/while/body/eval_jaxpr/ppermute | solution.py:21
  224.4 8.8 %collective-permute-start = (bf16[1,48,3072]{2,1,0:T(8,128)(2,1)S(1)}, bf16[1,48,3072]{2,1,0:T(8,128)(2,1)S(1)}, u32[]{:S(2)}, u32[]{:S(2)}) collective-permute-start(bf16[1,48,3072]{2,1,0:T(8,128)(2,1)S(1)} %get-tuple-element.1191), channel_id=1, source_target_pairs={{0,4},{4,8},{8,12},{1,5},{5,9},{9,13},{2,6},{6,10},{10,14},{3,7},{... | collective-permute-start | bytes 884744 | tf_op jit(solution)/shard_map/while/body/eval_jaxpr/ppermute | solution.py:21
  233.3 23.2 %collective-permute-start = (bf16[1,48,3072]{2,1,0:T(8,128)(2,1)S(1)}, bf16[1,48,3072]{2,1,0:T(8,128)(2,1)S(1)}, u32[]{:S(2)}, u32[]{:S(2)}) collective-permute-start(bf16[1,48,3072]{2,1,0:T(8,128)(2,1)S(1)} %get-tuple-element.1191), channel_id=1, source_target_pairs={{0,4},{4,8},{8,12},{1,5},{5,9},{9,13},{2,6},{6,10},{10,14},{3,7},{... | collective-permute-start | bytes 884744 | tf_op jit(solution)/shard_map/while/body/eval_jaxpr/ppermute | solution.py:21
  256.6 8.6 %collective-permute-start = (bf16[1,48,3072]{2,1,0:T(8,128)(2,1)S(1)}, bf16[1,48,3072]{2,1,0:T(8,128)(2,1)S(1)}, u32[]{:S(2)}, u32[]{:S(2)}) collective-permute-start(bf16[1,48,3072]{2,1,0:T(8,128)(2,1)S(1)} %get-tuple-element.1191), channel_id=1, source_target_pairs={{0,4},{4,8},{8,12},{1,5},{5,9},{9,13},{2,6},{6,10},{10,14},{3,7},{... | collective-permute-start | bytes 884744 | tf_op jit(solution)/shard_map/while/body/eval_jaxpr/ppermute | solution.py:21
  265.3 21.6 %collective-permute-start = (bf16[1,48,3072]{2,1,0:T(8,128)(2,1)S(1)}, bf16[1,48,3072]{2,1,0:T(8,128)(2,1)S(1)}, u32[]{:S(2)}, u32[]{:S(2)}) collective-permute-start(bf16[1,48,3072]{2,1,0:T(8,128)(2,1)S(1)} %get-tuple-element.1191), channel_id=1, source_target_pairs={{0,4},{4,8},{8,12},{1,5},{5,9},{9,13},{2,6},{6,10},{10,14},{3,7},{... | collective-permute-start | bytes 884744 | tf_op jit(solution)/shard_map/while/body/eval_jaxpr/ppermute | solution.py:21
  290.4 9.3 %collective-permute-start.1 = (bf16[1,48,3072]{2,1,0:T(8,128)(2,1)}, bf16[1,48,3072]{2,1,0:T(8,128)(2,1)S(1)}, u32[]{:S(2)}, u32[]{:S(2)}) collective-permute-start(bf16[1,48,3072]{2,1,0:T(8,128)(2,1)} %get-tuple-element.1210), channel_id=1, source_target_pairs={{4,0},{8,4},{12,8},{5,1},{9,5},{13,9},{6,2},{10,6},{14,10},{7,3},{... | collective-permute-start | bytes 884744 | tf_op jit(solution)/shard_map/while/body/eval_jaxpr/ppermute | solution.py:21
  300.5 21.4 %collective-permute-start.1 = (bf16[1,48,3072]{2,1,0:T(8,128)(2,1)}, bf16[1,48,3072]{2,1,0:T(8,128)(2,1)S(1)}, u32[]{:S(2)}, u32[]{:S(2)}) collective-permute-start(bf16[1,48,3072]{2,1,0:T(8,128)(2,1)} %get-tuple-element.1210), channel_id=1, source_target_pairs={{4,0},{8,4},{12,8},{5,1},{9,5},{13,9},{6,2},{10,6},{14,10},{7,3},{... | collective-permute-start | bytes 884744 | tf_op jit(solution)/shard_map/while/body/eval_jaxpr/ppermute | solution.py:21
  322.6 78.4 %collective-permute-start.1 = (bf16[1,48,3072]{2,1,0:T(8,128)(2,1)}, bf16[1,48,3072]{2,1,0:T(8,128)(2,1)S(1)}, u32[]{:S(2)}, u32[]{:S(2)}) collective-permute-start(bf16[1,48,3072]{2,1,0:T(8,128)(2,1)} %get-tuple-element.1210), channel_id=1, source_target_pairs={{4,0},{8,4},{12,8},{5,1},{9,5},{13,9},{6,2},{10,6},{14,10},{7,3},{... | collective-permute-start | bytes 884744 | tf_op jit(solution)/shard_map/while/body/eval_jaxpr/ppermute | solution.py:21
  404.9 0.9 copy-start.1
  412.4 4.4 copy-start
  416.7 8.3 %copy-start.2 = (bf16[3,1,48,3072]{3,2,1,0:T(8,128)(2,1)S(1)}, bf16[3,1,48,3072]{3,2,1,0:T(8,128)(2,1)}, u32[]{:S(2)}) copy-start(bf16[3,1,48,3072]{3,2,1,0:T(8,128)(2,1)} %copy-done.1) | copy-start | bytes 2654212 | tf_op jit(solution)/shard_map/while/body/eval_jaxpr/cond
  425.0 8.8 %collective-permute-start.1 = (bf16[1,48,3072]{2,1,0:T(8,128)(2,1)}, bf16[1,48,3072]{2,1,0:T(8,128)(2,1)S(1)}, u32[]{:S(2)}, u32[]{:S(2)}) collective-permute-start(bf16[1,48,3072]{2,1,0:T(8,128)(2,1)} %get-tuple-element.1210), channel_id=1, source_target_pairs={{4,0},{8,4},{12,8},{5,1},{9,5},{13,9},{6,2},{10,6},{14,10},{7,3},{... | collective-permute-start | bytes 884744 | tf_op jit(solution)/shard_map/while/body/eval_jaxpr/ppermute | solution.py:21
  437.7 0.9 copy-start.1
  445.2 4.4 copy-start
  449.6 8.3 %copy-start.2 = (bf16[3,1,48,3072]{3,2,1,0:T(8,128)(2,1)S(1)}, bf16[3,1,48,3072]{3,2,1,0:T(8,128)(2,1)}, u32[]{:S(2)}) copy-start(bf16[3,1,48,3072]{3,2,1,0:T(8,128)(2,1)} %copy-done.1) | copy-start | bytes 2654212 | tf_op jit(solution)/shard_map/while/body/eval_jaxpr/cond
  457.9 8.8 %collective-permute-start.1 = (bf16[1,48,3072]{2,1,0:T(8,128)(2,1)}, bf16[1,48,3072]{2,1,0:T(8,128)(2,1)S(1)}, u32[]{:S(2)}, u32[]{:S(2)}) collective-permute-start(bf16[1,48,3072]{2,1,0:T(8,128)(2,1)} %get-tuple-element.1210), channel_id=1, source_target_pairs={{4,0},{8,4},{12,8},{5,1},{9,5},{13,9},{6,2},{10,6},{14,10},{7,3},{... | collective-permute-start | bytes 884744 | tf_op jit(solution)/shard_map/while/body/eval_jaxpr/ppermute | solution.py:21
  470.5 0.9 copy-start.1
  478.0 4.4 copy-start
  482.4 8.3 %copy-start.2 = (bf16[3,1,48,3072]{3,2,1,0:T(8,128)(2,1)S(1)}, bf16[3,1,48,3072]{3,2,1,0:T(8,128)(2,1)}, u32[]{:S(2)}) copy-start(bf16[3,1,48,3072]{3,2,1,0:T(8,128)(2,1)} %copy-done.1) | copy-start | bytes 2654212 | tf_op jit(solution)/shard_map/while/body/eval_jaxpr/cond
  490.7 8.8 %collective-permute-start.1 = (bf16[1,48,3072]{2,1,0:T(8,128)(2,1)}, bf16[1,48,3072]{2,1,0:T(8,128)(2,1)S(1)}, u32[]{:S(2)}, u32[]{:S(2)}) collective-permute-start(bf16[1,48,3072]{2,1,0:T(8,128)(2,1)} %get-tuple-element.1210), channel_id=1, source_target_pairs={{4,0},{8,4},{12,8},{5,1},{9,5},{13,9},{6,2},{10,6},{14,10},{7,3},{... | collective-permute-start | bytes 884744 | tf_op jit(solution)/shard_map/while/body/eval_jaxpr/ppermute | solution.py:21
  499.5 0.9 copy-start.3
  499.5 59.7 %all-gather.6.cloned.1.call-start = ((), (), s32[]{:S(2)}) async-start(), calls=%async_computation.1 | async-start | bytes 4423680 | tf_op jit(solution)/shard_map/all_gather | solution.py:381
  501.6 28.4 %collective-permute-start.5 = (bf16[144,384]{1,0:T(8,128)(2,1)S(1)}, bf16[144,384]{1,0:T(8,128)(2,1)S(1)}, u32[]{:S(2)}, u32[]{:S(2)}) collective-permute-start(bf16[144,384]{1,0:T(8,128)(2,1)S(1)} %get-tuple-element.1033), channel_id=1, source_target_pairs={{0,1},{1,2},{2,3},{3,0},{4,5},{5,6},{6,7},{7,4},{8,9},{9,10},{10,1... | collective-permute-start | bytes 331784 | tf_op jit(solution)/shard_map/ppermute | solution.py:285
  501.6 30.0 %collective-permute-start.6 = (bf16[144,384]{1,0:T(8,128)(2,1)S(1)}, bf16[144,384]{1,0:T(8,128)(2,1)S(1)}, u32[]{:S(2)}, u32[]{:S(2)}) collective-permute-start(bf16[144,384]{1,0:T(8,128)(2,1)S(1)} %get-tuple-element.1032), channel_id=1, source_target_pairs={{0,2},{1,3},{2,0},{3,1},{4,6},{5,7},{6,4},{7,5},{8,10},{9,11},{10,... | collective-permute-start | bytes 331784 | tf_op jit(solution)/shard_map/ppermute | solution.py:285
  503.2 28.5 %collective-permute-start.7 = (bf16[144,384]{1,0:T(8,128)(2,1)S(1)}, bf16[144,384]{1,0:T(8,128)(2,1)S(1)}, u32[]{:S(2)}, u32[]{:S(2)}) collective-permute-start(bf16[144,384]{1,0:T(8,128)(2,1)S(1)} %get-tuple-element.1031), channel_id=1, source_target_pairs={{0,3},{1,0},{2,1},{3,2},{4,7},{5,4},{6,5},{7,6},{8,11},{9,8},{10,9... | collective-permute-start | bytes 331784 | tf_op jit(solution)/shard_map/ppermute | solution.py:285
  505.8 25.8 %collective-permute-start.2 = (bf16[144,768]{1,0:T(8,128)(2,1)S(1)}, bf16[144,768]{1,0:T(8,128)(2,1)S(1)}, u32[]{:S(2)}, u32[]{:S(2)}) collective-permute-start(bf16[144,768]{1,0:T(8,128)(2,1)S(1)} %get-tuple-element.1030), channel_id=1, source_target_pairs={{0,1},{1,2},{2,3},{3,0},{4,5},{5,6},{6,7},{7,4},{8,9},{9,10},{10,1... | collective-permute-start | bytes 663560 | tf_op jit(solution)/shard_map/ppermute | solution.py:285
  506.1 25.6 %collective-permute-start.3 = (bf16[144,768]{1,0:T(8,128)(2,1)S(1)}, bf16[144,768]{1,0:T(8,128)(2,1)S(1)}, u32[]{:S(2)}, u32[]{:S(2)}) collective-permute-start(bf16[144,768]{1,0:T(8,128)(2,1)S(1)} %get-tuple-element.1029), channel_id=1, source_target_pairs={{0,2},{1,3},{2,0},{3,1},{4,6},{5,7},{6,4},{7,5},{8,10},{9,11},{10,... | collective-permute-start | bytes 663560 | tf_op jit(solution)/shard_map/ppermute | solution.py:285
  530.0 5.0 collective-permute-start.4
Sparse Core Ops, SparseCore 0:
  499.6 28.7 all-gather.3
  530.1 29.0 all-gather.5

commit v3 on v2

--- a/solution.py
+++ b/solution.py
@@ -131,13 +131,19 @@
 CHUNKS = 4
 
 
-def gather_kernel(chips, groups, joined_ref, out_ref, full_joined, full_out, local_sems, *sems):
-    send_x, recv_x, send_y, recv_y, send_own, recv_own, send_c, recv_c = sems
+def gather_kernel(chips, groups, joined_ref, out_ref, full_joined, full_out, held_joined, held_out, *sems):
+    load_sems, store_sems, send_x, recv_x, send_y, recv_y, send_own, recv_own, send_c, recv_c = sems
     me = lax.axis_index("dp")
     chip, core = me // CORES, lax.rem(me, CORES)
     group = lax.axis_index("groups")
     sibling = me + 1 - 2 * core
     pairs = ((joined_ref, full_joined), (out_ref, full_out))
+    held = (held_joined, held_out)
+    loads = [
+        pltpu.make_async_copy(pairs[w][0], held[w], load_sems.at[w]) for w in range(2)
+    ]
+    for copy in loads:
+        copy.start()
 
     barrier = pltpu.get_barrier_semaphore()
     partners = [{"dp": sibling}]
@@ -185,7 +191,8 @@
         place = full.at[pl.ds(me * rows, rows)]
         own.append(remote(mine, place, send_own.at[w], recv_own.at[w], partners[0]))
         own[-1].start()
-        local.append(pltpu.make_async_copy(mine, place, local_sems.at[w]))
+        loads[w].wait()
+        local.append(pltpu.make_async_copy(held[w], place, store_sems.at[w]))
         local[-1].start()
 
     second, third = {}, []
@@ -264,11 +271,14 @@
         ],
         in_specs=[anywhere] * 2,
         out_specs=[anywhere] * 2,
-        scratch_shapes=[dma((2,)), dma(x_shape), dma(x_shape)]
+        scratch_shapes=[pltpu.VMEM(each.shape, each.dtype) for each in shards]
+        + [dma((2,)), dma((2,)), dma(x_shape), dma(x_shape)]
         + [dma(x_shape + (groups - 1,))] * 2
         + [dma((2,))] * 2
         + [dma(x_shape + (groups,))] * 2,
-        compiler_params=pltpu.CompilerParams(collective_id=0, has_side_effects=True),
+        compiler_params=pltpu.CompilerParams(
+            collective_id=0, has_side_effects=True, vmem_limit_bytes=16 << 20
+        ),
     )(*shards)
 
 

time: 573 us -> 493 us (0.86)
  Pallas kernels: 154 us -> 68.8 us
    pallas_call x1, Pallas kernels: 154 us -> 68.8 us  [gather_weights(): pl.pallas_call(functools.partial(gather_kernel, chips, groups), out_shape...]
where the time goes in v3:
time: 493 us; the launch traced here: 492 us
  waiting for transfers between devices  179 us (36%)
  matrix products  98.3 us (20%)
  Pallas kernels  68.8 us (14%)
  starting transfers between devices  63.3 us (13%)
  local copies, waits for them, and re-layouts  30.3 us (6%)
  blocking collectives  20.8 us (4%)
  other arithmetic  15.4 us (3%)
  between operations  14.2 us (3%)
    ppermute x12, waiting for transfers between devices, from_behind(): lax.ppermute(value, axis, [(source, source + steps) for source in range(i...  160 us
    pallas_call x1, Pallas kernels, gather_weights(): pl.pallas_call(functools.partial(gather_kernel, chips, groups), out_shape...  68.8 us
    ppermute x12, starting transfers between devices, from_behind(): lax.ppermute(value, axis, [(source, source + steps) for source in range(i...  58.7 us
    dot_general x3, matrix products, layer_backward(): lax.dot_general(grad_joined_rows.reshape(-1, grad_joined_rows.shape[2]),...  21.7 us
    all_gather x1, blocking collectives, body(): gain_total = jnp.sum(lax.all_gather(stores[4], 'dp', axis=0), axis=0)  20.8 us
    dot_general x3, matrix products, layer_backward(): lax.dot_general(upstream.reshape(-1, model_width), w_out, (((1,), (1,)),...  19.9 us
    dot_general x3, matrix products, project(): jnp.dot(normed.reshape(-1, model_width), weight, preferred_element_type=j...  19.6 us
    dot_general x3, matrix products, layer_forward(): jnp.dot(mixed_heads.reshape(-1, mixed_heads.shape[2]), w_out, preferred_e...  16.3 us
  transfers between devices with their start and end apart: 20, of which 14 were waited for; matrix products, arithmetic and copies ran while one was open for 2% of the time, Pallas kernels for 0%

profile of v3, /device:TPU:0, one launch (start us, length us, event | category | flops | bytes accessed | tf_op | source)
XLA Modules:
  0.0 491.8 jit_solution(9578483095778957420)
XLA Ops:
  11.7 68.8 %shard_map.85 = (bf16[3072,1664]{1,0:T(8,128)(2,1)}, bf16[1536,3072]{1,0:T(8,128)(2,1)}) custom-call(bf16[768,1664]{1,0:T(8,128)(2,1)S(1)} %bitcast.196, bf16[384,3072]{1,0:T(8,128)(2,1)S(1)} %bitcast.197), custom_call_target="tpu_custom_call" | custom-call | tf_op jit(solution)/shard_map/pallas_call | solution.py:266
  81.5 126.7 %while.45 = (s32[]{:T(128)}, bf16[1,48,3072]{2,1,0:T(8,128)(2,1)S(1)}, bf16[3,1,48,3072]{3,2,1,0:T(8,128)(2,1)S(1)}, bf16[3,1,48,1664]{3,2,1,0:T(8,128)(2,1)}, s...) while((s32[]{:T(128)}, ...), condition=%wide.region_7.8_spmd.clone, body=%wide.region_1.7_spmd.clone.sunk | while | flops 960089920 | bytes 26415392 | solution.py:346
  81.5 14.7 %conditional.6 = (bf16[1,48,3072]{2,1,0:T(8,128)(2,1)S(1)}, bf16[3,1,48,3072]{3,2,1,0:T(8,128)(2,1)S(1)}, bf16[3,1,48,1664]{3,2,1,0:T(8,128)(2,1)}) conditional(s32[]{:T(128)} %convert_element_type.242, (bf16[3,1,48,3072]{3,2,1,0:T(8,128)(2,1)S(1)}, bf16[3,1,48,1664]{3,2,1,0:T(8,128)(2,1)}) %tuple.126, (pred[]{:T(512)}, s32[]{:T(128)}, ...), branch_computations={%region_2.2_spmd, %region_3.6_spmd} | conditional | flops 960089920 | bytes 25228092 | solution.py:336
  82.8 6.5 %bitcast_dynamic-update-slice_fusion.1 = (bf16[3,1,48,1664]{3,2,1,0:T(8,128)(2,1)}, bf16[48,1664]{1,0:T(8,128)(2,1)S(1)}) fusion(bf16[3,1,48,1664]{3,2,1,0:T(8,128)(2,1)} %get-tuple-element.807, s32[]{:T(128)S(6)} %min.20, bf16[3072,1664]{1,0:T(8,128)(2,1)} %get-tuple-element.803, bf16[1,48,3072]{2,1,0:T(8,128)(2,1)S(1)} %get-tuple-element.1013, ...), kind=kOutput, calls=%fused_computation.26 | convolution fusion | flops 491403264 | bytes 10850500 | tf_op jit(solution)/shard_map/while/body/eval_jaxpr/cond/branch_1_fun/dot_general | solution.py:40
  97.5 7.0 %collective-permute-done = bf16[1,48,3072]{2,1,0:T(8,128)(2,1)S(1)} collective-permute-done((bf16[1,48,3072]{2,1,0:T(8,128)(2,1)S(1)}, bf16[1,48,3072]{2,1,0:T(8,128)(2,1)S(1)}, u32[]{:S(2)}, u32[]{:S(2)}) %collective-permute-start) | collective-permute-done | bytes 294944 | tf_op jit(solution)/shard_map/while/body/eval_jaxpr/ppermute | solution.py:21
  104.5 14.7 %conditional.6 = (bf16[1,48,3072]{2,1,0:T(8,128)(2,1)S(1)}, bf16[3,1,48,3072]{3,2,1,0:T(8,128)(2,1)S(1)}, bf16[3,1,48,1664]{3,2,1,0:T(8,128)(2,1)}) conditional(s32[]{:T(128)} %convert_element_type.242, (bf16[3,1,48,3072]{3,2,1,0:T(8,128)(2,1)S(1)}, bf16[3,1,48,1664]{3,2,1,0:T(8,128)(2,1)}) %tuple.126, (pred[]{:T(512)}, s32[]{:T(128)}, ...), branch_computations={%region_2.2_spmd, %region_3.6_spmd} | conditional | flops 960089920 | bytes 25228092 | solution.py:336
  105.8 6.5 %bitcast_dynamic-update-slice_fusion.1 = (bf16[3,1,48,1664]{3,2,1,0:T(8,128)(2,1)}, bf16[48,1664]{1,0:T(8,128)(2,1)S(1)}) fusion(bf16[3,1,48,1664]{3,2,1,0:T(8,128)(2,1)} %get-tuple-element.807, s32[]{:T(128)S(6)} %min.20, bf16[3072,1664]{1,0:T(8,128)(2,1)} %get-tuple-element.803, bf16[1,48,3072]{2,1,0:T(8,128)(2,1)S(1)} %get-tuple-element.1013, ...), kind=kOutput, calls=%fused_computation.26 | convolution fusion | flops 491403264 | bytes 10850500 | tf_op jit(solution)/shard_map/while/body/eval_jaxpr/cond/branch_1_fun/dot_general | solution.py:40
  123.6 6.2 %collective-permute-done = bf16[1,48,3072]{2,1,0:T(8,128)(2,1)S(1)} collective-permute-done((bf16[1,48,3072]{2,1,0:T(8,128)(2,1)S(1)}, bf16[1,48,3072]{2,1,0:T(8,128)(2,1)S(1)}, u32[]{:S(2)}, u32[]{:S(2)}) %collective-permute-start) | collective-permute-done | bytes 294944 | tf_op jit(solution)/shard_map/while/body/eval_jaxpr/ppermute | solution.py:21
  129.8 14.7 %conditional.6 = (bf16[1,48,3072]{2,1,0:T(8,128)(2,1)S(1)}, bf16[3,1,48,3072]{3,2,1,0:T(8,128)(2,1)S(1)}, bf16[3,1,48,1664]{3,2,1,0:T(8,128)(2,1)}) conditional(s32[]{:T(128)} %convert_element_type.242, (bf16[3,1,48,3072]{3,2,1,0:T(8,128)(2,1)S(1)}, bf16[3,1,48,1664]{3,2,1,0:T(8,128)(2,1)}) %tuple.126, (pred[]{:T(512)}, s32[]{:T(128)}, ...), branch_computations={%region_2.2_spmd, %region_3.6_spmd} | conditional | flops 960089920 | bytes 25228092 | solution.py:336
  131.1 6.5 %bitcast_dynamic-update-slice_fusion.1 = (bf16[3,1,48,1664]{3,2,1,0:T(8,128)(2,1)}, bf16[48,1664]{1,0:T(8,128)(2,1)S(1)}) fusion(bf16[3,1,48,1664]{3,2,1,0:T(8,128)(2,1)} %get-tuple-element.807, s32[]{:T(128)S(6)} %min.20, bf16[3072,1664]{1,0:T(8,128)(2,1)} %get-tuple-element.803, bf16[1,48,3072]{2,1,0:T(8,128)(2,1)S(1)} %get-tuple-element.1013, ...), kind=kOutput, calls=%fused_computation.26 | convolution fusion | flops 491403264 | bytes 10850500 | tf_op jit(solution)/shard_map/while/body/eval_jaxpr/cond/branch_1_fun/dot_general | solution.py:40
  154.3 19.0 %collective-permute-start = (bf16[1,48,3072]{2,1,0:T(8,128)(2,1)S(1)}, bf16[1,48,3072]{2,1,0:T(8,128)(2,1)S(1)}, u32[]{:S(2)}, u32[]{:S(2)}) collective-permute-start(bf16[1,48,3072]{2,1,0:T(8,128)(2,1)S(1)} %get-tuple-element.1191), channel_id=1, source_target_pairs={{0,4},{4,8},{8,12},{1,5},{5,9},{9,13},{2,6},{6,10},{10,14},{3,7},{... | collective-permute-start | bytes 884744 | tf_op jit(solution)/shard_map/while/body/eval_jaxpr/ppermute | solution.py:21
  186.5 17.5 %collective-permute-start = (bf16[1,48,3072]{2,1,0:T(8,128)(2,1)S(1)}, bf16[1,48,3072]{2,1,0:T(8,128)(2,1)S(1)}, u32[]{:S(2)}, u32[]{:S(2)}) collective-permute-start(bf16[1,48,3072]{2,1,0:T(8,128)(2,1)S(1)} %get-tuple-element.1191), channel_id=1, source_target_pairs={{0,4},{4,8},{8,12},{1,5},{5,9},{9,13},{2,6},{6,10},{10,14},{3,7},{... | collective-permute-start | bytes 884744 | tf_op jit(solution)/shard_map/while/body/eval_jaxpr/ppermute | solution.py:21
  210.9 210.7 %while.46 = (s32[]{:T(128)}, bf16[1,48,3072]{2,1,0:T(8,128)(2,1)S(1)}, bf16[3,1,48,3072]{3,2,1,0:T(8,128)(2,1)}, bf16[3,1,48,1664]{3,2,1,0:T(8,128)(2,1)}, bf16[...) while((s32[]{:T(128)}, ...), condition=%wide.region_17.18_spmd.clone, body=%wide.region_8.17_spmd.clone.sunk | while | flops 991109952 | bytes 41387848 | solution.py:384
  213.2 8.0 %collective-permute-done.1 = bf16[1,48,3072]{2,1,0:T(8,128)(2,1)S(1)} collective-permute-done((bf16[1,48,3072]{2,1,0:T(8,128)(2,1)}, bf16[1,48,3072]{2,1,0:T(8,128)(2,1)S(1)}, u32[]{:S(2)}, u32[]{:S(2)}) %collective-permute-start.1) | collective-permute-done | bytes 294944 | tf_op jit(solution)/shard_map/while/body/eval_jaxpr/ppermute | solution.py:21
  223.2 20.7 %collective-permute-done.1 = bf16[1,48,3072]{2,1,0:T(8,128)(2,1)S(1)} collective-permute-done((bf16[1,48,3072]{2,1,0:T(8,128)(2,1)}, bf16[1,48,3072]{2,1,0:T(8,128)(2,1)S(1)}, u32[]{:S(2)}, u32[]{:S(2)}) %collective-permute-start.1) | collective-permute-done | bytes 294944 | tf_op jit(solution)/shard_map/while/body/eval_jaxpr/ppermute | solution.py:21
  245.9 77.1 %collective-permute-done.1 = bf16[1,48,3072]{2,1,0:T(8,128)(2,1)S(1)} collective-permute-done((bf16[1,48,3072]{2,1,0:T(8,128)(2,1)}, bf16[1,48,3072]{2,1,0:T(8,128)(2,1)S(1)}, u32[]{:S(2)}, u32[]{:S(2)}) %collective-permute-start.1) | collective-permute-done | bytes 294944 | tf_op jit(solution)/shard_map/while/body/eval_jaxpr/ppermute | solution.py:21
  323.1 24.0 %conditional.7 = (bf16[1,48,3072]{2,1,0:T(8,128)(2,1)}, bf16[3,1,48,3072]{3,2,1,0:T(8,128)(2,1)}, bf16[3,1,48,1664]{3,2,1,0:T(8,128)(2,1)}, bf16[3,1,48,1536]{3,...) conditional(s32[]{:T(128)} %convert_element_type.243, ...), branch_computations={%region_9.9_spmd, %region_10.16_spmd} | conditional | flops 991109952 | bytes 40200444 | solution.py:373
  327.8 6.6 %convolution_convert_fusion.2 = bf16[48,1536]{1,0:T(8,128)(2,1)S(1)} fusion(bf16[1536,3072]{1,0:T(8,128)(2,1)} %get-tuple-element.835, bf16[1,48,3072]{2,1,0:T(8,128)(2,1)S(1)} %get-tuple-element.1015), kind=kOutput, calls=%fused_computation.31 | convolution fusion | flops 453058560 | bytes 9879552 | tf_op jit(solution)/shard_map/while/body/eval_jaxpr/cond/branch_1_fun/dot_general | solution.py:82
  338.9 7.2 %fusion.35 = (f32[3072]{0:T(1024)S(1)}, f32[48]{0:T(128)S(1)}, f32[48,3072]{1,0:T(8,128)S(1)}) fusion(f32[48]{0:T(128)S(1)} %get-tuple-element.1021, bf16[3,1,48,3072]{3,2,1,0:T(8,128)(2,1)S(1)} %get-tuple-element.832, s32[]{:T(128)S(6)} %min.21, f32[3072]{0:T(1024)S(1)} %bitcast.203, bf16[48,1664]{1,0:T(8,128)(2,1)S(1)} %concatenate.26, ...), kind=kOutput, calls=%fused_computation.57 | convolution fusion | flops 491762624 | bytes 11293060 | tf_op jit(solution)/shard_map/while/body/eval_jaxpr/cond/branch_1_fun/dot_general | solution.py:106
  348.4 7.5 %collective-permute-done.1 = bf16[1,48,3072]{2,1,0:T(8,128)(2,1)S(1)} collective-permute-done((bf16[1,48,3072]{2,1,0:T(8,128)(2,1)}, bf16[1,48,3072]{2,1,0:T(8,128)(2,1)S(1)}, u32[]{:S(2)}, u32[]{:S(2)}) %collective-permute-start.1) | collective-permute-done | bytes 294944 | tf_op jit(solution)/shard_map/while/body/eval_jaxpr/ppermute | solution.py:21
  355.9 24.0 %conditional.7 = (bf16[1,48,3072]{2,1,0:T(8,128)(2,1)}, bf16[3,1,48,3072]{3,2,1,0:T(8,128)(2,1)}, bf16[3,1,48,1664]{3,2,1,0:T(8,128)(2,1)}, bf16[3,1,48,1536]{3,...) conditional(s32[]{:T(128)} %convert_element_type.243, ...), branch_computations={%region_9.9_spmd, %region_10.16_spmd} | conditional | flops 991109952 | bytes 40200444 | solution.py:373
  360.7 6.6 %convolution_convert_fusion.2 = bf16[48,1536]{1,0:T(8,128)(2,1)S(1)} fusion(bf16[1536,3072]{1,0:T(8,128)(2,1)} %get-tuple-element.835, bf16[1,48,3072]{2,1,0:T(8,128)(2,1)S(1)} %get-tuple-element.1015), kind=kOutput, calls=%fused_computation.31 | convolution fusion | flops 453058560 | bytes 9879552 | tf_op jit(solution)/shard_map/while/body/eval_jaxpr/cond/branch_1_fun/dot_general | solution.py:82
  371.7 7.2 %fusion.35 = (f32[3072]{0:T(1024)S(1)}, f32[48]{0:T(128)S(1)}, f32[48,3072]{1,0:T(8,128)S(1)}) fusion(f32[48]{0:T(128)S(1)} %get-tuple-element.1021, bf16[3,1,48,3072]{3,2,1,0:T(8,128)(2,1)S(1)} %get-tuple-element.832, s32[]{:T(128)S(6)} %min.21, f32[3072]{0:T(1024)S(1)} %bitcast.203, bf16[48,1664]{1,0:T(8,128)(2,1)S(1)} %concatenate.26, ...), kind=kOutput, calls=%fused_computation.57 | convolution fusion | flops 491762624 | bytes 11293060 | tf_op jit(solution)/shard_map/while/body/eval_jaxpr/cond/branch_1_fun/dot_general | solution.py:106
  381.2 7.5 %collective-permute-done.1 = bf16[1,48,3072]{2,1,0:T(8,128)(2,1)S(1)} collective-permute-done((bf16[1,48,3072]{2,1,0:T(8,128)(2,1)}, bf16[1,48,3072]{2,1,0:T(8,128)(2,1)S(1)}, u32[]{:S(2)}, u32[]{:S(2)}) %collective-permute-start.1) | collective-permute-done | bytes 294944 | tf_op jit(solution)/shard_map/while/body/eval_jaxpr/ppermute | solution.py:21
  388.8 24.0 %conditional.7 = (bf16[1,48,3072]{2,1,0:T(8,128)(2,1)}, bf16[3,1,48,3072]{3,2,1,0:T(8,128)(2,1)}, bf16[3,1,48,1664]{3,2,1,0:T(8,128)(2,1)}, bf16[3,1,48,1536]{3,...) conditional(s32[]{:T(128)} %convert_element_type.243, ...), branch_computations={%region_9.9_spmd, %region_10.16_spmd} | conditional | flops 991109952 | bytes 40200444 | solution.py:373
  393.5 6.6 %convolution_convert_fusion.2 = bf16[48,1536]{1,0:T(8,128)(2,1)S(1)} fusion(bf16[1536,3072]{1,0:T(8,128)(2,1)} %get-tuple-element.835, bf16[1,48,3072]{2,1,0:T(8,128)(2,1)S(1)} %get-tuple-element.1015), kind=kOutput, calls=%fused_computation.31 | convolution fusion | flops 453058560 | bytes 9879552 | tf_op jit(solution)/shard_map/while/body/eval_jaxpr/cond/branch_1_fun/dot_general | solution.py:82
  404.5 7.2 %fusion.35 = (f32[3072]{0:T(1024)S(1)}, f32[48]{0:T(128)S(1)}, f32[48,3072]{1,0:T(8,128)S(1)}) fusion(f32[48]{0:T(128)S(1)} %get-tuple-element.1021, bf16[3,1,48,3072]{3,2,1,0:T(8,128)(2,1)S(1)} %get-tuple-element.832, s32[]{:T(128)S(6)} %min.21, f32[3072]{0:T(1024)S(1)} %bitcast.203, bf16[48,1664]{1,0:T(8,128)(2,1)S(1)} %concatenate.26, ...), kind=kOutput, calls=%fused_computation.57 | convolution fusion | flops 491762624 | bytes 11293060 | tf_op jit(solution)/shard_map/while/body/eval_jaxpr/cond/branch_1_fun/dot_general | solution.py:106
  414.0 7.5 %collective-permute-done.1 = bf16[1,48,3072]{2,1,0:T(8,128)(2,1)S(1)} collective-permute-done((bf16[1,48,3072]{2,1,0:T(8,128)(2,1)}, bf16[1,48,3072]{2,1,0:T(8,128)(2,1)S(1)}, u32[]{:S(2)}, u32[]{:S(2)}) %collective-permute-start.1) | collective-permute-done | bytes 294944 | tf_op jit(solution)/shard_map/while/body/eval_jaxpr/ppermute | solution.py:21
  428.7 20.8 %all-gather = f32[12288]{0:T(1024)S(1)} all-gather(f32[3072]{0:T(1024)S(1)} %get-tuple-element.886), channel_id=2, replica_groups=mesh['groups'=2,'section'=4,'dp'=4] {'dp'}, dimensions={0}, use_global_device_ids=true | all-gather | bytes 61440 | tf_op jit(solution)/shard_map/all_gather | solution.py:390
  457.1 6.2 %convolution_bitcast_fusion.5 = f32[1,768,1664]{2,1,0:T(8,128)} fusion(bf16[576,768]{1,0:T(8,128)(2,1)S(1)} %bitcast.211, bf16[576,1664]{1,0:T(8,128)(2,1)} %all-gather.4.cloned.1.call-done), kind=kOutput, calls=%fused_computation.89 | convolution fusion | flops 1472200704 | bytes 7913472 | tf_op jit(solution)/shard_map/dot_general | solution.py:396
  463.2 15.5 %all-gather.6.cloned.1.call-done = bf16[576,3072]{1,0:T(8,128)(2,1)} async-done(((bf16[144,3072]{1,0:T(8,128)(2,1)}), bf16[576,3072]{1,0:T(8,128)(2,1)}) %all-gather.6.cloned.1.call-update) | async-done | bytes 3538960 | tf_op jit(solution)/shard_map/all_gather | solution.py:391
  478.7 6.2 %convolution_bitcast_fusion.4 = f32[1,384,3072]{2,1,0:T(8,128)} fusion(bf16[576,384]{1,0:T(8,128)(2,1)S(1)} %bitcast.208, bf16[576,3072]{1,0:T(8,128)(2,1)} %all-gather.6.cloned.1.call-done), kind=kOutput, calls=%fused_computation.88 | convolution fusion | flops 1358954496 | bytes 8699904 | tf_op jit(solution)/shard_map/dot_general | solution.py:393
  (226 shorter events, 121.9 us)
Async XLA Ops:
  7.2 449.9 %all-gather.4.cloned.1.call-start = ((), (), s32[]{:S(2)}) async-start(), calls=%async_computation | async-start | bytes 2396160 | tf_op jit(solution)/shard_map/all_gather | solution.py:392
  8.3 1.7 copy-start
  10.0 1.7 copy-start.1
  96.2 8.4 %collective-permute-start = (bf16[1,48,3072]{2,1,0:T(8,128)(2,1)S(1)}, bf16[1,48,3072]{2,1,0:T(8,128)(2,1)S(1)}, u32[]{:S(2)}, u32[]{:S(2)}) collective-permute-start(bf16[1,48,3072]{2,1,0:T(8,128)(2,1)S(1)} %get-tuple-element.1191), channel_id=1, source_target_pairs={{0,4},{4,8},{8,12},{1,5},{5,9},{9,13},{2,6},{6,10},{10,14},{3,7},{... | collective-permute-start | bytes 884744 | tf_op jit(solution)/shard_map/while/body/eval_jaxpr/ppermute | solution.py:21
  119.2 10.6 %collective-permute-start = (bf16[1,48,3072]{2,1,0:T(8,128)(2,1)S(1)}, bf16[1,48,3072]{2,1,0:T(8,128)(2,1)S(1)}, u32[]{:S(2)}, u32[]{:S(2)}) collective-permute-start(bf16[1,48,3072]{2,1,0:T(8,128)(2,1)S(1)} %get-tuple-element.1191), channel_id=1, source_target_pairs={{0,4},{4,8},{8,12},{1,5},{5,9},{9,13},{2,6},{6,10},{10,14},{3,7},{... | collective-permute-start | bytes 884744 | tf_op jit(solution)/shard_map/while/body/eval_jaxpr/ppermute | solution.py:21
  144.5 9.7 %collective-permute-start = (bf16[1,48,3072]{2,1,0:T(8,128)(2,1)S(1)}, bf16[1,48,3072]{2,1,0:T(8,128)(2,1)S(1)}, u32[]{:S(2)}, u32[]{:S(2)}) collective-permute-start(bf16[1,48,3072]{2,1,0:T(8,128)(2,1)S(1)} %get-tuple-element.1191), channel_id=1, source_target_pairs={{0,4},{4,8},{8,12},{1,5},{5,9},{9,13},{2,6},{6,10},{10,14},{3,7},{... | collective-permute-start | bytes 884744 | tf_op jit(solution)/shard_map/while/body/eval_jaxpr/ppermute | solution.py:21
  154.3 23.4 %collective-permute-start = (bf16[1,48,3072]{2,1,0:T(8,128)(2,1)S(1)}, bf16[1,48,3072]{2,1,0:T(8,128)(2,1)S(1)}, u32[]{:S(2)}, u32[]{:S(2)}) collective-permute-start(bf16[1,48,3072]{2,1,0:T(8,128)(2,1)S(1)} %get-tuple-element.1191), channel_id=1, source_target_pairs={{0,4},{4,8},{8,12},{1,5},{5,9},{9,13},{2,6},{6,10},{10,14},{3,7},{... | collective-permute-start | bytes 884744 | tf_op jit(solution)/shard_map/while/body/eval_jaxpr/ppermute | solution.py:21
  177.8 8.6 %collective-permute-start = (bf16[1,48,3072]{2,1,0:T(8,128)(2,1)S(1)}, bf16[1,48,3072]{2,1,0:T(8,128)(2,1)S(1)}, u32[]{:S(2)}, u32[]{:S(2)}) collective-permute-start(bf16[1,48,3072]{2,1,0:T(8,128)(2,1)S(1)} %get-tuple-element.1191), channel_id=1, source_target_pairs={{0,4},{4,8},{8,12},{1,5},{5,9},{9,13},{2,6},{6,10},{10,14},{3,7},{... | collective-permute-start | bytes 884744 | tf_op jit(solution)/shard_map/while/body/eval_jaxpr/ppermute | solution.py:21
  186.5 21.7 %collective-permute-start = (bf16[1,48,3072]{2,1,0:T(8,128)(2,1)S(1)}, bf16[1,48,3072]{2,1,0:T(8,128)(2,1)S(1)}, u32[]{:S(2)}, u32[]{:S(2)}) collective-permute-start(bf16[1,48,3072]{2,1,0:T(8,128)(2,1)S(1)} %get-tuple-element.1191), channel_id=1, source_target_pairs={{0,4},{4,8},{8,12},{1,5},{5,9},{9,13},{2,6},{6,10},{10,14},{3,7},{... | collective-permute-start | bytes 884744 | tf_op jit(solution)/shard_map/while/body/eval_jaxpr/ppermute | solution.py:21
  211.9 9.3 %collective-permute-start.1 = (bf16[1,48,3072]{2,1,0:T(8,128)(2,1)}, bf16[1,48,3072]{2,1,0:T(8,128)(2,1)S(1)}, u32[]{:S(2)}, u32[]{:S(2)}) collective-permute-start(bf16[1,48,3072]{2,1,0:T(8,128)(2,1)} %get-tuple-element.1210), channel_id=1, source_target_pairs={{4,0},{8,4},{12,8},{5,1},{9,5},{13,9},{6,2},{10,6},{14,10},{7,3},{... | collective-permute-start | bytes 884744 | tf_op jit(solution)/shard_map/while/body/eval_jaxpr/ppermute | solution.py:21
  221.9 22.0 %collective-permute-start.1 = (bf16[1,48,3072]{2,1,0:T(8,128)(2,1)}, bf16[1,48,3072]{2,1,0:T(8,128)(2,1)S(1)}, u32[]{:S(2)}, u32[]{:S(2)}) collective-permute-start(bf16[1,48,3072]{2,1,0:T(8,128)(2,1)} %get-tuple-element.1210), channel_id=1, source_target_pairs={{4,0},{8,4},{12,8},{5,1},{9,5},{13,9},{6,2},{10,6},{14,10},{7,3},{... | collective-permute-start | bytes 884744 | tf_op jit(solution)/shard_map/while/body/eval_jaxpr/ppermute | solution.py:21
  244.7 78.4 %collective-permute-start.1 = (bf16[1,48,3072]{2,1,0:T(8,128)(2,1)}, bf16[1,48,3072]{2,1,0:T(8,128)(2,1)S(1)}, u32[]{:S(2)}, u32[]{:S(2)}) collective-permute-start(bf16[1,48,3072]{2,1,0:T(8,128)(2,1)} %get-tuple-element.1210), channel_id=1, source_target_pairs={{4,0},{8,4},{12,8},{5,1},{9,5},{13,9},{6,2},{10,6},{14,10},{7,3},{... | collective-permute-start | bytes 884744 | tf_op jit(solution)/shard_map/while/body/eval_jaxpr/ppermute | solution.py:21
  326.9 0.9 copy-start.3
  334.5 4.5 copy-start.2
  338.8 8.3 %copy-start.4 = (bf16[3,1,48,3072]{3,2,1,0:T(8,128)(2,1)S(1)}, bf16[3,1,48,3072]{3,2,1,0:T(8,128)(2,1)}, u32[]{:S(2)}) copy-start(bf16[3,1,48,3072]{3,2,1,0:T(8,128)(2,1)} %copy-done.3) | copy-start | bytes 2654212 | tf_op jit(solution)/shard_map/while/body/eval_jaxpr/cond
  347.1 8.8 %collective-permute-start.1 = (bf16[1,48,3072]{2,1,0:T(8,128)(2,1)}, bf16[1,48,3072]{2,1,0:T(8,128)(2,1)S(1)}, u32[]{:S(2)}, u32[]{:S(2)}) collective-permute-start(bf16[1,48,3072]{2,1,0:T(8,128)(2,1)} %get-tuple-element.1210), channel_id=1, source_target_pairs={{4,0},{8,4},{12,8},{5,1},{9,5},{13,9},{6,2},{10,6},{14,10},{7,3},{... | collective-permute-start | bytes 884744 | tf_op jit(solution)/shard_map/while/body/eval_jaxpr/ppermute | solution.py:21
  359.8 0.9 copy-start.3
  367.3 4.4 copy-start.2
  371.6 8.3 %copy-start.4 = (bf16[3,1,48,3072]{3,2,1,0:T(8,128)(2,1)S(1)}, bf16[3,1,48,3072]{3,2,1,0:T(8,128)(2,1)}, u32[]{:S(2)}) copy-start(bf16[3,1,48,3072]{3,2,1,0:T(8,128)(2,1)} %copy-done.3) | copy-start | bytes 2654212 | tf_op jit(solution)/shard_map/while/body/eval_jaxpr/cond
  379.9 8.8 %collective-permute-start.1 = (bf16[1,48,3072]{2,1,0:T(8,128)(2,1)}, bf16[1,48,3072]{2,1,0:T(8,128)(2,1)S(1)}, u32[]{:S(2)}, u32[]{:S(2)}) collective-permute-start(bf16[1,48,3072]{2,1,0:T(8,128)(2,1)} %get-tuple-element.1210), channel_id=1, source_target_pairs={{4,0},{8,4},{12,8},{5,1},{9,5},{13,9},{6,2},{10,6},{14,10},{7,3},{... | collective-permute-start | bytes 884744 | tf_op jit(solution)/shard_map/while/body/eval_jaxpr/ppermute | solution.py:21
  392.6 0.9 copy-start.3
  400.1 4.4 copy-start.2
  404.4 8.3 %copy-start.4 = (bf16[3,1,48,3072]{3,2,1,0:T(8,128)(2,1)S(1)}, bf16[3,1,48,3072]{3,2,1,0:T(8,128)(2,1)}, u32[]{:S(2)}) copy-start(bf16[3,1,48,3072]{3,2,1,0:T(8,128)(2,1)} %copy-done.3) | copy-start | bytes 2654212 | tf_op jit(solution)/shard_map/while/body/eval_jaxpr/cond
  412.7 8.8 %collective-permute-start.1 = (bf16[1,48,3072]{2,1,0:T(8,128)(2,1)}, bf16[1,48,3072]{2,1,0:T(8,128)(2,1)S(1)}, u32[]{:S(2)}, u32[]{:S(2)}) collective-permute-start(bf16[1,48,3072]{2,1,0:T(8,128)(2,1)} %get-tuple-element.1210), channel_id=1, source_target_pairs={{4,0},{8,4},{12,8},{5,1},{9,5},{13,9},{6,2},{10,6},{14,10},{7,3},{... | collective-permute-start | bytes 884744 | tf_op jit(solution)/shard_map/while/body/eval_jaxpr/ppermute | solution.py:21
  421.6 0.9 copy-start.5
  421.6 57.1 %all-gather.6.cloned.1.call-start = ((), (), s32[]{:S(2)}) async-start(), calls=%async_computation.1 | async-start | bytes 4423680 | tf_op jit(solution)/shard_map/all_gather | solution.py:391
  423.6 28.6 %collective-permute-start.5 = (bf16[144,384]{1,0:T(8,128)(2,1)S(1)}, bf16[144,384]{1,0:T(8,128)(2,1)S(1)}, u32[]{:S(2)}, u32[]{:S(2)}) collective-permute-start(bf16[144,384]{1,0:T(8,128)(2,1)S(1)} %get-tuple-element.1033), channel_id=1, source_target_pairs={{0,1},{1,2},{2,3},{3,0},{4,5},{5,6},{6,7},{7,4},{8,9},{9,10},{10,1... | collective-permute-start | bytes 331784 | tf_op jit(solution)/shard_map/ppermute | solution.py:295
  423.6 29.2 %collective-permute-start.6 = (bf16[144,384]{1,0:T(8,128)(2,1)S(1)}, bf16[144,384]{1,0:T(8,128)(2,1)S(1)}, u32[]{:S(2)}, u32[]{:S(2)}) collective-permute-start(bf16[144,384]{1,0:T(8,128)(2,1)S(1)} %get-tuple-element.1032), channel_id=1, source_target_pairs={{0,2},{1,3},{2,0},{3,1},{4,6},{5,7},{6,4},{7,5},{8,10},{9,11},{10,... | collective-permute-start | bytes 331784 | tf_op jit(solution)/shard_map/ppermute | solution.py:295
  424.4 28.6 %collective-permute-start.7 = (bf16[144,384]{1,0:T(8,128)(2,1)S(1)}, bf16[144,384]{1,0:T(8,128)(2,1)S(1)}, u32[]{:S(2)}, u32[]{:S(2)}) collective-permute-start(bf16[144,384]{1,0:T(8,128)(2,1)S(1)} %get-tuple-element.1031), channel_id=1, source_target_pairs={{0,3},{1,0},{2,1},{3,2},{4,7},{5,4},{6,5},{7,6},{8,11},{9,8},{10,9... | collective-permute-start | bytes 331784 | tf_op jit(solution)/shard_map/ppermute | solution.py:295
  427.0 26.0 %collective-permute-start.2 = (bf16[144,768]{1,0:T(8,128)(2,1)S(1)}, bf16[144,768]{1,0:T(8,128)(2,1)S(1)}, u32[]{:S(2)}, u32[]{:S(2)}) collective-permute-start(bf16[144,768]{1,0:T(8,128)(2,1)S(1)} %get-tuple-element.1030), channel_id=1, source_target_pairs={{0,1},{1,2},{2,3},{3,0},{4,5},{5,6},{6,7},{7,4},{8,9},{9,10},{10,1... | collective-permute-start | bytes 663560 | tf_op jit(solution)/shard_map/ppermute | solution.py:295
  427.1 25.9 %collective-permute-start.3 = (bf16[144,768]{1,0:T(8,128)(2,1)S(1)}, bf16[144,768]{1,0:T(8,128)(2,1)S(1)}, u32[]{:S(2)}, u32[]{:S(2)}) collective-permute-start(bf16[144,768]{1,0:T(8,128)(2,1)S(1)} %get-tuple-element.1029), channel_id=1, source_target_pairs={{0,2},{1,3},{2,0},{3,1},{4,6},{5,7},{6,4},{7,5},{8,10},{9,11},{10,... | collective-permute-start | bytes 663560 | tf_op jit(solution)/shard_map/ppermute | solution.py:295
  452.2 4.8 collective-permute-start.4
Sparse Core Ops, SparseCore 0:
  421.7 27.5 all-gather.3
  450.9 27.7 all-gather.5

commit v4 on v3

--- a/solution.py
+++ b/solution.py
@@ -298,6 +298,12 @@
     return taken.reshape(n * count, width)
 
 
+def repeat(count, step, state):
+    for now in range(count):
+        state = step(now, state)
+    return state
+
+
 def body(stream_in, out_grad, mask_blocks, norm_gain, w_joined, w_out):
     full_joined, full_out = gather_weights(w_joined, w_out)
     gain_row = norm_gain[0]
@@ -313,43 +319,40 @@
     upstreams = out_grad.reshape(micro_count, per_group, length, model_width)
     allowed = allowed_tokens(mask_blocks, BLOCK_LEN).reshape(micro_count, per_group, length, length)
     step_count = micro_count + sections - 1
-    keep_shape = (micro_count, per_group, length, joined_width)
+    keep_shape = (micro_count + 1, per_group, length, joined_width)
 
     def forward_step(step_now, state_now):
         incoming, kept_inputs, kept_joined = state_now
         slot_index = step_now - section_index
         active = jnp.logical_and(slot_index >= 0, slot_index < micro_count)
         group_index = jnp.clip(slot_index, 0, micro_count - 1)
+        place = jnp.where(active, group_index, micro_count)
         source = jnp.where(section_index == 0, inputs[group_index], incoming)
 
         def forward_run(kept_pair):
             result, joined_rows = layer_forward(
                 source, gain_row, full_joined, full_out, allowed[group_index]
             )
-            new_inputs = lax.dynamic_update_index_in_dim(kept_pair[0], source, group_index, 0)
-            new_joined = lax.dynamic_update_index_in_dim(kept_pair[1], joined_rows, group_index, 0)
+            new_inputs = lax.dynamic_update_index_in_dim(kept_pair[0], source, place, 0)
+            new_joined = lax.dynamic_update_index_in_dim(kept_pair[1], joined_rows, place, 0)
             return (result, new_inputs, new_joined)
 
-        def forward_rest(kept_pair):
-            return (jnp.zeros_like(source), kept_pair[0], kept_pair[1])
-
-        result, kept_inputs, kept_joined = lax.cond(
-            active, forward_run, forward_rest, (kept_inputs, kept_joined)
-        )
+        result, kept_inputs, kept_joined = forward_run((kept_inputs, kept_joined))
         return (pass_forward(result), kept_inputs, kept_joined)
 
     start_state = (
         jnp.zeros((per_group, length, model_width), jnp.bfloat16),
-        jnp.zeros((micro_count, per_group, length, model_width), jnp.bfloat16),
+        jnp.zeros((micro_count + 1, per_group, length, model_width), jnp.bfloat16),
         jnp.zeros(keep_shape, jnp.bfloat16),
     )
-    _, kept_inputs, kept_joined = lax.fori_loop(0, step_count, forward_step, start_state)
+    _, kept_inputs, kept_joined = repeat(step_count, forward_step, start_state)
 
     def backward_step(step_now, state_now):
         incoming, stores = state_now
         slot_index = step_now - (sections - 1 - section_index)
         active = jnp.logical_and(slot_index >= 0, slot_index < micro_count)
         group_index = jnp.clip(slot_index, 0, micro_count - 1)
+        place = jnp.where(active, group_index, micro_count)
         upstream = jnp.where(section_index == sections - 1, upstreams[group_index], incoming)
 
         def backward_run(store_now):
@@ -359,33 +362,30 @@
                 source, gain_row, joined_rows, full_joined, full_out, allowed[group_index], upstream
             )
             new_store = (
-                lax.dynamic_update_index_in_dim(store_now[0], normed, group_index, 0),
-                lax.dynamic_update_index_in_dim(store_now[1], grad_joined_rows, group_index, 0),
-                lax.dynamic_update_index_in_dim(store_now[2], mixed_heads, group_index, 0),
-                lax.dynamic_update_index_in_dim(store_now[3], upstream, group_index, 0),
-                store_now[4] + gain_part,
+                lax.dynamic_update_index_in_dim(store_now[0], normed, place, 0),
+                lax.dynamic_update_index_in_dim(store_now[1], grad_joined_rows, place, 0),
+                lax.dynamic_update_index_in_dim(store_now[2], mixed_heads, place, 0),
+                lax.dynamic_update_index_in_dim(store_now[3], upstream, place, 0),
+                store_now[4] + jnp.where(active, gain_part, 0.0),
             )
             return (down_grad, new_store)
 
-        def backward_rest(store_now):
-            return (jnp.zeros_like(upstream), store_now)
-
-        down_grad, stores = lax.cond(active, backward_run, backward_rest, stores)
+        down_grad, stores = backward_run(stores)
         return (pass_backward(down_grad), stores)
 
     empty_stores = (
-        jnp.zeros((micro_count, per_group, length, model_width), jnp.bfloat16),
-        jnp.zeros((micro_count, per_group, length, joined_width), jnp.bfloat16),
-        jnp.zeros((micro_count, per_group, length, inner_width), jnp.bfloat16),
-        jnp.zeros((micro_count, per_group, length, model_width), jnp.bfloat16),
+        jnp.zeros((micro_count + 1, per_group, length, model_width), jnp.bfloat16),
+        jnp.zeros((micro_count + 1, per_group, length, joined_width), jnp.bfloat16),
+        jnp.zeros((micro_count + 1, per_group, length, inner_width), jnp.bfloat16),
+        jnp.zeros((micro_count + 1, per_group, length, model_width), jnp.bfloat16),
         jnp.zeros((model_width,), jnp.float32),
     )
     start_back = (jnp.zeros((per_group, length, model_width), jnp.bfloat16), empty_stores)
-    _, stores = lax.fori_loop(0, step_count, backward_step, start_back)
-    rows_normed = stores[0].reshape(-1, model_width)
-    rows_joined = stores[1].reshape(-1, joined_width)
-    rows_mixed = stores[2].reshape(-1, inner_width)
-    rows_upstream = stores[3].reshape(-1, model_width)
+    _, stores = repeat(step_count, backward_step, start_back)
+    rows_normed = stores[0][:micro_count].reshape(-1, model_width)
+    rows_joined = stores[1][:micro_count].reshape(-1, joined_width)
+    rows_mixed = stores[2][:micro_count].reshape(-1, inner_width)
+    rows_upstream = stores[3][:micro_count].reshape(-1, model_width)
     over_rows = (((0,), (0,)), ((), ()))
     gain_total = jnp.sum(lax.all_gather(stores[4], "dp", axis=0), axis=0)
     all_upstream = lax.all_gather(rows_upstream, "dp", axis=0, tiled=True)

time: 493 us -> 485 us (0.984); the launches traced: 492 us -> 479 us
  waiting for transfers between devices: 179 us -> 51.8 us
  matrix products: 98.3 us -> 183 us
  local copies, waits for them, and re-layouts: 30.3 us -> 79.9 us
  starting transfers between devices: 63.3 us -> 41.6 us
  other arithmetic: 15.4 us -> 30.6 us
  blocking collectives: 20.8 us -> 7.43 us
    ppermute x12 -> x10, waiting for transfers between devices: 160 us -> 37.1 us  [from_behind(): lax.ppermute(value, axis, [(source, source + steps) for source in range(i...]
    ppermute x12 -> x10, starting transfers between devices: 58.7 us -> 36.2 us  [from_behind(): lax.ppermute(value, axis, [(source, source + steps) for source in range(i...]
    dot_general x3 -> x6, matrix products: 21.7 us -> 43.8 us  [layer_backward(): lax.dot_general(grad_joined_rows.reshape(-1, grad_joined_rows.shape[2]),...]
    dot_general x3 -> x6, matrix products: 19.9 us -> 39.8 us  [layer_backward(): lax.dot_general(upstream.reshape(-1, model_width), w_out, (((1,), (1,)),...]
    concatenate x12 -> x24, local copies, waits for them, and re-layouts: 1.92 us -> 21.3 us  [layer_backward(): jnp.concatenate([grad_queries.reshape(batch_size, length, inner_width), g...]
    all_gather x1, blocking collectives: 20.8 us -> 7.43 us  [body(): gain_total = jnp.sum(lax.all_gather(stores[4], 'dp', axis=0), axis=0)]
    dot_general x3 -> x5, matrix products: 16.3 us -> 28 us  [layer_forward(): jnp.dot(mixed_heads.reshape(-1, mixed_heads.shape[2]), w_out, preferred_e...]
    another operation x25 -> x33, local copies, waits for them, and re-layouts: 6.99 us -> 17.5 us
  transfers between devices with their start and end apart: 20 -> 18, of which waited for: 14 -> 11; matrix products, arithmetic and copies ran while one was open for 2% -> 16% of each run, Pallas kernels for 0% -> 0%
where the time goes in v4:
time: 485 us; the launch traced here: 479 us
  matrix products  183 us (38%)
  local copies, waits for them, and re-layouts  79.9 us (16%)
  Pallas kernels  68 us (14%)
  waiting for transfers between devices  51.8 us (11%)
  starting transfers between devices  41.6 us (9%)
  other arithmetic  30.6 us (6%)
  between operations  16.4 us (3%)
  blocking collectives  7.43 us (2%)
    pallas_call x1, Pallas kernels, gather_weights(): pl.pallas_call(functools.partial(gather_kernel, chips, groups), out_shape...  68 us
    dot_general x6, matrix products, layer_backward(): lax.dot_general(grad_joined_rows.reshape(-1, grad_joined_rows.shape[2]),...  43.8 us
    dot_general x6, matrix products, layer_backward(): lax.dot_general(upstream.reshape(-1, model_width), w_out, (((1,), (1,)),...  39.8 us
    ppermute x10, waiting for transfers between devices, from_behind(): lax.ppermute(value, axis, [(source, source + steps) for source in range(i...  37.1 us
    ppermute x10, starting transfers between devices, from_behind(): lax.ppermute(value, axis, [(source, source + steps) for source in range(i...  36.2 us
    dot_general x5, matrix products, layer_forward(): jnp.dot(mixed_heads.reshape(-1, mixed_heads.shape[2]), w_out, preferred_e...  28 us
    concatenate x24, local copies, waits for them, and re-layouts, layer_backward(): jnp.concatenate([grad_queries.reshape(batch_size, length, inner_width), g...  21.3 us
    dot_general x6, matrix products, project(): jnp.dot(normed.reshape(-1, model_width), weight, preferred_element_type=j...  20.2 us
  transfers between devices with their start and end apart: 18, of which 11 were waited for; matrix products, arithmetic and copies ran while one was open for 16% of the time, Pallas kernels for 0%

profile of v4, /device:TPU:0, one launch (start us, length us, event | category | flops | bytes accessed | tf_op | source)
XLA Modules:
  0.0 478.7 jit_solution(6737052340361497330)
XLA Ops:
  12.9 68.0 %shard_map.88 = (bf16[3072,1664]{1,0:T(8,128)(2,1)S(1)}, bf16[1536,3072]{1,0:T(8,128)(2,1)S(1)}) custom-call(bf16[768,1664]{1,0:T(8,128)(2,1)S(1)} %bitcast.886, bf16[384,3072]{1,0:T(8,128)(2,1)S(1)} %bitcast.887), custom_call_target="tpu_custom_call" | custom-call | tf_op jit(solution)/shard_map/pallas_call | solution.py:266
  90.9 5.5 %fusion.10 = bf16[1,48,3072]{2,1,0:T(8,128)(2,1)S(1)} fusion(bf16[48,1536]{1,0:T(8,128)(2,1)S(1)} %reshape_reshape.19, bf16[1536,3072]{1,0:T(8,128)(2,1)} %copy-done.1, bf16[3,1,48,3072]{3,2,1,0:T(8,128)(2,1)S(1)} %bitcast.925, s32[]{:T(128)S(6)} %min.37, pred[]{:T(512)S(6)} %eq.10), kind=kOutput, calls=%fused_computation.18 | convolution fusion | flops 453574656 | bytes 10174469 | tf_op jit(solution)/shard_map/dot_general | solution.py:70
  100.6 6.6 %convolution_convert_fusion.11 = bf16[48,1536]{1,0:T(8,128)(2,1)S(1)} fusion(bf16[1536,3072]{1,0:T(8,128)(2,1)} %copy-done.1, bf16[3,1,48,3072]{3,2,1,0:T(8,128)(2,1)S(1)} %bitcast.910, s32[]{:T(128)S(6)} %min.43, pred[]{:T(512)S(6)} %eq.14), kind=kOutput, calls=%fused_computation.30 | convolution fusion | flops 453206016 | bytes 9879557 | tf_op jit(solution)/shard_map/dot_general | solution.py:82
  109.7 6.5 %bitcast_dynamic-update-slice_fusion.17 = (bf16[4,1,48,1664]{3,2,1,0:T(8,128)(2,1)}, bf16[48,1664]{1,0:T(8,128)(2,1)S(1)}) fusion(bf16[4,1,48,1664]{3,2,1,0:T(8,128)(2,1)} %get-tuple-element.84, s32[]{:T(128)S(6)} %select_n.360, bf16[3072,1664]{1,0:T(8,128)(2,1)} %copy-done, bf16[1,48,3072]{2,1,0:T(8,128)(2,1)S(1)} %get-tuple-element.40, ...), kind=kOutput, calls=%fused_computation.408 | convolution fusion | flops 491403264 | bytes 10850500 | tf_op jit(solution)/shard_map/dot_general | solution.py:40
  119.4 5.6 %fusion.5 = bf16[1,48,3072]{2,1,0:T(8,128)(2,1)S(1)} fusion(bf16[48,1536]{1,0:T(8,128)(2,1)S(1)} %reshape_reshape.20, bf16[1536,3072]{1,0:T(8,128)(2,1)} %copy-done.1, bf16[1,48,3072]{2,1,0:T(8,128)(2,1)S(1)} %get-tuple-element.40), kind=kOutput, calls=%fused_computation.13 | convolution fusion | flops 453427200 | bytes 10174464 | tf_op jit(solution)/shard_map/dot_general | solution.py:70
  128.7 6.2 %collective-permute-done.1 = bf16[1,48,3072]{2,1,0:T(8,128)(2,1)S(1)} collective-permute-done((bf16[1,48,3072]{2,1,0:T(8,128)(2,1)S(1)}, bf16[1,48,3072]{2,1,0:T(8,128)(2,1)S(1)}, u32[]{:S(2)}, u32[]{:S(2)}) %collective-permute-start.1) | collective-permute-done | bytes 294944 | tf_op jit(solution)/shard_map/ppermute | solution.py:21
  141.8 5.6 %fusion.6 = bf16[1,48,3072]{2,1,0:T(8,128)(2,1)S(1)} fusion(bf16[48,1536]{1,0:T(8,128)(2,1)S(1)} %reshape_reshape.21, bf16[1536,3072]{1,0:T(8,128)(2,1)} %copy-done.1, bf16[1,48,3072]{2,1,0:T(8,128)(2,1)S(1)} %get-tuple-element.38), kind=kOutput, calls=%fused_computation.14 | convolution fusion | flops 453427200 | bytes 10174464 | tf_op jit(solution)/shard_map/dot_general | solution.py:70
  147.5 4.4 collective-permute-start.2
  151.9 5.6 %collective-permute-done.2 = bf16[1,48,3072]{2,1,0:T(8,128)(2,1)S(1)} collective-permute-done((bf16[1,48,3072]{2,1,0:T(8,128)(2,1)S(1)}, bf16[1,48,3072]{2,1,0:T(8,128)(2,1)S(1)}, u32[]{:S(2)}, u32[]{:S(2)}) %collective-permute-start.2) | collective-permute-done | bytes 294944 | tf_op jit(solution)/shard_map/ppermute | solution.py:21
  164.5 5.6 %fusion.7 = bf16[1,48,3072]{2,1,0:T(8,128)(2,1)S(1)} fusion(bf16[48,1536]{1,0:T(8,128)(2,1)S(1)} %reshape_reshape.22, bf16[1536,3072]{1,0:T(8,128)(2,1)} %copy-done.1, bf16[1,48,3072]{2,1,0:T(8,128)(2,1)S(1)} %get-tuple-element.36), kind=kOutput, calls=%fused_computation.15 | convolution fusion | flops 453427200 | bytes 10174464 | tf_op jit(solution)/shard_map/dot_general | solution.py:70
  170.2 4.4 collective-permute-start.3
  174.6 4.7 collective-permute-done.3
  186.3 5.6 %fusion.8 = bf16[1,48,3072]{2,1,0:T(8,128)(2,1)S(1)} fusion(bf16[48,1536]{1,0:T(8,128)(2,1)S(1)} %reshape_reshape.23, bf16[1536,3072]{1,0:T(8,128)(2,1)} %copy-done.1, bf16[1,48,3072]{2,1,0:T(8,128)(2,1)S(1)} %get-tuple-element.34), kind=kOutput, calls=%fused_computation.16 | convolution fusion | flops 453427200 | bytes 10174464 | tf_op jit(solution)/shard_map/dot_general | solution.py:70
  191.9 12.6 %collective-permute-start.4 = (bf16[1,48,3072]{2,1,0:T(8,128)(2,1)S(1)}, bf16[1,48,3072]{2,1,0:T(8,128)(2,1)S(1)}, u32[]{:S(2)}, u32[]{:S(2)}) collective-permute-start(bf16[1,48,3072]{2,1,0:T(8,128)(2,1)S(1)} %fusion.8), channel_id=1, source_target_pairs={{0,4},{4,8},{8,12},{1,5},{5,9},{9,13},{2,6},{6,10},{10,14},{3,7},{... | collective-permute-start | bytes 884744 | tf_op jit(solution)/shard_map/ppermute | solution.py:21
  220.1 7.4 %fusion.105 = (f32[3072]{0:T(1024)S(1)}, f32[48]{0:T(128)S(1)}, f32[48,3072]{1,0:T(8,128)S(1)}) fusion(f32[48]{0:T(128)S(1)} %get-tuple-element.73, bf16[4,1,48,3072]{3,2,1,0:T(8,128)(2,1)S(1)} %bitcast_dynamic-update-slice_fusion.5, s32[]{:T(128)S(6)} %min.43, f32[3072]{0:T(1024)S(1)} %bitcast.894, bf16[48,1664]{1,0:T(8,128)(2,1)} %concatenate.155, ...), kind=kOutput, calls=%fused_computation.201 | convolution fusion | flops 491762624 | bytes 11293060 | tf_op jit(solution)/shard_map/dot_general | solution.py:106
  253.7 6.6 %convolution_convert_fusion.10 = bf16[48,1536]{1,0:T(8,128)(2,1)S(1)} fusion(bf16[1536,3072]{1,0:T(8,128)(2,1)} %copy-done.1, bf16[1,48,3072]{2,1,0:T(8,128)(2,1)S(1)} %get-tuple-element.30), kind=kOutput, calls=%fused_computation.29 | convolution fusion | flops 453058560 | bytes 9879552 | tf_op jit(solution)/shard_map/dot_general | solution.py:82
  268.2 7.2 %fusion.116 = (f32[3072]{0:T(1024)S(1)}, f32[48]{0:T(128)S(1)}, f32[48,3072]{1,0:T(8,128)S(1)}) fusion(f32[48]{0:T(128)} %get-tuple-element.71, bf16[4,1,48,3072]{3,2,1,0:T(8,128)(2,1)S(1)} %bitcast_dynamic-update-slice_fusion.5, s32[]{:T(128)S(6)} %min.44, f32[3072]{0:T(1024)S(1)} %bitcast.896, bf16[48,1664]{1,0:T(8,128)(2,1)} %concatenate.161, ...), kind=kOutput, calls=%fused_computation.212 | convolution fusion | flops 491762624 | bytes 11293060 | tf_op jit(solution)/shard_map/dot_general | solution.py:106
  281.3 5.7 %collective-permute-done.9 = bf16[1,48,3072]{2,1,0:T(8,128)(2,1)} collective-permute-done((bf16[1,48,3072]{2,1,0:T(8,128)(2,1)}, bf16[1,48,3072]{2,1,0:T(8,128)(2,1)}, u32[]{:S(2)}, u32[]{:S(2)}) %collective-permute-start.9) | collective-permute-done | bytes 294944 | tf_op jit(solution)/shard_map/ppermute | solution.py:21
  288.8 6.6 %convolution_convert_fusion.9 = bf16[48,1536]{1,0:T(8,128)(2,1)S(1)} fusion(bf16[1536,3072]{1,0:T(8,128)(2,1)} %copy-done.1, bf16[1,48,3072]{2,1,0:T(8,128)(2,1)S(1)} %get-tuple-element.28), kind=kOutput, calls=%fused_computation.28 | convolution fusion | flops 453058560 | bytes 9879552 | tf_op jit(solution)/shard_map/dot_general | solution.py:82
  303.3 7.3 %fusion.127 = (f32[3072]{0:T(1024)S(1)}, f32[48]{0:T(128)S(1)}, f32[48,3072]{1,0:T(8,128)S(1)}) fusion(f32[48]{0:T(128)} %get-tuple-element.69, bf16[4,1,48,3072]{3,2,1,0:T(8,128)(2,1)S(1)} %bitcast_dynamic-update-slice_fusion.5, s32[]{:T(128)S(6)} %min.45, f32[3072]{0:T(1024)S(1)} %bitcast.898, bf16[48,1664]{1,0:T(8,128)(2,1)} %concatenate.167, ...), kind=kOutput, calls=%fused_computation.223 | convolution fusion | flops 491762624 | bytes 11293060 | tf_op jit(solution)/shard_map/dot_general | solution.py:106
  322.7 6.6 %convolution_convert_fusion.8 = bf16[48,1536]{1,0:T(8,128)(2,1)S(1)} fusion(bf16[1536,3072]{1,0:T(8,128)(2,1)} %copy-done.1, bf16[1,48,3072]{2,1,0:T(8,128)(2,1)S(1)} %get-tuple-element.26), kind=kOutput, calls=%fused_computation.27 | convolution fusion | flops 453058560 | bytes 9879552 | tf_op jit(solution)/shard_map/dot_general | solution.py:82
  336.0 7.7 %fusion.138 = (f32[3072]{0:T(1024)}, f32[48]{0:T(128)S(1)}, f32[48,3072]{1,0:T(8,128)S(1)}) fusion(f32[48]{0:T(128)} %get-tuple-element.67, bf16[4,1,48,3072]{3,2,1,0:T(8,128)(2,1)S(1)} %bitcast_dynamic-update-slice_fusion.5, s32[]{:T(128)S(6)} %min.46, f32[3072]{0:T(1024)S(1)} %bitcast.900, bf16[48,1664]{1,0:T(8,128)(2,1)} %concatenate.173, ...), kind=kOutput, calls=%fused_computation.234 | convolution fusion | flops 491762624 | bytes 11293060 | tf_op jit(solution)/shard_map/dot_general | solution.py:106
  355.4 6.6 %convolution_convert_fusion.7 = bf16[48,1536]{1,0:T(8,128)(2,1)S(1)} fusion(bf16[1536,3072]{1,0:T(8,128)(2,1)} %copy-done.1, bf16[1,48,3072]{2,1,0:T(8,128)(2,1)S(1)} %get-tuple-element.24), kind=kOutput, calls=%fused_computation.26 | convolution fusion | flops 453058560 | bytes 9879552 | tf_op jit(solution)/shard_map/dot_general | solution.py:82
  369.8 7.2 %fusion.149 = (f32[3072]{0:T(1024)S(1)}, f32[48]{0:T(128)S(1)}, f32[48,3072]{1,0:T(8,128)S(1)}) fusion(f32[48]{0:T(128)} %get-tuple-element.65, bf16[4,1,48,3072]{3,2,1,0:T(8,128)(2,1)S(1)} %bitcast_dynamic-update-slice_fusion.5, s32[]{:T(128)S(6)} %min.47, f32[3072]{0:T(1024)S(1)} %bitcast.902, bf16[48,1664]{1,0:T(8,128)(2,1)} %concatenate.179, ...), kind=kOutput, calls=%fused_computation.245 | convolution fusion | flops 491762624 | bytes 11293060 | tf_op jit(solution)/shard_map/dot_general | solution.py:106
  382.5 4.3 collective-permute-done.12
  386.8 6.7 %convolution_convert_fusion.6 = bf16[48,1536]{1,0:T(8,128)(2,1)S(1)} fusion(bf16[1536,3072]{1,0:T(8,128)(2,1)} %copy-done.1, bf16[1,48,3072]{2,1,0:T(8,128)(2,1)S(1)} %collective-permute-done.12, bf16[3,1,48,3072]{3,2,1,0:T(8,128)(2,1)S(1)} %bitcast.917, s32[]{:T(128)S(6)} %min.48, pred[]{:T(512)S(6)} %eq.14), kind=kOutput, calls=%fused_computation.25 | convolution fusion | flops 453206016 | bytes 10174469 | tf_op jit(solution)/shard_map/dot_general | solution.py:82
  426.8 5.1 %collective-permute-done.5 = bf16[144,768]{1,0:T(8,128)(2,1)S(1)} collective-permute-done((bf16[144,768]{1,0:T(8,128)(2,1)S(1)}, bf16[144,768]{1,0:T(8,128)(2,1)S(1)}, u32[]{:S(2)}, u32[]{:S(2)}) %collective-permute-start.5) | collective-permute-done | bytes 221216 | tf_op jit(solution)/shard_map/ppermute | solution.py:295
  435.7 7.0 %fusion.35 = f32[3072]{0:T(1024)S(1)} fusion(bf16[48,1664]{1,0:T(8,128)(2,1)S(1)} %concatenate.185, bf16[3072,1664]{1,0:T(8,128)(2,1)} %copy-done, f32[48]{0:T(128)S(1)} %copy-done.76, bf16[4,1,48,3072]{3,2,1,0:T(8,128)(2,1)S(1)} %bitcast_dynamic-update-slice_fusion.5, s32[]{:T(128)S(6)} %min.48), kind=kOutput, calls=%fused_computation.89 | convolution fusion | flops 491320320 | bytes 10690756 | tf_op jit(solution)/shard_map/dot_general | solution.py:106
  442.8 7.4 %all-gather = f32[12288]{0:T(1024)S(1)} all-gather(f32[3072]{0:T(1024)S(1)} %add_add_fusion), channel_id=2, replica_groups=mesh['groups'=2,'section'=4,'dp'=4] {'dp'}, dimensions={0}, use_global_device_ids=true | all-gather | bytes 61440 | tf_op jit(solution)/shard_map/all_gather | solution.py:390
  450.9 6.4 %convolution_bitcast_fusion.1 = f32[1,768,1664]{2,1,0:T(8,128)} fusion(bf16[576,768]{1,0:T(8,128)(2,1)} %bitcast.85, bf16[576,1664]{1,0:T(8,128)(2,1)} %all-gather.4.cloned.1.call-done), kind=kOutput, calls=%fused_computation.1 | convolution fusion | flops 1472200704 | bytes 7913472 | tf_op jit(solution)/shard_map/dot_general | solution.py:396
  457.3 8.1 %all-gather.6.cloned.1.call-done = bf16[576,3072]{1,0:T(8,128)(2,1)} async-done(((bf16[144,3072]{1,0:T(8,128)(2,1)}), bf16[576,3072]{1,0:T(8,128)(2,1)}) %all-gather.6.cloned.1.call-update) | async-done | bytes 3538960 | tf_op jit(solution)/shard_map/all_gather | solution.py:391
  465.5 6.2 %convolution_bitcast_fusion = f32[1,384,3072]{2,1,0:T(8,128)} fusion(bf16[576,384]{1,0:T(8,128)(2,1)S(1)} %bitcast.931, bf16[576,3072]{1,0:T(8,128)(2,1)} %all-gather.6.cloned.1.call-done), kind=kOutput, calls=%fused_computation | convolution fusion | flops 1358954496 | bytes 8699904 | tf_op jit(solution)/shard_map/dot_general | solution.py:393
  (456 shorter events, 194.9 us)
Async XLA Ops:
  7.2 443.7 %all-gather.4.cloned.1.call-start = ((), (), s32[]{:S(2)}) async-start(), calls=%async_computation | async-start | bytes 2396160 | tf_op jit(solution)/shard_map/all_gather | solution.py:392
  12.9 72.6 %copy-start.4 = (f32[1,3072]{1,0:T(1,128)S(1)}, f32[1,3072]{1,0:T(1,128)}, u32[]{:S(2)}) copy-start(f32[1,3072]{1,0:T(1,128)} %param.9) | copy-start | bytes 36868
  12.9 72.6 %copy-start.7 = (bf16[144,3072]{1,0:T(8,128)(2,1)S(1)}, bf16[144,3072]{1,0:T(8,128)(2,1)}, u32[]{:S(2)}) copy-start(bf16[144,3072]{1,0:T(8,128)(2,1)} %param.6) | copy-start | bytes 2654212
  96.4 12.3 %collective-permute-start = (bf16[1,48,3072]{2,1,0:T(8,128)(2,1)S(1)}, bf16[1,48,3072]{2,1,0:T(8,128)(2,1)}, u32[]{:S(2)}, u32[]{:S(2)}) collective-permute-start(bf16[1,48,3072]{2,1,0:T(8,128)(2,1)S(1)} %fusion.10), channel_id=1, source_target_pairs={{0,4},{4,8},{8,12},{1,5},{5,9},{9,13},{2,6},{6,10},{10,14},{3,7},{... | collective-permute-start | bytes 884744 | tf_op jit(solution)/shard_map/ppermute | solution.py:21
  117.3 18.7 %slice-start = ((s8[10223616]{0:T(1024)(128)(4,1)}), s8[1835008]{0:T(1024)(128)(4,1)S(1)}, s32[]{:S(2)}) async-start(s8[10223616]{0:T(1024)(128)(4,1)} %bitcast.878), calls=%async_computation.2 | async-start | bytes 3670016
  119.3 16.7 %slice-start.1 = ((s8[10223616]{0:T(1024)(128)(4,1)}), s8[4194304]{0:T(1024)(128)(4,1)S(1)}, s32[]{:S(2)}) async-start(s8[10223616]{0:T(1024)(128)(4,1)} %bitcast.878), calls=%async_computation.3 | async-start | bytes 8388608
  119.4 16.7 %slice-start.2 = ((s8[10223616]{0:T(1024)(128)(4,1)}), s8[4194304]{0:T(1024)(128)(4,1)S(1)}, s32[]{:S(2)}) async-start(s8[10223616]{0:T(1024)(128)(4,1)} %bitcast.878), calls=%async_computation.4 | async-start | bytes 8388608
  125.0 9.8 %collective-permute-start.1 = (bf16[1,48,3072]{2,1,0:T(8,128)(2,1)S(1)}, bf16[1,48,3072]{2,1,0:T(8,128)(2,1)S(1)}, u32[]{:S(2)}, u32[]{:S(2)}) collective-permute-start(bf16[1,48,3072]{2,1,0:T(8,128)(2,1)S(1)} %fusion.5), channel_id=1, source_target_pairs={{0,4},{4,8},{8,12},{1,5},{5,9},{9,13},{2,6},{6,10},{10,14},{3,7},{... | collective-permute-start | bytes 884744 | tf_op jit(solution)/shard_map/ppermute | solution.py:21
  139.5 19.2 %slice-start.3 = ((s8[10223616]{0:T(1024)(128)(4,1)}), s8[1835008]{0:T(1024)(128)(4,1)S(1)}, s32[]{:S(2)}) async-start(s8[10223616]{0:T(1024)(128)(4,1)} %bitcast.880), calls=%async_computation.5 | async-start | bytes 3670016
  141.8 16.9 %slice-start.4 = ((s8[10223616]{0:T(1024)(128)(4,1)}), s8[4194304]{0:T(1024)(128)(4,1)S(1)}, s32[]{:S(2)}) async-start(s8[10223616]{0:T(1024)(128)(4,1)} %bitcast.880), calls=%async_computation.6 | async-start | bytes 8388608
  141.8 16.9 %slice-start.5 = ((s8[10223616]{0:T(1024)(128)(4,1)}), s8[4194304]{0:T(1024)(128)(4,1)S(1)}, s32[]{:S(2)}) async-start(s8[10223616]{0:T(1024)(128)(4,1)} %bitcast.880), calls=%async_computation.7 | async-start | bytes 8388608
  147.5 10.0 %collective-permute-start.2 = (bf16[1,48,3072]{2,1,0:T(8,128)(2,1)S(1)}, bf16[1,48,3072]{2,1,0:T(8,128)(2,1)S(1)}, u32[]{:S(2)}, u32[]{:S(2)}) collective-permute-start(bf16[1,48,3072]{2,1,0:T(8,128)(2,1)S(1)} %fusion.6), channel_id=1, source_target_pairs={{0,4},{4,8},{8,12},{1,5},{5,9},{9,13},{2,6},{6,10},{10,14},{3,7},{... | collective-permute-start | bytes 884744 | tf_op jit(solution)/shard_map/ppermute | solution.py:21
  162.2 18.3 %slice-start.6 = ((s8[10223616]{0:T(1024)(128)(4,1)}), s8[1835008]{0:T(1024)(128)(4,1)S(1)}, s32[]{:S(2)}) async-start(s8[10223616]{0:T(1024)(128)(4,1)} %bitcast.882), calls=%async_computation.8 | async-start | bytes 3670016
  170.2 9.1 %collective-permute-start.3 = (bf16[1,48,3072]{2,1,0:T(8,128)(2,1)S(1)}, bf16[1,48,3072]{2,1,0:T(8,128)(2,1)S(1)}, u32[]{:S(2)}, u32[]{:S(2)}) collective-permute-start(bf16[1,48,3072]{2,1,0:T(8,128)(2,1)S(1)} %fusion.7), channel_id=1, source_target_pairs={{0,4},{4,8},{8,12},{1,5},{5,9},{9,13},{2,6},{6,10},{10,14},{3,7},{... | collective-permute-start | bytes 884744 | tf_op jit(solution)/shard_map/ppermute | solution.py:21
  183.9 26.0 %slice-start.9 = ((s8[10223616]{0:T(1024)(128)(4,1)}), s8[1835008]{0:T(1024)(128)(4,1)S(1)}, s32[]{:S(2)}) async-start(s8[10223616]{0:T(1024)(128)(4,1)} %bitcast.884), calls=%async_computation.11 | async-start | bytes 3670016
  186.2 23.7 %slice-start.10 = ((s8[10223616]{0:T(1024)(128)(4,1)}), s8[4194304]{0:T(1024)(128)(4,1)S(1)}, s32[]{:S(2)}) async-start(s8[10223616]{0:T(1024)(128)(4,1)} %bitcast.884), calls=%async_computation.12 | async-start | bytes 8388608
  186.3 23.7 %slice-start.11 = ((s8[10223616]{0:T(1024)(128)(4,1)}), s8[4194304]{0:T(1024)(128)(4,1)S(1)}, s32[]{:S(2)}) async-start(s8[10223616]{0:T(1024)(128)(4,1)} %bitcast.884), calls=%async_computation.13 | async-start | bytes 8388608
  191.9 16.8 %collective-permute-start.4 = (bf16[1,48,3072]{2,1,0:T(8,128)(2,1)S(1)}, bf16[1,48,3072]{2,1,0:T(8,128)(2,1)S(1)}, u32[]{:S(2)}, u32[]{:S(2)}) collective-permute-start(bf16[1,48,3072]{2,1,0:T(8,128)(2,1)S(1)} %fusion.8), channel_id=1, source_target_pairs={{0,4},{4,8},{8,12},{1,5},{5,9},{9,13},{2,6},{6,10},{10,14},{3,7},{... | collective-permute-start | bytes 884744 | tf_op jit(solution)/shard_map/ppermute | solution.py:21
  214.7 18.7 %copy-start.39 = (bf16[1,48,1664]{2,1,0:T(8,128)(2,1)}, bf16[1,48,1664]{2,1,0:T(8,128)(2,1)S(1)}, u32[]{:S(2)}) copy-start(bf16[1,48,1664]{2,1,0:T(8,128)(2,1)S(1)} %get-tuple-element.45) | copy-start | bytes 479236
  214.7 19.5 %copy-start.38 = (bf16[1,48,1664]{2,1,0:T(8,128)(2,1)}, bf16[1,48,1664]{2,1,0:T(8,128)(2,1)S(1)}, u32[]{:S(2)}) copy-start(bf16[1,48,1664]{2,1,0:T(8,128)(2,1)S(1)} %get-tuple-element.44) | copy-start | bytes 479236
  228.5 23.5 %collective-permute-start.8 = (bf16[1,48,3072]{2,1,0:T(8,128)(2,1)}, bf16[1,48,3072]{2,1,0:T(8,128)(2,1)}, u32[]{:S(2)}, u32[]{:S(2)}) collective-permute-start(bf16[1,48,3072]{2,1,0:T(8,128)(2,1)} %fusion.185), channel_id=1, source_target_pairs={{4,0},{8,4},{12,8},{5,1},{9,5},{13,9},{6,2},{10,6},{14,10},{7,3},{... | collective-permute-start | bytes 884744 | tf_op jit(solution)/shard_map/ppermute | solution.py:21
  276.4 10.7 %collective-permute-start.9 = (bf16[1,48,3072]{2,1,0:T(8,128)(2,1)}, bf16[1,48,3072]{2,1,0:T(8,128)(2,1)}, u32[]{:S(2)}, u32[]{:S(2)}) collective-permute-start(bf16[1,48,3072]{2,1,0:T(8,128)(2,1)} %fusion.113), channel_id=1, source_target_pairs={{4,0},{8,4},{12,8},{5,1},{9,5},{13,9},{6,2},{10,6},{14,10},{7,3},{... | collective-permute-start | bytes 884744 | tf_op jit(solution)/shard_map/ppermute | solution.py:21
  311.6 9.4 %collective-permute-start.10 = (bf16[1,48,3072]{2,1,0:T(8,128)(2,1)}, bf16[1,48,3072]{2,1,0:T(8,128)(2,1)}, u32[]{:S(2)}, u32[]{:S(2)}) collective-permute-start(bf16[1,48,3072]{2,1,0:T(8,128)(2,1)} %fusion.124), channel_id=1, source_target_pairs={{4,0},{8,4},{12,8},{5,1},{9,5},{13,9},{6,2},{10,6},{14,10},{7,3},{... | collective-permute-start | bytes 884744 | tf_op jit(solution)/shard_map/ppermute | solution.py:21
  344.7 8.9 %collective-permute-start.11 = (bf16[1,48,3072]{2,1,0:T(8,128)(2,1)}, bf16[1,48,3072]{2,1,0:T(8,128)(2,1)}, u32[]{:S(2)}, u32[]{:S(2)}) collective-permute-start(bf16[1,48,3072]{2,1,0:T(8,128)(2,1)} %fusion.135), channel_id=1, source_target_pairs={{4,0},{8,4},{12,8},{5,1},{9,5},{13,9},{6,2},{10,6},{14,10},{7,3},{... | collective-permute-start | bytes 884744 | tf_op jit(solution)/shard_map/ppermute | solution.py:21
  378.0 8.8 %collective-permute-start.12 = (bf16[1,48,3072]{2,1,0:T(8,128)(2,1)}, bf16[1,48,3072]{2,1,0:T(8,128)(2,1)S(1)}, u32[]{:S(2)}, u32[]{:S(2)}) collective-permute-start(bf16[1,48,3072]{2,1,0:T(8,128)(2,1)} %fusion.146), channel_id=1, source_target_pairs={{4,0},{8,4},{12,8},{5,1},{9,5},{13,9},{6,2},{10,6},{14,10},{7,3},{... | collective-permute-start | bytes 884744 | tf_op jit(solution)/shard_map/ppermute | solution.py:21
  403.1 62.4 %all-gather.6.cloned.1.call-start = ((), (), s32[]{:S(2)}) async-start(), calls=%async_computation.1 | async-start | bytes 4423680 | tf_op jit(solution)/shard_map/all_gather | solution.py:391
  410.9 14.3 %collective-permute-start.13 = (bf16[144,384]{1,0:T(8,128)(2,1)}, bf16[144,384]{1,0:T(8,128)(2,1)S(1)}, u32[]{:S(2)}, u32[]{:S(2)}) collective-permute-start(bf16[144,384]{1,0:T(8,128)(2,1)} %get-tuple-element.52), channel_id=1, source_target_pairs={{0,1},{1,2},{2,3},{3,0},{4,5},{5,6},{6,7},{7,4},{8,9},{9,10},{10,1... | collective-permute-start | bytes 331784 | tf_op jit(solution)/shard_map/ppermute | solution.py:295
  410.9 15.7 %collective-permute-start.14 = (bf16[144,384]{1,0:T(8,128)(2,1)}, bf16[144,384]{1,0:T(8,128)(2,1)S(1)}, u32[]{:S(2)}, u32[]{:S(2)}) collective-permute-start(bf16[144,384]{1,0:T(8,128)(2,1)} %get-tuple-element.51), channel_id=1, source_target_pairs={{0,2},{1,3},{2,0},{3,1},{4,6},{5,7},{6,4},{7,5},{8,10},{9,11},{10,... | collective-permute-start | bytes 331784 | tf_op jit(solution)/shard_map/ppermute | solution.py:295
  411.6 15.1 %collective-permute-start.15 = (bf16[144,384]{1,0:T(8,128)(2,1)}, bf16[144,384]{1,0:T(8,128)(2,1)S(1)}, u32[]{:S(2)}, u32[]{:S(2)}) collective-permute-start(bf16[144,384]{1,0:T(8,128)(2,1)} %get-tuple-element.50), channel_id=1, source_target_pairs={{0,3},{1,0},{2,1},{3,2},{4,7},{5,4},{6,5},{7,6},{8,11},{9,8},{10,9... | collective-permute-start | bytes 331784 | tf_op jit(solution)/shard_map/ppermute | solution.py:295
  421.9 10.0 %collective-permute-start.5 = (bf16[144,768]{1,0:T(8,128)(2,1)S(1)}, bf16[144,768]{1,0:T(8,128)(2,1)S(1)}, u32[]{:S(2)}, u32[]{:S(2)}) collective-permute-start(bf16[144,768]{1,0:T(8,128)(2,1)S(1)} %get-tuple-element.43), channel_id=1, source_target_pairs={{0,1},{1,2},{2,3},{3,0},{4,5},{5,6},{6,7},{7,4},{8,9},{9,10},{10,1... | collective-permute-start | bytes 663560 | tf_op jit(solution)/shard_map/ppermute | solution.py:295
  422.0 10.6 %collective-permute-start.6 = (bf16[144,768]{1,0:T(8,128)(2,1)S(1)}, bf16[144,768]{1,0:T(8,128)(2,1)S(1)}, u32[]{:S(2)}, u32[]{:S(2)}) collective-permute-start(bf16[144,768]{1,0:T(8,128)(2,1)S(1)} %get-tuple-element.42), channel_id=1, source_target_pairs={{0,2},{1,3},{2,0},{3,1},{4,6},{5,7},{6,4},{7,5},{8,10},{9,11},{10,... | collective-permute-start | bytes 663560 | tf_op jit(solution)/shard_map/ppermute | solution.py:295
  425.2 9.5 %collective-permute-start.7 = (bf16[144,768]{1,0:T(8,128)(2,1)S(1)}, bf16[144,768]{1,0:T(8,128)(2,1)S(1)}, u32[]{:S(2)}, u32[]{:S(2)}) collective-permute-start(bf16[144,768]{1,0:T(8,128)(2,1)S(1)} %get-tuple-element.41), channel_id=1, source_target_pairs={{0,3},{1,0},{2,1},{3,2},{4,7},{5,4},{6,5},{7,6},{8,11},{9,8},{10,9... | collective-permute-start | bytes 663560 | tf_op jit(solution)/shard_map/ppermute | solution.py:295
  (79 other events, 446.3 us)
Sparse Core Ops, SparseCore 0:
  403.2 28.0 all-gather.3
  432.9 32.5 all-gather.5

commit v5 on v3

--- a/solution.py
+++ b/solution.py
@@ -298,6 +298,12 @@
     return taken.reshape(n * count, width)
 
 
+def repeat(count, step, state):
+    for now in range(count):
+        state = step(now, state)
+    return state
+
+
 def body(stream_in, out_grad, mask_blocks, norm_gain, w_joined, w_out):
     full_joined, full_out = gather_weights(w_joined, w_out)
     gain_row = norm_gain[0]
@@ -313,37 +319,33 @@
     upstreams = out_grad.reshape(micro_count, per_group, length, model_width)
     allowed = allowed_tokens(mask_blocks, BLOCK_LEN).reshape(micro_count, per_group, length, length)
     step_count = micro_count + sections - 1
-    keep_shape = (micro_count, per_group, length, joined_width)
+    keep_shape = (micro_count + 1, per_group, length, joined_width)
 
     def forward_step(step_now, state_now):
         incoming, kept_inputs, kept_joined = state_now
         slot_index = step_now - section_index
         active = jnp.logical_and(slot_index >= 0, slot_index < micro_count)
         group_index = jnp.clip(slot_index, 0, micro_count - 1)
+        place = jnp.where(active, group_index, micro_count)
         source = jnp.where(section_index == 0, inputs[group_index], incoming)
 
         def forward_run(kept_pair):
             result, joined_rows = layer_forward(
                 source, gain_row, full_joined, full_out, allowed[group_index]
             )
-            new_inputs = lax.dynamic_update_index_in_dim(kept_pair[0], source, group_index, 0)
-            new_joined = lax.dynamic_update_index_in_dim(kept_pair[1], joined_rows, group_index, 0)
+            new_inputs = lax.dynamic_update_index_in_dim(kept_pair[0], source, place, 0)
+            new_joined = lax.dynamic_update_index_in_dim(kept_pair[1], joined_rows, place, 0)
             return (result, new_inputs, new_joined)
 
-        def forward_rest(kept_pair):
-            return (jnp.zeros_like(source), kept_pair[0], kept_pair[1])
-
-        result, kept_inputs, kept_joined = lax.cond(
-            active, forward_run, forward_rest, (kept_inputs, kept_joined)
-        )
+        result, kept_inputs, kept_joined = forward_run((kept_inputs, kept_joined))
         return (pass_forward(result), kept_inputs, kept_joined)
 
     start_state = (
         jnp.zeros((per_group, length, model_width), jnp.bfloat16),
-        jnp.zeros((micro_count, per_group, length, model_width), jnp.bfloat16),
+        jnp.zeros((micro_count + 1, per_group, length, model_width), jnp.bfloat16),
         jnp.zeros(keep_shape, jnp.bfloat16),
     )
-    _, kept_inputs, kept_joined = lax.fori_loop(0, step_count, forward_step, start_state)
+    _, kept_inputs, kept_joined = repeat(step_count, forward_step, start_state)
 
     def backward_step(step_now, state_now):
         incoming, stores = state_now

time: 493 us -> 461 us (0.935)
  starting transfers between devices: 63.3 us -> 33.6 us
  waiting for transfers between devices: 179 us -> 156 us
  matrix products: 98.3 us -> 112 us
  local copies, waits for them, and re-layouts: 30.3 us -> 37.3 us
    ppermute x12 -> x11, starting transfers between devices: 58.7 us -> 29.1 us  [from_behind(): lax.ppermute(value, axis, [(source, source + steps) for source in range(i...]
    ppermute x12 -> x11, waiting for transfers between devices: 160 us -> 136 us  [from_behind(): lax.ppermute(value, axis, [(source, source + steps) for source in range(i...]
    dot_general x3 -> x5, matrix products: 16.3 us -> 27.8 us  [layer_forward(): jnp.dot(mixed_heads.reshape(-1, mixed_heads.shape[2]), w_out, preferred_e...]
    reduce_sum x6 -> x9, other arithmetic: 1.03 us -> 6.64 us  [normalize(): jnp.mean(stream_wide * stream_wide, axis=-1, keepdims=True) + EPSILON]
    dot_general x3 -> x6, matrix products: 19.6 us -> 20.6 us  [project(): jnp.dot(normed.reshape(-1, model_width), weight, preferred_element_type=j...]
  transfers between devices with their start and end apart: 20 -> 19, of which waited for: 14 -> 13; matrix products, arithmetic and copies ran while one was open for 2% -> 3% of each run, Pallas kernels for 0% -> 0%
where the time goes in v5:
time: 461 us; the launch traced here: 460 us
  waiting for transfers between devices  156 us (34%)
  matrix products  112 us (24%)
  Pallas kernels  68.5 us (15%)
  local copies, waits for them, and re-layouts  37.3 us (8%)
  starting transfers between devices  33.6 us (7%)
  blocking collectives  20.8 us (5%)
  other arithmetic  15.6 us (3%)
  between operations  15 us (3%)
    ppermute x11, waiting for transfers between devices, from_behind(): lax.ppermute(value, axis, [(source, source + steps) for source in range(i...  136 us
    pallas_call x1, Pallas kernels, gather_weights(): pl.pallas_call(functools.partial(gather_kernel, chips, groups), out_shape...  68.5 us
    ppermute x11, starting transfers between devices, from_behind(): lax.ppermute(value, axis, [(source, source + steps) for source in range(i...  29.1 us
    dot_general x5, matrix products, layer_forward(): jnp.dot(mixed_heads.reshape(-1, mixed_heads.shape[2]), w_out, preferred_e...  27.8 us
    dot_general x3, matrix products, layer_backward(): lax.dot_general(grad_joined_rows.reshape(-1, grad_joined_rows.shape[2]),...  21.5 us
    all_gather x1, blocking collectives, body(): gain_total = jnp.sum(lax.all_gather(stores[4], 'dp', axis=0), axis=0)  20.8 us
    dot_general x6, matrix products, project(): jnp.dot(normed.reshape(-1, model_width), weight, preferred_element_type=j...  20.6 us
    dot_general x3, matrix products, layer_backward(): lax.dot_general(upstream.reshape(-1, model_width), w_out, (((1,), (1,)),...  19.8 us
  transfers between devices with their start and end apart: 19, of which 13 were waited for; matrix products, arithmetic and copies ran while one was open for 3% of the time, Pallas kernels for 0%

profile of v5, /device:TPU:0, one launch (start us, length us, event | category | flops | bytes accessed | tf_op | source)
XLA Modules:
  0.0 460.0 jit_solution(15194993147473998437)
XLA Ops:
  11.8 68.5 %shard_map.88 = (bf16[3072,1664]{1,0:T(8,128)(2,1)S(1)}, bf16[1536,3072]{1,0:T(8,128)(2,1)}) custom-call(bf16[768,1664]{1,0:T(8,128)(2,1)S(1)} %bitcast.402, bf16[384,3072]{1,0:T(8,128)(2,1)S(1)} %bitcast.403), custom_call_target="tpu_custom_call" | custom-call | tf_op jit(solution)/shard_map/pallas_call | solution.py:266
  90.0 5.4 %fusion.46 = bf16[1,48,3072]{2,1,0:T(8,128)(2,1)S(1)} fusion(bf16[48,1536]{1,0:T(8,128)(2,1)S(1)} %reshape_reshape.19, bf16[1536,3072]{1,0:T(8,128)(2,1)} %get-tuple-element.809, bf16[3,1,48,3072]{3,2,1,0:T(8,128)(2,1)S(1)} %bitcast.427, s32[]{:T(128)S(6)} %min.30, pred[]{:T(512)S(6)} %eq.31), kind=kOutput, calls=%fused_computation.74 | convolution fusion | flops 453574656 | bytes 10174469 | tf_op jit(solution)/shard_map/dot_general | solution.py:70
  99.2 6.5 %collective-permute-done.1 = bf16[1,48,3072]{2,1,0:T(8,128)(2,1)S(1)} collective-permute-done((bf16[1,48,3072]{2,1,0:T(8,128)(2,1)S(1)}, bf16[1,48,3072]{2,1,0:T(8,128)(2,1)S(1)}, u32[]{:S(2)}, u32[]{:S(2)}) %collective-permute-start.1) | collective-permute-done | bytes 294944 | tf_op jit(solution)/shard_map/ppermute | solution.py:21
  105.9 6.5 %bitcast_dynamic-update-slice_fusion.13 = (bf16[4,1,48,1664]{3,2,1,0:T(8,128)(2,1)}, bf16[48,1664]{1,0:T(8,128)(2,1)S(1)}) fusion(bf16[4,1,48,1664]{3,2,1,0:T(8,128)(2,1)} %get-tuple-element.666, s32[]{:T(128)S(6)} %select_n.203, bf16[3072,1664]{1,0:T(8,128)(2,1)} %copy-done.2, bf16[1,48,3072]{2,1,0:T(8,128)(2,1)S(1)} %get-tuple-element.636, ...), kind=kOutput, calls=%fused_computation.199 | convolution fusion | flops 491403264 | bytes 10850500 | tf_op jit(solution)/shard_map/dot_general | solution.py:40
  115.5 5.6 %fusion.41 = bf16[1,48,3072]{2,1,0:T(8,128)(2,1)S(1)} fusion(bf16[48,1536]{1,0:T(8,128)(2,1)S(1)} %reshape_reshape.20, bf16[1536,3072]{1,0:T(8,128)(2,1)} %get-tuple-element.809, bf16[1,48,3072]{2,1,0:T(8,128)(2,1)S(1)} %get-tuple-element.636), kind=kOutput, calls=%fused_computation.69 | convolution fusion | flops 453427200 | bytes 10174464 | tf_op jit(solution)/shard_map/dot_general | solution.py:70
  121.1 4.6 collective-permute-start.2
  125.8 5.7 %collective-permute-done.2 = bf16[1,48,3072]{2,1,0:T(8,128)(2,1)S(1)} collective-permute-done((bf16[1,48,3072]{2,1,0:T(8,128)(2,1)S(1)}, bf16[1,48,3072]{2,1,0:T(8,128)(2,1)S(1)}, u32[]{:S(2)}, u32[]{:S(2)}) %collective-permute-start.2) | collective-permute-done | bytes 294944 | tf_op jit(solution)/shard_map/ppermute | solution.py:21
  138.5 5.6 %fusion.42 = bf16[1,48,3072]{2,1,0:T(8,128)(2,1)S(1)} fusion(bf16[48,1536]{1,0:T(8,128)(2,1)S(1)} %reshape_reshape.21, bf16[1536,3072]{1,0:T(8,128)(2,1)} %get-tuple-element.809, bf16[1,48,3072]{2,1,0:T(8,128)(2,1)S(1)} %get-tuple-element.634), kind=kOutput, calls=%fused_computation.70 | convolution fusion | flops 453427200 | bytes 10174464 | tf_op jit(solution)/shard_map/dot_general | solution.py:70
  148.5 5.0 %collective-permute-done.3 = bf16[1,48,3072]{2,1,0:T(8,128)(2,1)S(1)} collective-permute-done((bf16[1,48,3072]{2,1,0:T(8,128)(2,1)S(1)}, bf16[1,48,3072]{2,1,0:T(8,128)(2,1)S(1)}, u32[]{:S(2)}, u32[]{:S(2)}) %collective-permute-start.3) | collective-permute-done | bytes 294944 | tf_op jit(solution)/shard_map/ppermute | solution.py:21
  160.5 5.6 %fusion.43 = bf16[1,48,3072]{2,1,0:T(8,128)(2,1)S(1)} fusion(bf16[48,1536]{1,0:T(8,128)(2,1)S(1)} %reshape_reshape.22, bf16[1536,3072]{1,0:T(8,128)(2,1)} %get-tuple-element.809, bf16[1,48,3072]{2,1,0:T(8,128)(2,1)S(1)} %get-tuple-element.632), kind=kOutput, calls=%fused_computation.71 | convolution fusion | flops 453427200 | bytes 10174464 | tf_op jit(solution)/shard_map/dot_general | solution.py:70
  166.1 4.4 collective-permute-start.4
  181.8 5.6 %fusion.44 = bf16[1,48,3072]{2,1,0:T(8,128)(2,1)S(1)} fusion(bf16[48,1536]{1,0:T(8,128)(2,1)S(1)} %reshape_reshape.23, bf16[1536,3072]{1,0:T(8,128)(2,1)} %get-tuple-element.809, bf16[1,48,3072]{2,1,0:T(8,128)(2,1)S(1)} %get-tuple-element.630), kind=kOutput, calls=%fused_computation.72 | convolution fusion | flops 453427200 | bytes 10174464 | tf_op jit(solution)/shard_map/dot_general | solution.py:70
  202.8 186.3 %while.26 = (s32[]{:T(128)}, bf16[1,48,3072]{2,1,0:T(8,128)(2,1)S(1)}, bf16[3,1,48,3072]{3,2,1,0:T(8,128)(2,1)}, bf16[3,1,48,1664]{3,2,1,0:T(8,128)(2,1)S(1)}, b...) while((s32[]{:T(128)}, ...), condition=%wide.region_26.27_spmd.clone, body=%wide.region_17.26_spmd.clone.sunk | while | flops 991109952 | bytes 38094312 | solution.py:386
  204.2 8.6 %collective-permute-done = bf16[1,48,3072]{2,1,0:T(8,128)(2,1)S(1)} collective-permute-done((bf16[1,48,3072]{2,1,0:T(8,128)(2,1)S(1)}, bf16[1,48,3072]{2,1,0:T(8,128)(2,1)S(1)}, u32[]{:S(2)}, u32[]{:S(2)}) %collective-permute-start) | collective-permute-done | bytes 294944 | tf_op jit(solution)/shard_map/while/body/eval_jaxpr/ppermute | solution.py:21
  214.2 7.3 %collective-permute-done = bf16[1,48,3072]{2,1,0:T(8,128)(2,1)S(1)} collective-permute-done((bf16[1,48,3072]{2,1,0:T(8,128)(2,1)S(1)}, bf16[1,48,3072]{2,1,0:T(8,128)(2,1)S(1)}, u32[]{:S(2)}, u32[]{:S(2)}) %collective-permute-start) | collective-permute-done | bytes 294944 | tf_op jit(solution)/shard_map/while/body/eval_jaxpr/ppermute | solution.py:21
  222.9 72.6 %collective-permute-done = bf16[1,48,3072]{2,1,0:T(8,128)(2,1)S(1)} collective-permute-done((bf16[1,48,3072]{2,1,0:T(8,128)(2,1)S(1)}, bf16[1,48,3072]{2,1,0:T(8,128)(2,1)S(1)}, u32[]{:S(2)}, u32[]{:S(2)}) %collective-permute-start) | collective-permute-done | bytes 294944 | tf_op jit(solution)/shard_map/while/body/eval_jaxpr/ppermute | solution.py:21
  295.5 22.6 %conditional.3 = (bf16[1,48,3072]{2,1,0:T(8,128)(2,1)S(1)}, bf16[3,1,48,3072]{3,2,1,0:T(8,128)(2,1)}, bf16[3,1,48,1664]{3,2,1,0:T(8,128)(2,1)S(1)}, bf16[3,1,48,...) conditional(s32[]{:T(128)} %convert_element_type.525, ...), branch_computations={%region_18.18_spmd, %region_19.25_spmd} | conditional | flops 991109952 | bytes 36906912 | solution.py:375
  299.6 6.6 %convolution_convert_fusion = bf16[48,1536]{1,0:T(8,128)(2,1)S(1)} fusion(bf16[1536,3072]{1,0:T(8,128)(2,1)} %get-tuple-element.502, bf16[1,48,3072]{2,1,0:T(8,128)(2,1)S(1)} %get-tuple-element.626), kind=kOutput, calls=%fused_computation.1 | convolution fusion | flops 453058560 | bytes 9879552 | tf_op jit(solution)/shard_map/while/body/eval_jaxpr/cond/branch_1_fun/dot_general | solution.py:82
  310.6 7.2 %fusion.18 = (f32[3072]{0:T(1024)S(1)}, f32[48]{0:T(128)S(1)}, f32[48,3072]{1,0:T(8,128)S(1)}) fusion(f32[48]{0:T(128)S(1)} %get-tuple-element.638, bf16[4,1,48,3072]{3,2,1,0:T(8,128)(2,1)S(1)} %get-tuple-element.499, s32[]{:T(128)S(6)} %min.23, f32[3072]{0:T(1024)S(1)} %bitcast.419, bf16[48,1664]{1,0:T(8,128)(2,1)S(1)} %concatenate.26, ...), kind=kOutput, calls=%fused_computation.27 | convolution fusion | flops 491762624 | bytes 11293060 | tf_op jit(solution)/shard_map/while/body/eval_jaxpr/cond/branch_1_fun/dot_general | solution.py:106
  319.4 7.3 %collective-permute-done = bf16[1,48,3072]{2,1,0:T(8,128)(2,1)S(1)} collective-permute-done((bf16[1,48,3072]{2,1,0:T(8,128)(2,1)S(1)}, bf16[1,48,3072]{2,1,0:T(8,128)(2,1)S(1)}, u32[]{:S(2)}, u32[]{:S(2)}) %collective-permute-start) | collective-permute-done | bytes 294944 | tf_op jit(solution)/shard_map/while/body/eval_jaxpr/ppermute | solution.py:21
  326.7 22.6 %conditional.3 = (bf16[1,48,3072]{2,1,0:T(8,128)(2,1)S(1)}, bf16[3,1,48,3072]{3,2,1,0:T(8,128)(2,1)}, bf16[3,1,48,1664]{3,2,1,0:T(8,128)(2,1)S(1)}, bf16[3,1,48,...) conditional(s32[]{:T(128)} %convert_element_type.525, ...), branch_computations={%region_18.18_spmd, %region_19.25_spmd} | conditional | flops 991109952 | bytes 36906912 | solution.py:375
  330.8 6.6 %convolution_convert_fusion = bf16[48,1536]{1,0:T(8,128)(2,1)S(1)} fusion(bf16[1536,3072]{1,0:T(8,128)(2,1)} %get-tuple-element.502, bf16[1,48,3072]{2,1,0:T(8,128)(2,1)S(1)} %get-tuple-element.626), kind=kOutput, calls=%fused_computation.1 | convolution fusion | flops 453058560 | bytes 9879552 | tf_op jit(solution)/shard_map/while/body/eval_jaxpr/cond/branch_1_fun/dot_general | solution.py:82
  341.8 7.2 %fusion.18 = (f32[3072]{0:T(1024)S(1)}, f32[48]{0:T(128)S(1)}, f32[48,3072]{1,0:T(8,128)S(1)}) fusion(f32[48]{0:T(128)S(1)} %get-tuple-element.638, bf16[4,1,48,3072]{3,2,1,0:T(8,128)(2,1)S(1)} %get-tuple-element.499, s32[]{:T(128)S(6)} %min.23, f32[3072]{0:T(1024)S(1)} %bitcast.419, bf16[48,1664]{1,0:T(8,128)(2,1)S(1)} %concatenate.26, ...), kind=kOutput, calls=%fused_computation.27 | convolution fusion | flops 491762624 | bytes 11293060 | tf_op jit(solution)/shard_map/while/body/eval_jaxpr/cond/branch_1_fun/dot_general | solution.py:106
  350.6 7.3 %collective-permute-done = bf16[1,48,3072]{2,1,0:T(8,128)(2,1)S(1)} collective-permute-done((bf16[1,48,3072]{2,1,0:T(8,128)(2,1)S(1)}, bf16[1,48,3072]{2,1,0:T(8,128)(2,1)S(1)}, u32[]{:S(2)}, u32[]{:S(2)}) %collective-permute-start) | collective-permute-done | bytes 294944 | tf_op jit(solution)/shard_map/while/body/eval_jaxpr/ppermute | solution.py:21
  357.9 22.6 %conditional.3 = (bf16[1,48,3072]{2,1,0:T(8,128)(2,1)S(1)}, bf16[3,1,48,3072]{3,2,1,0:T(8,128)(2,1)}, bf16[3,1,48,1664]{3,2,1,0:T(8,128)(2,1)S(1)}, bf16[3,1,48,...) conditional(s32[]{:T(128)} %convert_element_type.525, ...), branch_computations={%region_18.18_spmd, %region_19.25_spmd} | conditional | flops 991109952 | bytes 36906912 | solution.py:375
  362.0 6.6 %convolution_convert_fusion = bf16[48,1536]{1,0:T(8,128)(2,1)S(1)} fusion(bf16[1536,3072]{1,0:T(8,128)(2,1)} %get-tuple-element.502, bf16[1,48,3072]{2,1,0:T(8,128)(2,1)S(1)} %get-tuple-element.626), kind=kOutput, calls=%fused_computation.1 | convolution fusion | flops 453058560 | bytes 9879552 | tf_op jit(solution)/shard_map/while/body/eval_jaxpr/cond/branch_1_fun/dot_general | solution.py:82
  373.1 7.2 %fusion.18 = (f32[3072]{0:T(1024)S(1)}, f32[48]{0:T(128)S(1)}, f32[48,3072]{1,0:T(8,128)S(1)}) fusion(f32[48]{0:T(128)S(1)} %get-tuple-element.638, bf16[4,1,48,3072]{3,2,1,0:T(8,128)(2,1)S(1)} %get-tuple-element.499, s32[]{:T(128)S(6)} %min.23, f32[3072]{0:T(1024)S(1)} %bitcast.419, bf16[48,1664]{1,0:T(8,128)(2,1)S(1)} %concatenate.26, ...), kind=kOutput, calls=%fused_computation.27 | convolution fusion | flops 491762624 | bytes 11293060 | tf_op jit(solution)/shard_map/while/body/eval_jaxpr/cond/branch_1_fun/dot_general | solution.py:106
  381.8 7.3 %collective-permute-done = bf16[1,48,3072]{2,1,0:T(8,128)(2,1)S(1)} collective-permute-done((bf16[1,48,3072]{2,1,0:T(8,128)(2,1)S(1)}, bf16[1,48,3072]{2,1,0:T(8,128)(2,1)S(1)}, u32[]{:S(2)}, u32[]{:S(2)}) %collective-permute-start) | collective-permute-done | bytes 294944 | tf_op jit(solution)/shard_map/while/body/eval_jaxpr/ppermute | solution.py:21
  396.9 20.8 %all-gather = f32[12288]{0:T(1024)S(1)} all-gather(f32[3072]{0:T(1024)S(1)} %get-tuple-element.549), channel_id=2, replica_groups=mesh['groups'=2,'section'=4,'dp'=4] {'dp'}, dimensions={0}, use_global_device_ids=true | all-gather | bytes 61440 | tf_op jit(solution)/shard_map/all_gather | solution.py:392
  425.2 6.2 %convolution_bitcast_fusion.4 = f32[1,768,1664]{2,1,0:T(8,128)} fusion(bf16[576,768]{1,0:T(8,128)(2,1)S(1)} %bitcast.435, bf16[576,1664]{1,0:T(8,128)(2,1)} %all-gather.4.cloned.1.call-done), kind=kOutput, calls=%fused_computation.59 | convolution fusion | flops 1472200704 | bytes 7913472 | tf_op jit(solution)/shard_map/dot_general | solution.py:398
  431.4 15.6 %all-gather.6.cloned.1.call-done = bf16[576,3072]{1,0:T(8,128)(2,1)} async-done(((bf16[144,3072]{1,0:T(8,128)(2,1)}), bf16[576,3072]{1,0:T(8,128)(2,1)}) %all-gather.6.cloned.1.call-update) | async-done | bytes 3538960 | tf_op jit(solution)/shard_map/all_gather | solution.py:393
  447.0 6.2 %convolution_bitcast_fusion.3 = f32[1,384,3072]{2,1,0:T(8,128)} fusion(bf16[576,384]{1,0:T(8,128)(2,1)S(1)} %bitcast.431, bf16[576,3072]{1,0:T(8,128)(2,1)} %all-gather.6.cloned.1.call-done), kind=kOutput, calls=%fused_computation.58 | convolution fusion | flops 1358954496 | bytes 8699904 | tf_op jit(solution)/shard_map/dot_general | solution.py:395
  (264 shorter events, 114.8 us)
Async XLA Ops:
  7.2 418.1 %all-gather.4.cloned.1.call-start = ((), (), s32[]{:S(2)}) async-start(), calls=%async_computation | async-start | bytes 2396160 | tf_op jit(solution)/shard_map/all_gather | solution.py:394
  89.9 16.0 %copy-start.3 = (f32[1,3072]{1,0:T(1,128)S(1)}, f32[1,3072]{1,0:T(1,128)}, u32[]{:S(2)}) copy-start(f32[1,3072]{1,0:T(1,128)} %param.13) | copy-start | bytes 36868
  95.4 10.3 %collective-permute-start.1 = (bf16[1,48,3072]{2,1,0:T(8,128)(2,1)S(1)}, bf16[1,48,3072]{2,1,0:T(8,128)(2,1)S(1)}, u32[]{:S(2)}, u32[]{:S(2)}) collective-permute-start(bf16[1,48,3072]{2,1,0:T(8,128)(2,1)S(1)} %fusion.46), channel_id=1, source_target_pairs={{0,4},{4,8},{8,12},{1,5},{5,9},{9,13},{2,6},{6,10},{10,14},{3,7},{... | collective-permute-start | bytes 884744 | tf_op jit(solution)/shard_map/ppermute | solution.py:21
  113.5 19.2 %slice-start = ((s8[10223616]{0:T(1024)(128)(4,1)}), s8[1835008]{0:T(1024)(128)(4,1)S(1)}, s32[]{:S(2)}) async-start(s8[10223616]{0:T(1024)(128)(4,1)} %bitcast.404), calls=%async_computation.2 | async-start | bytes 3670016
  115.5 17.2 %slice-start.1 = ((s8[10223616]{0:T(1024)(128)(4,1)}), s8[4194304]{0:T(1024)(128)(4,1)S(1)}, s32[]{:S(2)}) async-start(s8[10223616]{0:T(1024)(128)(4,1)} %bitcast.404), calls=%async_computation.3 | async-start | bytes 8388608
  115.5 17.2 %slice-start.2 = ((s8[10223616]{0:T(1024)(128)(4,1)}), s8[4194304]{0:T(1024)(128)(4,1)S(1)}, s32[]{:S(2)}) async-start(s8[10223616]{0:T(1024)(128)(4,1)} %bitcast.404), calls=%async_computation.4 | async-start | bytes 8388608
  121.1 10.4 %collective-permute-start.2 = (bf16[1,48,3072]{2,1,0:T(8,128)(2,1)S(1)}, bf16[1,48,3072]{2,1,0:T(8,128)(2,1)S(1)}, u32[]{:S(2)}, u32[]{:S(2)}) collective-permute-start(bf16[1,48,3072]{2,1,0:T(8,128)(2,1)S(1)} %fusion.41), channel_id=1, source_target_pairs={{0,4},{4,8},{8,12},{1,5},{5,9},{9,13},{2,6},{6,10},{10,14},{3,7},{... | collective-permute-start | bytes 884744 | tf_op jit(solution)/shard_map/ppermute | solution.py:21
  136.5 18.3 %slice-start.3 = ((s8[10223616]{0:T(1024)(128)(4,1)}), s8[1835008]{0:T(1024)(128)(4,1)S(1)}, s32[]{:S(2)}) async-start(s8[10223616]{0:T(1024)(128)(4,1)} %bitcast.406), calls=%async_computation.5 | async-start | bytes 3670016
  138.5 16.3 %slice-start.4 = ((s8[10223616]{0:T(1024)(128)(4,1)}), s8[4194304]{0:T(1024)(128)(4,1)S(1)}, s32[]{:S(2)}) async-start(s8[10223616]{0:T(1024)(128)(4,1)} %bitcast.406), calls=%async_computation.6 | async-start | bytes 8388608
  138.5 16.3 %slice-start.5 = ((s8[10223616]{0:T(1024)(128)(4,1)}), s8[4194304]{0:T(1024)(128)(4,1)S(1)}, s32[]{:S(2)}) async-start(s8[10223616]{0:T(1024)(128)(4,1)} %bitcast.406), calls=%async_computation.7 | async-start | bytes 8388608
  144.1 9.5 %collective-permute-start.3 = (bf16[1,48,3072]{2,1,0:T(8,128)(2,1)S(1)}, bf16[1,48,3072]{2,1,0:T(8,128)(2,1)S(1)}, u32[]{:S(2)}, u32[]{:S(2)}) collective-permute-start(bf16[1,48,3072]{2,1,0:T(8,128)(2,1)S(1)} %fusion.42), channel_id=1, source_target_pairs={{0,4},{4,8},{8,12},{1,5},{5,9},{9,13},{2,6},{6,10},{10,14},{3,7},{... | collective-permute-start | bytes 884744 | tf_op jit(solution)/shard_map/ppermute | solution.py:21
  158.5 17.4 %slice-start.6 = ((s8[10223616]{0:T(1024)(128)(4,1)}), s8[1835008]{0:T(1024)(128)(4,1)S(1)}, s32[]{:S(2)}) async-start(s8[10223616]{0:T(1024)(128)(4,1)} %bitcast.408), calls=%async_computation.8 | async-start | bytes 3670016
  160.5 15.4 %slice-start.7 = ((s8[10223616]{0:T(1024)(128)(4,1)}), s8[4194304]{0:T(1024)(128)(4,1)S(1)}, s32[]{:S(2)}) async-start(s8[10223616]{0:T(1024)(128)(4,1)} %bitcast.408), calls=%async_computation.9 | async-start | bytes 8388608
  160.5 15.4 %slice-start.8 = ((s8[10223616]{0:T(1024)(128)(4,1)}), s8[4194304]{0:T(1024)(128)(4,1)S(1)}, s32[]{:S(2)}) async-start(s8[10223616]{0:T(1024)(128)(4,1)} %bitcast.408), calls=%async_computation.10 | async-start | bytes 8388608
  166.1 8.6 %collective-permute-start.4 = (bf16[1,48,3072]{2,1,0:T(8,128)(2,1)S(1)}, bf16[1,48,3072]{2,1,0:T(8,128)(2,1)S(1)}, u32[]{:S(2)}, u32[]{:S(2)}) collective-permute-start(bf16[1,48,3072]{2,1,0:T(8,128)(2,1)S(1)} %fusion.43), channel_id=1, source_target_pairs={{0,4},{4,8},{8,12},{1,5},{5,9},{9,13},{2,6},{6,10},{10,14},{3,7},{... | collective-permute-start | bytes 884744 | tf_op jit(solution)/shard_map/ppermute | solution.py:21
  180.5 16.8 %slice-start.9 = ((s8[10223616]{0:T(1024)(128)(4,1)}), s8[1835008]{0:T(1024)(128)(4,1)S(1)}, s32[]{:S(2)}) async-start(s8[10223616]{0:T(1024)(128)(4,1)} %bitcast.410), calls=%async_computation.11 | async-start | bytes 3670016
  181.8 15.5 %slice-start.10 = ((s8[10223616]{0:T(1024)(128)(4,1)}), s8[4194304]{0:T(1024)(128)(4,1)S(1)}, s32[]{:S(2)}) async-start(s8[10223616]{0:T(1024)(128)(4,1)} %bitcast.410), calls=%async_computation.12 | async-start | bytes 8388608
  181.8 15.5 %slice-start.11 = ((s8[10223616]{0:T(1024)(128)(4,1)}), s8[4194304]{0:T(1024)(128)(4,1)S(1)}, s32[]{:S(2)}) async-start(s8[10223616]{0:T(1024)(128)(4,1)} %bitcast.410), calls=%async_computation.13 | async-start | bytes 8388608
  187.4 8.6 %collective-permute-start.5 = (bf16[1,48,3072]{2,1,0:T(8,128)(2,1)S(1)}, bf16[1,48,3072]{2,1,0:T(8,128)(2,1)S(1)}, u32[]{:S(2)}, u32[]{:S(2)}) collective-permute-start(bf16[1,48,3072]{2,1,0:T(8,128)(2,1)S(1)} %fusion.44), channel_id=1, source_target_pairs={{0,4},{4,8},{8,12},{1,5},{5,9},{9,13},{2,6},{6,10},{10,14},{3,7},{... | collective-permute-start | bytes 884744 | tf_op jit(solution)/shard_map/ppermute | solution.py:21
  202.9 9.9 %collective-permute-start = (bf16[1,48,3072]{2,1,0:T(8,128)(2,1)S(1)}, bf16[1,48,3072]{2,1,0:T(8,128)(2,1)S(1)}, u32[]{:S(2)}, u32[]{:S(2)}) collective-permute-start(bf16[1,48,3072]{2,1,0:T(8,128)(2,1)S(1)} %get-tuple-element.779), channel_id=1, source_target_pairs={{4,0},{8,4},{12,8},{5,1},{9,5},{13,9},{6,2},{10,6},{14,10},{7,3},{... | collective-permute-start | bytes 884744 | tf_op jit(solution)/shard_map/while/body/eval_jaxpr/ppermute | solution.py:21
  212.9 8.6 %collective-permute-start = (bf16[1,48,3072]{2,1,0:T(8,128)(2,1)S(1)}, bf16[1,48,3072]{2,1,0:T(8,128)(2,1)S(1)}, u32[]{:S(2)}, u32[]{:S(2)}) collective-permute-start(bf16[1,48,3072]{2,1,0:T(8,128)(2,1)S(1)} %get-tuple-element.779), channel_id=1, source_target_pairs={{4,0},{8,4},{12,8},{5,1},{9,5},{13,9},{6,2},{10,6},{14,10},{7,3},{... | collective-permute-start | bytes 884744 | tf_op jit(solution)/shard_map/while/body/eval_jaxpr/ppermute | solution.py:21
  221.6 73.9 %collective-permute-start = (bf16[1,48,3072]{2,1,0:T(8,128)(2,1)S(1)}, bf16[1,48,3072]{2,1,0:T(8,128)(2,1)S(1)}, u32[]{:S(2)}, u32[]{:S(2)}) collective-permute-start(bf16[1,48,3072]{2,1,0:T(8,128)(2,1)S(1)} %get-tuple-element.779), channel_id=1, source_target_pairs={{4,0},{8,4},{12,8},{5,1},{9,5},{13,9},{6,2},{10,6},{14,10},{7,3},{... | collective-permute-start | bytes 884744 | tf_op jit(solution)/shard_map/while/body/eval_jaxpr/ppermute | solution.py:21
  318.1 8.6 %collective-permute-start = (bf16[1,48,3072]{2,1,0:T(8,128)(2,1)S(1)}, bf16[1,48,3072]{2,1,0:T(8,128)(2,1)S(1)}, u32[]{:S(2)}, u32[]{:S(2)}) collective-permute-start(bf16[1,48,3072]{2,1,0:T(8,128)(2,1)S(1)} %get-tuple-element.779), channel_id=1, source_target_pairs={{4,0},{8,4},{12,8},{5,1},{9,5},{13,9},{6,2},{10,6},{14,10},{7,3},{... | collective-permute-start | bytes 884744 | tf_op jit(solution)/shard_map/while/body/eval_jaxpr/ppermute | solution.py:21
  349.3 8.6 %collective-permute-start = (bf16[1,48,3072]{2,1,0:T(8,128)(2,1)S(1)}, bf16[1,48,3072]{2,1,0:T(8,128)(2,1)S(1)}, u32[]{:S(2)}, u32[]{:S(2)}) collective-permute-start(bf16[1,48,3072]{2,1,0:T(8,128)(2,1)S(1)} %get-tuple-element.779), channel_id=1, source_target_pairs={{4,0},{8,4},{12,8},{5,1},{9,5},{13,9},{6,2},{10,6},{14,10},{7,3},{... | collective-permute-start | bytes 884744 | tf_op jit(solution)/shard_map/while/body/eval_jaxpr/ppermute | solution.py:21
  380.5 8.6 %collective-permute-start = (bf16[1,48,3072]{2,1,0:T(8,128)(2,1)S(1)}, bf16[1,48,3072]{2,1,0:T(8,128)(2,1)S(1)}, u32[]{:S(2)}, u32[]{:S(2)}) collective-permute-start(bf16[1,48,3072]{2,1,0:T(8,128)(2,1)S(1)} %get-tuple-element.779), channel_id=1, source_target_pairs={{4,0},{8,4},{12,8},{5,1},{9,5},{13,9},{6,2},{10,6},{14,10},{7,3},{... | collective-permute-start | bytes 884744 | tf_op jit(solution)/shard_map/while/body/eval_jaxpr/ppermute | solution.py:21
  389.9 57.0 %all-gather.6.cloned.1.call-start = ((), (), s32[]{:S(2)}) async-start(), calls=%async_computation.1 | async-start | bytes 4423680 | tf_op jit(solution)/shard_map/all_gather | solution.py:393
  391.8 28.6 %collective-permute-start.9 = (bf16[144,384]{1,0:T(8,128)(2,1)S(1)}, bf16[144,384]{1,0:T(8,128)(2,1)S(1)}, u32[]{:S(2)}, u32[]{:S(2)}) collective-permute-start(bf16[144,384]{1,0:T(8,128)(2,1)S(1)} %get-tuple-element.650), channel_id=1, source_target_pairs={{0,1},{1,2},{2,3},{3,0},{4,5},{5,6},{6,7},{7,4},{8,9},{9,10},{10,1... | collective-permute-start | bytes 331784 | tf_op jit(solution)/shard_map/ppermute | solution.py:295
  391.9 29.3 %collective-permute-start.10 = (bf16[144,384]{1,0:T(8,128)(2,1)S(1)}, bf16[144,384]{1,0:T(8,128)(2,1)S(1)}, u32[]{:S(2)}, u32[]{:S(2)}) collective-permute-start(bf16[144,384]{1,0:T(8,128)(2,1)S(1)} %get-tuple-element.649), channel_id=1, source_target_pairs={{0,2},{1,3},{2,0},{3,1},{4,6},{5,7},{6,4},{7,5},{8,10},{9,11},{10,... | collective-permute-start | bytes 331784 | tf_op jit(solution)/shard_map/ppermute | solution.py:295
  392.6 28.6 %collective-permute-start.11 = (bf16[144,384]{1,0:T(8,128)(2,1)S(1)}, bf16[144,384]{1,0:T(8,128)(2,1)S(1)}, u32[]{:S(2)}, u32[]{:S(2)}) collective-permute-start(bf16[144,384]{1,0:T(8,128)(2,1)S(1)} %get-tuple-element.648), channel_id=1, source_target_pairs={{0,3},{1,0},{2,1},{3,2},{4,7},{5,4},{6,5},{7,6},{8,11},{9,8},{10,9... | collective-permute-start | bytes 331784 | tf_op jit(solution)/shard_map/ppermute | solution.py:295
  395.2 26.0 %collective-permute-start.6 = (bf16[144,768]{1,0:T(8,128)(2,1)S(1)}, bf16[144,768]{1,0:T(8,128)(2,1)S(1)}, u32[]{:S(2)}, u32[]{:S(2)}) collective-permute-start(bf16[144,768]{1,0:T(8,128)(2,1)S(1)} %get-tuple-element.647), channel_id=1, source_target_pairs={{0,1},{1,2},{2,3},{3,0},{4,5},{5,6},{6,7},{7,4},{8,9},{9,10},{10,1... | collective-permute-start | bytes 663560 | tf_op jit(solution)/shard_map/ppermute | solution.py:295
  395.3 26.0 %collective-permute-start.7 = (bf16[144,768]{1,0:T(8,128)(2,1)S(1)}, bf16[144,768]{1,0:T(8,128)(2,1)S(1)}, u32[]{:S(2)}, u32[]{:S(2)}) collective-permute-start(bf16[144,768]{1,0:T(8,128)(2,1)S(1)} %get-tuple-element.646), channel_id=1, source_target_pairs={{0,2},{1,3},{2,0},{3,1},{4,6},{5,7},{6,4},{7,5},{8,10},{9,11},{10,... | collective-permute-start | bytes 663560 | tf_op jit(solution)/shard_map/ppermute | solution.py:295
  420.4 4.8 %collective-permute-start.8 = (bf16[144,768]{1,0:T(8,128)(2,1)S(1)}, bf16[144,768]{1,0:T(8,128)(2,1)S(1)}, u32[]{:S(2)}, u32[]{:S(2)}) collective-permute-start(bf16[144,768]{1,0:T(8,128)(2,1)S(1)} %get-tuple-element.645), channel_id=1, source_target_pairs={{0,3},{1,0},{2,1},{3,2},{4,7},{5,4},{6,5},{7,6},{8,11},{9,8},{10,9... | collective-permute-start | bytes 663560 | tf_op jit(solution)/shard_map/ppermute | solution.py:295
  (12 other events, 52.3 us)
Sparse Core Ops, SparseCore 0:
  390.1 27.5 all-gather.3
  419.2 27.7 all-gather.5
